TPU v7x, 32 devices: a whole 2x2x4 slice. The times are simulated.
32 devices in a mesh: dp: 2 (over x), pipe: 4 (over z), expert: 4 (over y, core).
Axes of the slice: x: 2, y: 2, z: 4, core: 2. Of those that a mesh axis runs over, the one named last changes fastest.
Arguments:
- tokens: bfloat16 [1024, 2048], P(('dp', 'expert')), may hold values from -6 to 6
- cotangent: bfloat16 [1024, 2048], P(('dp', 'expert')), may hold values from -6 to 6
- owner_ids: int32 [4, 1024, 4], P('pipe', ('dp', 'expert')), may hold values from 0 to 7, all different within a row; in each aligned block of 32 rows (0 to 31, 32 to 63, ..., all dimensions but the last counted through in order) at most 20 rows name the same one
- gate_weights: bfloat16 [4, 1024, 4], P('pipe', ('dp', 'expert')), may hold values from 0.049804688 to 0.25
- norm_gain: float32 [4, 2048], P('pipe'), may hold values from 0.5 to 1.5
- w_gate: bfloat16 [4, 8, 2048, 384], P('pipe', ('dp', 'expert')), may hold values from -0.125 to 0.125
- w_up: bfloat16 [4, 8, 2048, 384], P('pipe', ('dp', 'expert')), may hold values from -0.125 to 0.125
- w_down: bfloat16 [4, 8, 384, 2048], P('pipe', ('dp', 'expert')), may hold values from -0.3125 to 0.3125
Outputs:
- segment_out: bfloat16 [4, 1024, 2048], P('pipe', ('dp', 'expert'))
- segment_grad: bfloat16 [4, 1024, 2048], P('pipe', ('dp', 'expert'))
- gain_grad: float32 [4, 2048], P('pipe')
Inputs may be any that keep to these rules, and one draw needn't show every extreme that they name: `owner_ids`: each row names 4 different owners. In each aligned block of 32 rows (layers in order, then tokens) no owner is named by more than 20 rows, and that bound is reached.
All inputs are finite; a program needn't handle non-finite values.
Results may differ from a plain program's by a relative error of at most 0.014.
Values may be sent and summed in bfloat16 or wider, within the bound.
No kernel may reach another device: no remote copies, remote signals or barrier semaphores. Data moves between devices by JAX's collectives and lax.ppermute only.
A program may use at most 128 MiB of HBM per device.

v0:
```python
import jax
import jax.numpy as jnp
from jax import lax
from jax.experimental import pallas as pl
from jax.experimental.pallas import tpu as pltpu
import functools
import math
from jax.sharding import PartitionSpec as P

MICRO = 4
LIMIT = 12 * 1024 * 1024


epsilon = 1e-06


def from_behind(value, axis, steps):
    count = lax.axis_size(axis)
    leading, last = (max(0, -steps), min(count, count - steps))
    return lax.ppermute(value, axis, [(source, source + steps) for source in range(leading, last)])


def inverse_rms(values):
    return lax.rsqrt(jnp.mean(values * values, axis=-1, keepdims=True) + epsilon)


def contract_last(left, right):
    return lax.dot_general(
        left, right, (((1,), (1,)), ((), ())), preferred_element_type=jnp.float32
    )


def route_tables(ids_part, owners, capacity):
    owner_range = jnp.arange(owners, dtype=jnp.int32)
    onehot = (ids_part[:, :, None] == owner_range[None, None, :]).astype(jnp.int32)
    member = jnp.sum(onehot, axis=1)
    position = jnp.cumsum(member, axis=0) - member
    slot_range = jnp.arange(capacity, dtype=jnp.int32)
    placed = (position[:, :, None] == slot_range[None, None, :]) & (member[:, :, None] > 0)
    placing = jnp.transpose(placed, (1, 2, 0)).astype(jnp.bfloat16)
    return (onehot.astype(jnp.float32), placing)


def gate_slots(onehot, gates_part, placing, experts_here):
    gate_pairs = gates_part.astype(jnp.float32).reshape(gates_part.shape[0], -1, experts_here)
    chosen = jnp.einsum("rjo,rjc->roc", onehot, gate_pairs)
    return jnp.einsum("okr,roc->okc", placing.astype(jnp.float32), chosen).astype(jnp.bfloat16)


def send_rows(row_block, pair_block):
    got_rows, got_pairs = (
        lax.all_to_all(row_block, ("dp", "expert"), split_axis=0, concat_axis=0, tiled=True),
        lax.all_to_all(pair_block, ("dp", "expert"), split_axis=0, concat_axis=0, tiled=True),
    )
    return (got_rows, got_pairs)


def return_rows(row_block):
    return lax.all_to_all(row_block, ("dp", "expert"), split_axis=0, concat_axis=0, tiled=True)


def send_grads(row_block):
    return lax.all_to_all(row_block, ("dp", "expert"), split_axis=0, concat_axis=0, tiled=True)


def return_grads(row_block):
    return lax.all_to_all(row_block, ("dp", "expert"), split_axis=0, concat_axis=0, tiled=True)


def expert_forward(flat_rows, flat_pairs, joint_mats, down_mats):
    hidden_width = down_mats.shape[1]
    joint_pre = jnp.dot(flat_rows, joint_mats[0], preferred_element_type=jnp.float32)
    gate_pre = joint_pre[:, :hidden_width]
    up_pre = joint_pre[:, hidden_width:]
    hidden = (jax.nn.silu(gate_pre) * up_pre).astype(jnp.bfloat16)
    projected = jnp.dot(hidden, down_mats[0], preferred_element_type=jnp.float32)
    term = flat_pairs.astype(jnp.float32) * projected
    kept_both = [joint_pre]
    return (term.astype(jnp.bfloat16), jnp.stack(kept_both))


def expert_backward(grad_rows, flat_pairs, joint_keep, joint_mats, down_mats):
    hidden_width = down_mats.shape[1]
    q_vals = contract_last(grad_rows, down_mats[0])
    gate_pre = joint_keep[0][:, :hidden_width]
    up_pre = joint_keep[0][:, hidden_width:]
    sigma = jax.nn.sigmoid(gate_pre)
    weight = flat_pairs.astype(jnp.float32)
    d_gate = (q_vals * weight * up_pre * sigma * (1.0 + gate_pre * (1.0 - sigma))).astype(
        jnp.bfloat16
    )
    d_up = (q_vals * weight * gate_pre * sigma).astype(jnp.bfloat16)
    joint_grad = jnp.concatenate([d_gate, d_up], axis=1)
    term = contract_last(joint_grad, joint_mats[0])
    return term.astype(jnp.bfloat16)


def slot_body(tokens, cotangent, owner_ids, gate_weights, norm_gain, w_gate, w_up, w_down):
    segments = lax.axis_size("pipe")
    segment_index = lax.axis_index("pipe")
    owners = lax.axis_size("dp") * lax.axis_size("expert")
    tok_rows = tokens.shape[0]
    width = tokens.shape[1]
    micro_rows = tok_rows // MICRO
    route_count = owner_ids.shape[2]
    capacity = max(2, (5 * micro_rows * route_count + 4 * owners - 1) // (4 * owners))
    slot_count = owners * capacity
    gain_row = norm_gain[0]
    joint_mats = jnp.concatenate([w_gate[0], w_up[0]], axis=2)
    down_mats = w_down[0]
    layer_ids = owner_ids[0]
    layer_gates = gate_weights[0]
    experts_here = joint_mats.shape[0]
    joint_width = joint_mats.shape[2]

    def skip_forward(operands):
        return (
            jnp.zeros((slot_count, width), jnp.bfloat16),
            jnp.zeros((experts_here, slot_count, joint_width), jnp.float32),
        )

    def run_forward(operands):
        return expert_forward(operands[0], operands[1], joint_mats, down_mats)

    def skip_backward(operands):
        return jnp.zeros((slot_count, width), jnp.bfloat16)

    def run_backward(operands):
        return expert_backward(operands[0], operands[1], operands[2], joint_mats, down_mats)

    def timing(micro):
        is_valid = (micro >= 0) & (micro < MICRO)
        slot_pick = jnp.where(is_valid, micro, MICRO)
        start_row = jnp.clip(micro, 0, MICRO - 1) * micro_rows
        return (is_valid, slot_pick, start_row)

    layer_outs = jnp.zeros((MICRO + 1, micro_rows, width), jnp.bfloat16)
    layer_ins = jnp.zeros((MICRO + 1, micro_rows, width), jnp.bfloat16)
    kept_joint = jnp.zeros((MICRO + 1, experts_here, slot_count, joint_width), jnp.float32)
    kept_pairs = jnp.zeros((MICRO + 1, slot_count, experts_here), jnp.bfloat16)
    grad_outs = jnp.zeros((MICRO + 1, micro_rows, width), jnp.bfloat16)
    gain_sum = jnp.zeros((width,), jnp.float32)
    ticks = MICRO + segments - 1
    incoming = jnp.zeros((micro_rows, width), jnp.bfloat16)
    for tick_num in range(ticks):
        forward_is_valid, forward_slot_pick, forward_start_row = timing(tick_num - segment_index)
        forward_own_part = lax.dynamic_slice_in_dim(tokens, forward_start_row, micro_rows, 0)
        forward_layer_in = jnp.where(segment_index == 0, forward_own_part, incoming)
        forward_ids_part = lax.dynamic_slice_in_dim(layer_ids, forward_start_row, micro_rows, 0)
        gates_part = lax.dynamic_slice_in_dim(layer_gates, forward_start_row, micro_rows, 0)
        forward_x_float = forward_layer_in.astype(jnp.float32)
        forward_scale = inverse_rms(forward_x_float)
        normed = (forward_x_float * forward_scale * gain_row).astype(jnp.bfloat16)
        forward_onehot, forward_placing = route_tables(forward_ids_part, owners, capacity)
        row_block = jnp.einsum(
            "okr,rd->okd", forward_placing, normed, preferred_element_type=jnp.float32
        ).astype(jnp.bfloat16)
        pair_block = gate_slots(forward_onehot, gates_part, forward_placing, experts_here)
        f_valid, f_pick, layer_in, x_float, f_placing, row_block, pair_block = (
            forward_is_valid,
            forward_slot_pick,
            forward_layer_in,
            forward_x_float,
            forward_placing,
            row_block,
            pair_block,
        )
        got_rows, got_pairs = send_rows(row_block, pair_block)
        flat_rows = got_rows.reshape(slot_count, width)
        flat_pairs = got_pairs.reshape(slot_count, experts_here)
        result, joint_pre = lax.cond(f_valid, run_forward, skip_forward, (flat_rows, flat_pairs))
        returned = return_rows(result.reshape(owners, capacity, width))
        branch = jnp.einsum("okr,okd->rd", f_placing, returned, preferred_element_type=jnp.float32)
        layer_out = (x_float + branch).astype(jnp.bfloat16)
        layer_outs = lax.dynamic_update_index_in_dim(layer_outs, layer_out, f_pick, 0)
        layer_ins = lax.dynamic_update_index_in_dim(layer_ins, layer_in, f_pick, 0)
        kept_joint = lax.dynamic_update_index_in_dim(kept_joint, joint_pre, f_pick, 0)
        kept_pairs = lax.dynamic_update_index_in_dim(kept_pairs, flat_pairs, f_pick, 0)
        if tick_num + 1 < ticks:
            incoming = from_behind(layer_out, "pipe", 1)
    incoming = jnp.zeros((micro_rows, width), jnp.bfloat16)
    for tick_num in range(ticks):
        backward_is_valid, backward_slot_pick, backward_start_row = timing(
            tick_num - (segments - 1 - segment_index)
        )
        own_part = lax.dynamic_slice_in_dim(cotangent, backward_start_row, micro_rows, 0)
        backward_grad_in = jnp.where(segment_index == segments - 1, own_part, incoming)
        ids_part = lax.dynamic_slice_in_dim(layer_ids, backward_start_row, micro_rows, 0)
        backward_layer_in = lax.dynamic_index_in_dim(
            layer_ins, backward_slot_pick, 0, keepdims=False
        )
        backward_x_float = backward_layer_in.astype(jnp.float32)
        backward_scale = inverse_rms(backward_x_float)
        _, backward_placing = route_tables(ids_part, owners, capacity)
        grad_block = jnp.einsum(
            "okr,rd->okd", backward_placing, backward_grad_in, preferred_element_type=jnp.float32
        ).astype(jnp.bfloat16)
        b_valid, b_pick, grad_in, bx_float, b_scale, b_placing, grad_block = (
            backward_is_valid,
            backward_slot_pick,
            backward_grad_in,
            backward_x_float,
            backward_scale,
            backward_placing,
            grad_block,
        )
        got_grads = send_grads(grad_block).reshape(slot_count, width)
        joint_keep = lax.dynamic_index_in_dim(kept_joint, b_pick, 0, keepdims=False)
        pair_keep = lax.dynamic_index_in_dim(kept_pairs, b_pick, 0, keepdims=False)
        owner_grad = lax.cond(
            b_valid, run_backward, skip_backward, (got_grads, pair_keep, joint_keep)
        )
        returned = return_grads(owner_grad.reshape(owners, capacity, width))
        normed_grad = jnp.einsum(
            "okr,okd->rd", b_placing, returned, preferred_element_type=jnp.float32
        )
        weighted = gain_row * normed_grad
        grad_x = (
            grad_in.astype(jnp.float32)
            + b_scale * weighted
            - bx_float
            * b_scale
            * b_scale
            * b_scale
            * jnp.mean(weighted * bx_float, axis=-1, keepdims=True)
        )
        gain_term = jnp.where(b_valid, jnp.sum(normed_grad * bx_float * b_scale, axis=0), 0.0)
        grad_bf, gain_term = (grad_x.astype(jnp.bfloat16), gain_term)
        grad_outs = lax.dynamic_update_index_in_dim(grad_outs, grad_bf, b_pick, 0)
        gain_sum = gain_sum + gain_term
        if tick_num + 1 < ticks:
            incoming = from_behind(grad_bf, "pipe", -1)
    gain_grad = lax.psum(gain_sum, ("dp", "expert"))
    segment_out = layer_outs[:MICRO].reshape(1, tok_rows, width)
    segment_grad = grad_outs[:MICRO].reshape(1, tok_rows, width)
    return (segment_out, segment_grad, gain_grad.reshape(1, width))


def swap_cores(value):
    count = lax.axis_size("expert")
    return lax.ppermute(value, "expert", [(e, e ^ 1) for e in range(count)])


def device_number(dp, pipe, expert):
    return (dp * lax.axis_size("pipe") + pipe) * lax.axis_size("expert") + expert


def shifted(value, dp_step, chip_step, pipe_step):
    dps, pipes, experts = (lax.axis_size(name) for name in ("dp", "pipe", "expert"))
    pairs = []
    for dp in range(dps):
        for pipe in range(pipes):
            for expert in range(experts):
                target = device_number(
                    (dp + dp_step) % dps,
                    (pipe + pipe_step) % pipes,
                    (expert + 2 * chip_step) % experts,
                )
                pairs.append((device_number(dp, pipe, expert), target))
    return lax.ppermute(value, ("dp", "pipe", "expert"), pairs)


def chip_steps():
    dps, chips = lax.axis_size("dp"), lax.axis_size("expert") // 2
    steps = [(d, c) for d in range(dps) for c in range(chips)]
    return sorted(steps[1:], key=lambda step: -(step[0] + step[1]))


def spread(rows):
    return [rows] + [shifted(rows, d, c, 0) for d, c in chip_steps()]


def collect(blocks):
    dps, chips = lax.axis_size("dp"), lax.axis_size("expert") // 2
    back = [shifted(block, -d % dps, -c % chips, 0) for block, (d, c) in zip(blocks[1:], chip_steps())]
    return [blocks[0]] + back


VMEM = pl.BlockSpec(memory_space=pltpu.VMEM)
CHUNK = 256
HALVES = 2


def in_vmem(kernel, outs, scratch, flops, *operands, specs=None):
    moved = sum(math.prod(a.shape) * a.dtype.itemsize for a in [*outs, *operands])
    return pl.pallas_call(
        kernel,
        out_shape=outs,
        in_specs=specs or [VMEM] * len(operands),
        out_specs=[VMEM] * len(outs),
        scratch_shapes=scratch,
        compiler_params=pltpu.CompilerParams(vmem_limit_bytes=LIMIT),
        cost_estimate=pl.CostEstimate(flops=flops, bytes_accessed=moved, transcendentals=0),
    )(*operands)


def load_kernel(*refs):
    own, pair, outs, sems = refs[:3], refs[3:6], refs[6:10], refs[10]
    ff = own[0].shape[1]
    copies = []
    for e, (gate_ref, up_ref, down_ref) in enumerate((own, pair)):
        copies += [
            pltpu.make_async_copy(gate_ref, outs[e].at[:, :ff], sems.at[3 * e]),
            pltpu.make_async_copy(up_ref, outs[e].at[:, ff:], sems.at[3 * e + 1]),
            pltpu.make_async_copy(down_ref, outs[2 + e], sems.at[3 * e + 2]),
        ]
    for copy in copies:
        copy.start()
    for copy in copies:
        copy.wait()


def loaded(own, pair):
    gate, _, down = own
    joint, down = pltpu.VMEM((gate.shape[0], 2 * gate.shape[1]), gate.dtype), pltpu.VMEM(down.shape, down.dtype)
    specs = [pl.BlockSpec(memory_space=pltpu.HBM)] * 6
    scratch = [pltpu.SemaphoreType.DMA((6,))]
    return in_vmem(load_kernel, [joint, joint, down, down], scratch, 0, *own, *pair, specs=specs)


def stage_kernel(out_ref):
    out_ref[...] = jnp.full(out_ref.shape, lax.axis_index("pipe"), jnp.int32)


def turn_kernel(in_ref, out_ref):
    size = math.gcd(in_ref.shape[0], CHUNK)

    @pl.loop(0, in_ref.shape[0] // size)
    def _(at):
        window = pl.ds(pl.multiple_of(at * size, size), size)
        out_ref[:, window] = in_ref[window, :].T


def turned(part):
    outs = [pltpu.VMEM(part.shape[::-1], part.dtype)]
    return in_vmem(turn_kernel, outs, [], 0, part)[0]


def in_chunks(width):
    half = width // HALVES

    def run(work):
        @pl.loop(0, HALVES)
        def _(at):
            for start in range(0, half, CHUNK):
                work(pl.ds(pl.multiple_of(at * half + start, CHUNK), CHUNK))

    return run


def owner_number():
    return lax.axis_index("dp") * lax.axis_size("expert") + lax.axis_index("expert")


def forward_kernel(blocks, tick, *refs):
    row_refs, table_refs, refs = refs[:blocks], refs[blocks:2 * blocks], refs[2 * blocks:]
    gain_ref, *weight_refs = refs[:5]
    rate_ref, flat_ref, own_ref, *part_refs, pre, hidden = refs[5:]
    rows, width = row_refs[0].shape
    ff = weight_refs[2].shape[0]
    gain = gain_ref[...]
    for k, row_ref in enumerate(row_refs):
        x = row_ref[...].astype(jnp.float32)
        flat_ref[k * rows:(k + 1) * rows, :] = (x * inverse_rms(x) * gain).astype(jnp.bfloat16)
    micro = tick - lax.axis_index("pipe")
    is_valid = (micro >= 0) & (micro < MICRO)
    first = pl.multiple_of(jnp.clip(micro, 0, MICRO - 1) * rows, rows)
    routed = jnp.concatenate([ref[pl.ds(first, rows), :] for ref in table_refs], axis=0).astype(jnp.float32)
    number = lax.broadcasted_iota(jnp.int32, routed.shape, 1)
    me = owner_number()
    for e, owner in enumerate((me, me ^ 1)):
        weight = jnp.sum(jnp.where((number == owner) & is_valid, routed, 0.0), axis=1, keepdims=True)
        for start in range(0, 2 * ff, CHUNK):
            pre[:, start:start + CHUNK] = jnp.dot(
                flat_ref[...], weight_refs[e][:, start:start + CHUNK], preferred_element_type=jnp.float32
            )
        gate_pre, up_pre = pre[:, :ff], pre[:, ff:]
        sigma = jax.nn.sigmoid(gate_pre)
        up_rate = weight * gate_pre * sigma
        hidden[:, e * ff:(e + 1) * ff] = (up_rate * up_pre).astype(jnp.bfloat16)
        rate_ref[:, 2 * e * ff:(2 * e + 1) * ff] = weight * up_pre * sigma * (1.0 + gate_pre * (1.0 - sigma))
        rate_ref[:, (2 * e + 1) * ff:(2 * e + 2) * ff] = up_rate

    @in_chunks(width)
    def _(columns):
        partial = sum(
            jnp.dot(hidden[:, e * ff:(e + 1) * ff], weight_refs[2 + e][:, columns], preferred_element_type=jnp.float32)
            for e in range(2)
        )
        own_ref[:, columns] = row_refs[0][:, columns].astype(jnp.float32) + partial[:rows]
        for k, part_ref in enumerate(part_refs):
            part_ref[:, columns] = partial[(k + 1) * rows:(k + 2) * rows].astype(jnp.bfloat16)


def backward_kernel(blocks, first, picks, saves, *refs):
    row_refs, refs = refs[:blocks], refs[blocks:]
    rate_refs, normed_refs, refs = refs[:saves], refs[saves:2 * saves], refs[2 * saves:]
    weight_refs, (gain_ref, own_ref, *part_refs, flat, rate, normed, hidden, sems) = refs[:4], refs[4:]
    rows, width = row_refs[0].shape
    ff = weight_refs[2].shape[1]
    stage = lax.axis_index("pipe")

    def copies(at):
        return (
            pltpu.make_async_copy(rate_refs[at], rate, sems.at[0]),
            pltpu.make_async_copy(normed_refs[at], normed, sems.at[1]),
        )

    for at in range(saves):
        holders = [s for s, picked in enumerate(picks) if picked == at]

        @pl.when(functools.reduce(jnp.logical_or, [stage == s for s in holders]))
        def _():
            for copy in copies(at):
                copy.start()

    for k, row_ref in enumerate(row_refs):
        flat[k * rows:(k + 1) * rows, :] = row_ref[...]
    micro = first + stage
    kept = jnp.where((micro >= 0) & (micro < MICRO), 1.0, 0.0)
    for e in range(2):
        q = jnp.dot(flat[...], weight_refs[2 + e][...], preferred_element_type=jnp.float32) * kept
        if e == 0:
            for copy in copies(0):
                copy.wait()
        for half in range(2):
            columns = slice((2 * e + half) * ff, (2 * e + half + 1) * ff)
            hidden[:, columns] = (q * rate[:, columns]).astype(jnp.bfloat16)

    @in_chunks(width)
    def _(columns):
        partial = sum(
            jnp.dot(
                hidden[:, 2 * e * ff:(2 * e + 2) * ff], weight_refs[e][:, columns], preferred_element_type=jnp.float32
            )
            for e in range(2)
        )
        gain_ref[:, columns] = jnp.sum(partial * normed[:, columns].astype(jnp.float32), axis=0, keepdims=True)
        own_ref[:, columns] = partial[:rows]
        for k, part_ref in enumerate(part_refs):
            part_ref[:, columns] = partial[(k + 1) * rows:(k + 2) * rows].astype(jnp.bfloat16)


def forward_experts(tick, row_blocks, tables, gain, weights):
    blocks, (rows, width) = len(row_blocks), row_blocks[0].shape
    total, ff = blocks * rows, weights[2].shape[0]
    outs = [
        jax.ShapeDtypeStruct((total, 4 * ff), jnp.float32),
        jax.ShapeDtypeStruct((total, width), jnp.bfloat16),
        jax.ShapeDtypeStruct((rows, width), jnp.float32),
    ]
    outs += [jax.ShapeDtypeStruct((rows, width), jnp.bfloat16)] * (blocks - 1)
    scratch = [pltpu.VMEM((total, 2 * ff), jnp.float32), pltpu.VMEM((total, 2 * ff), jnp.bfloat16)]
    kernel = functools.partial(forward_kernel, blocks, tick)
    flops = 12 * total * width * ff
    rate, normed, *parts = in_vmem(kernel, outs, scratch, flops, *row_blocks, *tables, gain, *weights)
    return rate, normed, parts


def backward_experts(first, picks, row_blocks, rates, normeds, weights):
    blocks, (rows, width) = len(row_blocks), row_blocks[0].shape
    total, wide = rates[0].shape
    outs = [jax.ShapeDtypeStruct((1, width), jnp.float32), jax.ShapeDtypeStruct((rows, width), jnp.float32)]
    outs += [jax.ShapeDtypeStruct((rows, width), jnp.bfloat16)] * (blocks - 1)
    scratch = [
        pltpu.VMEM((total, width), jnp.bfloat16),
        pltpu.VMEM((total, wide), jnp.float32),
        pltpu.VMEM((total, width), jnp.bfloat16),
        pltpu.VMEM((total, wide), jnp.bfloat16),
        pltpu.SemaphoreType.DMA((2,)),
    ]
    used = sorted(set(picks))
    kernel = functools.partial(backward_kernel, blocks, first, [used.index(at) for at in picks], len(used))
    anywhere = pl.BlockSpec(memory_space=pl.ANY)
    specs = [VMEM] * blocks + [anywhere] * (2 * len(used)) + [VMEM] * 4
    saved = [rates[at] for at in used] + [normeds[at] for at in used]
    flops = 3 * total * width * wide
    gained, *parts = in_vmem(kernel, outs, scratch, flops, *row_blocks, *saved, *weights, specs=specs)
    return gained, parts


def summed_over_owners(value):
    dps, chips = lax.axis_size("dp"), lax.axis_size("expert") // 2
    value = value + swap_cores(value)
    total = value
    for step in range(1, chips):
        total = total + shifted(value, 0, step, 0)
    value = total
    for step in range(1, dps):
        total = total + shifted(value, step, 0, 0)
    return total


def dense_body(tokens, cotangent, owner_ids, gate_weights, norm_gain, w_gate, w_up, w_down):
    f32, bf16 = jnp.float32, jnp.bfloat16
    stages = lax.axis_size("pipe")
    owners = lax.axis_size("dp") * lax.axis_size("expert")
    tok_rows, width = tokens.shape
    rows = tok_rows // MICRO
    gain = norm_gain[0][None, :]
    ticks = MICRO + stages - 1
    stage = in_vmem(stage_kernel, [jax.ShapeDtypeStruct((1, width), jnp.int32)], [], 0)[0]

    own = [pltpu.with_memory_space_constraint(w[0, 0], pltpu.HBM) for w in (w_gate, w_up, w_down)]
    theirs = [swap_cores(w) for w in own]
    theirs = [pltpu.with_memory_space_constraint(w, pltpu.HBM) for w in theirs]
    forward_weights = loaded(own, theirs)
    backward_weights = []
    for number, part in enumerate(forward_weights):
        backward_weights.append(turned(part))

    onehot = owner_ids[0][:, :, None] == jnp.arange(owners, dtype=jnp.int32)
    table = jnp.sum(jnp.where(onehot, gate_weights[0].astype(f32)[:, :, None], 0.0), axis=1).astype(bf16)
    tables = spread(table)

    def choose(values):
        found = values[0]
        for s, value in enumerate(values):
            if value is not found:
                found = jnp.where(stage == s, value, found)
        return found

    rates, normeds, ins, outs, grads = [], [], [], [], []
    gain_sum = jnp.zeros((1, width), f32)
    behind = ahead = None
    last = ticks + stages - 2
    for tick in range(last + 1):
        if tick < ticks:
            if tick == 0:
                here = tokens[:rows]
            elif tick < MICRO:
                here = jnp.where(stage == 0, tokens[tick * rows:(tick + 1) * rows], behind)
            else:
                here = behind
            here_blocks = spread(here)
            rate, normed, parts = forward_experts(tick, here_blocks, tables, gain, forward_weights)
            parts = collect(parts)
            out = lax.optimization_barrier(sum(p.astype(f32) for p in parts).astype(bf16))
            rates.append(rate)
            normeds.append(normed)
            ins.append(here)
            outs.append(out)
            if tick + 1 < ticks:
                behind = shifted(out, 0, 0, 1)
        number = tick - (stages - 1)
        if number >= 0:
            first = number - (stages - 1)
            picks = [min(max(first + 2 * s, 0), min(ticks - 1, tick)) for s in range(stages)]
            if number == 0:
                grad = cotangent[:rows]
            elif number < MICRO:
                grad = jnp.where(stage == stages - 1, cotangent[number * rows:(number + 1) * rows], ahead)
            else:
                grad = ahead
            grad_blocks = spread(grad)
            gained, parts = backward_experts(first, picks, grad_blocks, rates, normeds, backward_weights)
            parts = collect(parts)
            normed_grad = sum(p.astype(f32) for p in parts)
            x = choose([ins[at] for at in picks]).astype(f32)
            scale = inverse_rms(x)
            weighted = gain * normed_grad
            grad_x = (
                grad.astype(f32)
                + scale * weighted
                - x * scale * scale * scale * jnp.mean(weighted * x, axis=-1, keepdims=True)
            ).astype(bf16)
            gain_sum = gain_sum + gained
            if tick < last:
                grad_x = lax.optimization_barrier(grad_x)
            grads.append(grad_x)
            if tick < last:
                ahead = shifted(grad_x, 0, 0, -1)
    gain_grad = summed_over_owners(gain_sum) / gain
    segment_out = jnp.concatenate([choose([outs[m + s] for s in range(stages)]) for m in range(MICRO)])
    segment_grad = jnp.concatenate(
        [choose([grads[m + stages - 1 - s] for s in range(stages)]) for m in range(MICRO)]
    )
    return (segment_out[None], segment_grad[None], gain_grad)


def body(tokens, cotangent, owner_ids, *rest):
    owners = lax.axis_size("dp") * lax.axis_size("expert")
    routed_densely = owners <= 2 * owner_ids.shape[2] and lax.axis_size("expert") % 2 == 0
    plan = dense_body if routed_densely else slot_body
    return plan(tokens, cotangent, owner_ids, *rest)


def solution(mesh):
    in_specs = (
        P(("dp", "expert"), None),
        P(("dp", "expert"), None),
        P("pipe", ("dp", "expert"), None),
        P("pipe", ("dp", "expert"), None),
        P("pipe", None),
        P("pipe", ("dp", "expert"), None, None),
        P("pipe", ("dp", "expert"), None, None),
        P("pipe", ("dp", "expert"), None, None),
    )
    out_specs = (
        P("pipe", ("dp", "expert"), None),
        P("pipe", ("dp", "expert"), None),
        P("pipe", None),
    )
    return jax.shard_map(body, mesh=mesh, in_specs=in_specs, out_specs=out_specs, check_vma=False)
```

profile of v0, /device:TPU:0, one launch (start us, length us, event | category | flops | bytes accessed | tf_op | source)
XLA Modules:
  0.0 297.8 jit_solution(16531949140270470870)
XLA Ops:
  3.2 3.6 %collective-permute-start.3 = (bf16[128,8]{1,0:T(8,128)(2,1)S(1)}, bf16[128,8]{1,0:T(8,128)(2,1)S(1)}, u32[]{:S(2)}, u32[]{:S(2)}) collective-permute-start(bf16[128,8]{1,0:T(8,128)(2,1)S(1)} %copy.13.refs_4_), channel_id=1, source_target_pairs={{0,18},{1,19},{2,16},{3,17},{4,22},{5,23},{6,20},{7,21},{8,26},{9,... | collective-permute-start | bytes 6152 | tf_op jit(solution)/shard_map/ppermute | solution.py:260
  13.3 3.8 %shard_map.104 = (bf16[2048,768]{1,0:T(8,128)(2,1)S(1)}, bf16[2048,768]{1,0:T(8,128)(2,1)S(1)}, bf16[384,2048]{1,0:T(8,128)(2,1)S(1)}, bf16[384,2048]{1,0:T(8,128)(2,1)S(1)}) custom-call(bf16[2048,384]{1,0:T(8,128)(2,1)} %bitcast.27, bf16[2048,384]{1,0:T(8,128)(2,1)} %bitcast.29, bf16[384,2048]{1,0:T(8,128)(2,1)} %bitcast.31, bf16[2048,384]{1,0:T(8,128)(2,1)} %copy-done.2, ...), custom_call_target="tpu_custom_call" | custom-call | bytes 18874368 | tf_op jit(solution)/shard_map/pallas_call | solution.py:286
  23.3 2.7 collective-permute-done.11
  26.0 2.5 collective-permute-done.10
  30.3 5.1 %collective-permute-done.12 = bf16[32,2048]{1,0:T(8,128)(2,1)S(1)} collective-permute-done((bf16[32,2048]{1,0:T(8,128)(2,1)S(1)}, bf16[32,2048]{1,0:T(8,128)(2,1)S(1)}, u32[]{:S(2)}, u32[]{:S(2)}) %collective-permute-start.12) | collective-permute-done | bytes 131104 | tf_op jit(solution)/shard_map/ppermute | solution.py:260
  38.9 2.4 collective-permute-done.13.refs_1_
  53.6 6.8 %collective-permute-done.19 = bf16[32,2048]{1,0:T(8,128)(2,1)S(1)} collective-permute-done((bf16[32,2048]{1,0:T(8,128)(2,1)S(1)}, bf16[32,2048]{1,0:T(8,128)(2,1)S(1)}, u32[]{:S(2)}, u32[]{:S(2)}) %collective-permute-start.19) | collective-permute-done | bytes 131104 | tf_op jit(solution)/shard_map/ppermute | solution.py:260
  63.9 3.4 %collective-permute-done.20.refs_1_ = bf16[32,2048]{1,0:T(8,128)(2,1)S(1)} collective-permute-done((bf16[32,2048]{1,0:T(8,128)(2,1)S(1)}, bf16[32,2048]{1,0:T(8,128)(2,1)S(1)}, u32[]{:S(2)}, u32[]{:S(2)}) %collective-permute-start.20) | collective-permute-done | bytes 131104 | tf_op jit(solution)/shard_map/ppermute | solution.py:260
  67.3 2.5 collective-permute-done.21.refs_2_
  80.2 6.8 %collective-permute-done.26 = bf16[32,2048]{1,0:T(8,128)(2,1)S(1)} collective-permute-done((bf16[32,2048]{1,0:T(8,128)(2,1)S(1)}, bf16[32,2048]{1,0:T(8,128)(2,1)S(1)}, u32[]{:S(2)}, u32[]{:S(2)}) %collective-permute-start.26) | collective-permute-done | bytes 131104 | tf_op jit(solution)/shard_map/ppermute | solution.py:260
  104.1 2.4 shard_map.116
  112.9 3.3 %collective-permute-done.57 = bf16[32,2048]{1,0:T(8,128)(2,1)S(1)} collective-permute-done((bf16[32,2048]{1,0:T(8,128)(2,1)S(1)}, bf16[32,2048]{1,0:T(8,128)(2,1)S(1)}, u32[]{:S(2)}, u32[]{:S(2)}) %collective-permute-start.57) | collective-permute-done | bytes 131104 | tf_op jit(solution)/shard_map/ppermute | solution.py:260
  142.3 3.4 %collective-permute-start.67 = (bf16[32,2048]{1,0:T(8,128)(2,1)S(1)}, bf16[32,2048]{1,0:T(8,128)(2,1)S(1)}, u32[]{:S(2)}, u32[]{:S(2)}) collective-permute-start(bf16[32,2048]{1,0:T(8,128)(2,1)S(1)} %fusion.12), channel_id=1, source_target_pairs={{0,12},{1,13},{2,14},{3,15},{4,0},{5,1},{6,2},{7,3},{8,4},{9,5},{1... | collective-permute-start | bytes 393224 | tf_op jit(solution)/shard_map/ppermute | solution.py:260
  158.5 2.9 collective-permute-start.44
  164.5 2.9 collective-permute-start.71
  167.5 2.6 collective-permute-done.73
  177.8 3.2 %collective-permute-done.48.refs_1_ = bf16[32,2048]{1,0:T(8,128)(2,1)S(1)} collective-permute-done((bf16[32,2048]{1,0:T(8,128)(2,1)S(1)}, bf16[32,2048]{1,0:T(8,128)(2,1)S(1)}, u32[]{:S(2)}, u32[]{:S(2)}) %collective-permute-start.48) | collective-permute-done | bytes 131104 | tf_op jit(solution)/shard_map/ppermute | solution.py:260
  196.7 2.5 collective-permute-done.75.refs_1_
  199.1 4.1 %collective-permute-done.76.refs_2_ = bf16[32,2048]{1,0:T(8,128)(2,1)S(1)} collective-permute-done((bf16[32,2048]{1,0:T(8,128)(2,1)S(1)}, bf16[32,2048]{1,0:T(8,128)(2,1)S(1)}, u32[]{:S(2)}, u32[]{:S(2)}) %collective-permute-start.76) | collective-permute-done | bytes 131104 | tf_op jit(solution)/shard_map/ppermute | solution.py:260
  203.2 2.4 shard_map.119
  209.1 2.9 collective-permute-done.80
  215.1 3.5 %collective-permute-start.81 = (bf16[32,2048]{1,0:T(8,128)(2,1)S(1)}, bf16[32,2048]{1,0:T(8,128)(2,1)S(1)}, u32[]{:S(2)}, u32[]{:S(2)}) collective-permute-start(bf16[32,2048]{1,0:T(8,128)(2,1)S(1)} %fusion.26), channel_id=1, source_target_pairs={{0,12},{1,13},{2,14},{3,15},{4,0},{5,1},{6,2},{7,3},{8,4},{9,5},{1... | collective-permute-start | bytes 393224 | tf_op jit(solution)/shard_map/ppermute | solution.py:260
  218.6 2.5 collective-permute-done.81.refs_0_
  224.6 2.5 collective-permute-done.82.refs_1_
  228.4 2.4 shard_map.120
  239.3 4.2 %collective-permute-start.88 = (bf16[32,2048]{1,0:T(8,128)(2,1)S(1)}, bf16[32,2048]{1,0:T(8,128)(2,1)S(1)}, u32[]{:S(2)}, u32[]{:S(2)}) collective-permute-start(bf16[32,2048]{1,0:T(8,128)(2,1)S(1)} %fusion.33), channel_id=1, source_target_pairs={{0,12},{1,13},{2,14},{3,15},{4,0},{5,1},{6,2},{7,3},{8,4},{9,5},{1... | collective-permute-start | bytes 393224 | tf_op jit(solution)/shard_map/ppermute | solution.py:260
  243.5 2.5 collective-permute-done.88.refs_0_
  249.5 2.5 collective-permute-done.89.refs_1_
  264.5 4.3 %collective-permute-start.95 = (bf16[32,2048]{1,0:T(8,128)(2,1)S(1)}, bf16[32,2048]{1,0:T(8,128)(2,1)S(1)}, u32[]{:S(2)}, u32[]{:S(2)}) collective-permute-start(bf16[32,2048]{1,0:T(8,128)(2,1)S(1)} %fusion.40), channel_id=1, source_target_pairs={{0,12},{1,13},{2,14},{3,15},{4,0},{5,1},{6,2},{7,3},{8,4},{9,5},{1... | collective-permute-start | bytes 393224 | tf_op jit(solution)/shard_map/ppermute | solution.py:260
  268.8 2.5 collective-permute-done.95.refs_0_
  274.8 2.5 collective-permute-done.96.refs_1_
  283.5 2.4 collective-permute-done.103
  (260 shorter events, 192.9 us)
Async XLA Ops:
  0.6 10.0 %collective-permute-start.6 = (bf16[2048,384]{1,0:T(8,128)(2,1)}, bf16[2048,384]{1,0:T(8,128)(2,1)S(1)}, u32[]{:S(2)}, u32[]{:S(2)}) collective-permute-start(bf16[2048,384]{1,0:T(8,128)(2,1)} %bitcast.26), channel_id=1, source_target_pairs={{0,1},{1,0},{2,3},{3,2},{4,5},{5,4},{6,7},{7,6},{8,9},{9,8},{10,11... | collective-permute-start | bytes 4718600 | tf_op jit(solution)/shard_map/ppermute | solution.py:241
  1.2 11.0 %collective-permute-start.7 = (bf16[2048,384]{1,0:T(8,128)(2,1)}, bf16[2048,384]{1,0:T(8,128)(2,1)S(1)}, u32[]{:S(2)}, u32[]{:S(2)}) collective-permute-start(bf16[2048,384]{1,0:T(8,128)(2,1)} %bitcast.28), channel_id=1, source_target_pairs={{0,1},{1,0},{2,3},{3,2},{4,5},{5,4},{6,7},{7,6},{8,9},{9,8},{10,11... | collective-permute-start | bytes 4718600 | tf_op jit(solution)/shard_map/ppermute | solution.py:241
  1.3 11.4 %collective-permute-start.8 = (bf16[384,2048]{1,0:T(8,128)(2,1)}, bf16[384,2048]{1,0:T(8,128)(2,1)}, u32[]{:S(2)}, u32[]{:S(2)}) collective-permute-start(bf16[384,2048]{1,0:T(8,128)(2,1)} %bitcast.30), channel_id=1, source_target_pairs={{0,1},{1,0},{2,3},{3,2},{4,5},{5,4},{6,7},{7,6},{8,9},{9,8},{10,11... | collective-permute-start | bytes 4718600 | tf_op jit(solution)/shard_map/ppermute | solution.py:241
  7.7 9.8 %collective-permute-start = (bf16[32,2048]{1,0:T(8,128)(2,1)S(1)}, bf16[32,2048]{1,0:T(8,128)(2,1)S(1)}, u32[]{:S(2)}, u32[]{:S(2)}) collective-permute-start(bf16[32,2048]{1,0:T(8,128)(2,1)S(1)} %slice.27.refs_0_), channel_id=1, source_target_pairs={{0,18},{1,19},{2,16},{3,17},{4,22},{5,23},{6,20},{7,21},{8,26},{9,... | collective-permute-start | bytes 393224 | tf_op jit(solution)/shard_map/ppermute | solution.py:260
  8.7 8.8 %collective-permute-start.1 = (bf16[32,2048]{1,0:T(8,128)(2,1)S(1)}, bf16[32,2048]{1,0:T(8,128)(2,1)S(1)}, u32[]{:S(2)}, u32[]{:S(2)}) collective-permute-start(bf16[32,2048]{1,0:T(8,128)(2,1)S(1)} %slice.27.refs_0_), channel_id=1, source_target_pairs={{0,2},{1,3},{2,0},{3,1},{4,6},{5,7},{6,4},{7,5},{8,10},{9,11},{10,... | collective-permute-start | bytes 393224 | tf_op jit(solution)/shard_map/ppermute | solution.py:260
  20.8 7.6 %collective-permute-start.10 = (bf16[32,2048]{1,0:T(8,128)(2,1)S(1)}, bf16[32,2048]{1,0:T(8,128)(2,1)S(1)}, u32[]{:S(2)}, u32[]{:S(2)}) collective-permute-start(bf16[32,2048]{1,0:T(8,128)(2,1)S(1)} %get-tuple-element.90), channel_id=1, source_target_pairs={{0,2},{1,3},{2,0},{3,1},{4,6},{5,7},{6,4},{7,5},{8,10},{9,11},{10,... | collective-permute-start | bytes 393224 | tf_op jit(solution)/shard_map/ppermute | solution.py:260
  61.6 8.2 %collective-permute-start.21 = (bf16[32,2048]{1,0:T(8,128)(2,1)S(1)}, bf16[32,2048]{1,0:T(8,128)(2,1)S(1)}, u32[]{:S(2)}, u32[]{:S(2)}) collective-permute-start(bf16[32,2048]{1,0:T(8,128)(2,1)S(1)} %slice_select_fusion.4.refs_0_), channel_id=1, source_target_pairs={{0,2},{1,3},{2,0},{3,1},{4,6},{5,7},{6,4},{7,5},{8,10},{9,11},{10,... | collective-permute-start | bytes 393224 | tf_op jit(solution)/shard_map/ppermute | solution.py:260
  90.6 8.5 %collective-permute-start.54 = (bf16[32,2048]{1,0:T(8,128)(2,1)S(1)}, bf16[32,2048]{1,0:T(8,128)(2,1)S(1)}, u32[]{:S(2)}, u32[]{:S(2)}) collective-permute-start(bf16[32,2048]{1,0:T(8,128)(2,1)S(1)} %slice.28.refs_0_), channel_id=1, source_target_pairs={{0,18},{1,19},{2,16},{3,17},{4,22},{5,23},{6,20},{7,21},{8,26},{9,... | collective-permute-start | bytes 393224 | tf_op jit(solution)/shard_map/ppermute | solution.py:260
  92.5 11.5 %collective-permute-start.55 = (bf16[32,2048]{1,0:T(8,128)(2,1)S(1)}, bf16[32,2048]{1,0:T(8,128)(2,1)S(1)}, u32[]{:S(2)}, u32[]{:S(2)}) collective-permute-start(bf16[32,2048]{1,0:T(8,128)(2,1)S(1)} %slice.28.refs_0_), channel_id=1, source_target_pairs={{0,2},{1,3},{2,0},{3,1},{4,6},{5,7},{6,4},{7,5},{8,10},{9,11},{10,... | collective-permute-start | bytes 393224 | tf_op jit(solution)/shard_map/ppermute | solution.py:260
  93.1 10.9 %collective-permute-start.56 = (bf16[32,2048]{1,0:T(8,128)(2,1)S(1)}, bf16[32,2048]{1,0:T(8,128)(2,1)S(1)}, u32[]{:S(2)}, u32[]{:S(2)}) collective-permute-start(bf16[32,2048]{1,0:T(8,128)(2,1)S(1)} %slice.28.refs_0_), channel_id=1, source_target_pairs={{0,16},{1,17},{2,18},{3,19},{4,20},{5,21},{6,22},{7,23},{8,24},{9,... | collective-permute-start | bytes 393224 | tf_op jit(solution)/shard_map/ppermute | solution.py:260
  96.7 12.1 %collective-permute-start.32 = (bf16[32,2048]{1,0:T(8,128)(2,1)S(1)}, bf16[32,2048]{1,0:T(8,128)(2,1)S(1)}, u32[]{:S(2)}, u32[]{:S(2)}) collective-permute-start(bf16[32,2048]{1,0:T(8,128)(2,1)S(1)} %get-tuple-element.103), channel_id=1, source_target_pairs={{0,16},{1,17},{2,18},{3,19},{4,20},{5,21},{6,22},{7,23},{8,24},{9,... | collective-permute-start | bytes 393224 | tf_op jit(solution)/shard_map/ppermute | solution.py:260
  97.8 12.3 %collective-permute-start.31 = (bf16[32,2048]{1,0:T(8,128)(2,1)S(1)}, bf16[32,2048]{1,0:T(8,128)(2,1)S(1)}, u32[]{:S(2)}, u32[]{:S(2)}) collective-permute-start(bf16[32,2048]{1,0:T(8,128)(2,1)S(1)} %get-tuple-element.102), channel_id=1, source_target_pairs={{0,2},{1,3},{2,0},{3,1},{4,6},{5,7},{6,4},{7,5},{8,10},{9,11},{10,... | collective-permute-start | bytes 393224 | tf_op jit(solution)/shard_map/ppermute | solution.py:260
  99.1 11.0 %collective-permute-start.30 = (bf16[32,2048]{1,0:T(8,128)(2,1)S(1)}, bf16[32,2048]{1,0:T(8,128)(2,1)S(1)}, u32[]{:S(2)}, u32[]{:S(2)}) collective-permute-start(bf16[32,2048]{1,0:T(8,128)(2,1)S(1)} %get-tuple-element.101), channel_id=1, source_target_pairs={{0,18},{1,19},{2,16},{3,17},{4,22},{5,23},{6,20},{7,21},{8,26},{9,... | collective-permute-start | bytes 393224 | tf_op jit(solution)/shard_map/ppermute | solution.py:260
  108.8 7.5 %collective-permute-start.57 = (bf16[32,2048]{1,0:T(8,128)(2,1)S(1)}, bf16[32,2048]{1,0:T(8,128)(2,1)S(1)}, u32[]{:S(2)}, u32[]{:S(2)}) collective-permute-start(bf16[32,2048]{1,0:T(8,128)(2,1)S(1)} %get-tuple-element.123), channel_id=1, source_target_pairs={{0,18},{1,19},{2,16},{3,17},{4,22},{5,23},{6,20},{7,21},{8,26},{9,... | collective-permute-start | bytes 393224 | tf_op jit(solution)/shard_map/ppermute | solution.py:260
  121.8 7.6 %collective-permute-start.61 = (bf16[32,2048]{1,0:T(8,128)(2,1)S(1)}, bf16[32,2048]{1,0:T(8,128)(2,1)S(1)}, u32[]{:S(2)}, u32[]{:S(2)}) collective-permute-start(bf16[32,2048]{1,0:T(8,128)(2,1)S(1)} %slice_select_fusion.2.refs_0_), channel_id=1, source_target_pairs={{0,18},{1,19},{2,16},{3,17},{4,22},{5,23},{6,20},{7,21},{8,26},{9,... | collective-permute-start | bytes 393224 | tf_op jit(solution)/shard_map/ppermute | solution.py:260
  123.1 7.9 %collective-permute-start.62 = (bf16[32,2048]{1,0:T(8,128)(2,1)S(1)}, bf16[32,2048]{1,0:T(8,128)(2,1)S(1)}, u32[]{:S(2)}, u32[]{:S(2)}) collective-permute-start(bf16[32,2048]{1,0:T(8,128)(2,1)S(1)} %slice_select_fusion.2.refs_0_), channel_id=1, source_target_pairs={{0,2},{1,3},{2,0},{3,1},{4,6},{5,7},{6,4},{7,5},{8,10},{9,11},{10,... | collective-permute-start | bytes 393224 | tf_op jit(solution)/shard_map/ppermute | solution.py:260
  127.5 7.9 %collective-permute-start.39 = (bf16[32,2048]{1,0:T(8,128)(2,1)S(1)}, bf16[32,2048]{1,0:T(8,128)(2,1)S(1)}, u32[]{:S(2)}, u32[]{:S(2)}) collective-permute-start(bf16[32,2048]{1,0:T(8,128)(2,1)S(1)} %get-tuple-element.107), channel_id=1, source_target_pairs={{0,16},{1,17},{2,18},{3,19},{4,20},{5,21},{6,22},{7,23},{8,24},{9,... | collective-permute-start | bytes 393224 | tf_op jit(solution)/shard_map/ppermute | solution.py:260
  128.2 9.4 %collective-permute-start.38 = (bf16[32,2048]{1,0:T(8,128)(2,1)S(1)}, bf16[32,2048]{1,0:T(8,128)(2,1)S(1)}, u32[]{:S(2)}, u32[]{:S(2)}) collective-permute-start(bf16[32,2048]{1,0:T(8,128)(2,1)S(1)} %get-tuple-element.106), channel_id=1, source_target_pairs={{0,2},{1,3},{2,0},{3,1},{4,6},{5,7},{6,4},{7,5},{8,10},{9,11},{10,... | collective-permute-start | bytes 393224 | tf_op jit(solution)/shard_map/ppermute | solution.py:260
  129.4 8.2 %collective-permute-start.37 = (bf16[32,2048]{1,0:T(8,128)(2,1)S(1)}, bf16[32,2048]{1,0:T(8,128)(2,1)S(1)}, u32[]{:S(2)}, u32[]{:S(2)}) collective-permute-start(bf16[32,2048]{1,0:T(8,128)(2,1)S(1)} %get-tuple-element.105), channel_id=1, source_target_pairs={{0,18},{1,19},{2,16},{3,17},{4,22},{5,23},{6,20},{7,21},{8,26},{9,... | collective-permute-start | bytes 393224 | tf_op jit(solution)/shard_map/ppermute | solution.py:260
  137.7 8.0 %collective-permute-start.40 = (bf16[32,2048]{1,0:T(8,128)(2,1)S(1)}, bf16[32,2048]{1,0:T(8,128)(2,1)S(1)}, u32[]{:S(2)}, u32[]{:S(2)}) collective-permute-start(bf16[32,2048]{1,0:T(8,128)(2,1)S(1)} %add_convert_fusion.2), channel_id=1, source_target_pairs={{0,4},{1,5},{2,6},{3,7},{4,8},{5,9},{6,10},{7,11},{8,12},{9,13},{1... | collective-permute-start | bytes 393224 | tf_op jit(solution)/shard_map/ppermute | solution.py:260
  147.1 8.6 %collective-permute-start.42 = (bf16[32,2048]{1,0:T(8,128)(2,1)S(1)}, bf16[32,2048]{1,0:T(8,128)(2,1)S(1)}, u32[]{:S(2)}, u32[]{:S(2)}) collective-permute-start(bf16[32,2048]{1,0:T(8,128)(2,1)S(1)} %collective-permute-done.40.refs_0_), channel_id=1, source_target_pairs={{0,2},{1,3},{2,0},{3,1},{4,6},{5,7},{6,4},{7,5},{8,10},{9,11},{10,... | collective-permute-start | bytes 393224 | tf_op jit(solution)/shard_map/ppermute | solution.py:260
  149.2 9.3 %collective-permute-start.68 = (bf16[32,2048]{1,0:T(8,128)(2,1)S(1)}, bf16[32,2048]{1,0:T(8,128)(2,1)S(1)}, u32[]{:S(2)}, u32[]{:S(2)}) collective-permute-start(bf16[32,2048]{1,0:T(8,128)(2,1)S(1)} %slice_select_fusion.1.refs_0_), channel_id=1, source_target_pairs={{0,18},{1,19},{2,16},{3,17},{4,22},{5,23},{6,20},{7,21},{8,26},{9,... | collective-permute-start | bytes 393224 | tf_op jit(solution)/shard_map/ppermute | solution.py:260
  150.7 10.8 %collective-permute-start.69 = (bf16[32,2048]{1,0:T(8,128)(2,1)S(1)}, bf16[32,2048]{1,0:T(8,128)(2,1)S(1)}, u32[]{:S(2)}, u32[]{:S(2)}) collective-permute-start(bf16[32,2048]{1,0:T(8,128)(2,1)S(1)} %slice_select_fusion.1.refs_0_), channel_id=1, source_target_pairs={{0,2},{1,3},{2,0},{3,1},{4,6},{5,7},{6,4},{7,5},{8,10},{9,11},{10,... | collective-permute-start | bytes 393224 | tf_op jit(solution)/shard_map/ppermute | solution.py:260
  152.5 9.0 %collective-permute-start.70 = (bf16[32,2048]{1,0:T(8,128)(2,1)S(1)}, bf16[32,2048]{1,0:T(8,128)(2,1)S(1)}, u32[]{:S(2)}, u32[]{:S(2)}) collective-permute-start(bf16[32,2048]{1,0:T(8,128)(2,1)S(1)} %slice_select_fusion.1.refs_0_), channel_id=1, source_target_pairs={{0,16},{1,17},{2,18},{3,19},{4,20},{5,21},{6,22},{7,23},{8,24},{9,... | collective-permute-start | bytes 393224 | tf_op jit(solution)/shard_map/ppermute | solution.py:260
  158.0 9.4 %collective-permute-start.45 = (bf16[32,2048]{1,0:T(8,128)(2,1)S(1)}, bf16[32,2048]{1,0:T(8,128)(2,1)S(1)}, u32[]{:S(2)}, u32[]{:S(2)}) collective-permute-start(bf16[32,2048]{1,0:T(8,128)(2,1)S(1)} %get-tuple-element.110), channel_id=1, source_target_pairs={{0,2},{1,3},{2,0},{3,1},{4,6},{5,7},{6,4},{7,5},{8,10},{9,11},{10,... | collective-permute-start | bytes 393224 | tf_op jit(solution)/shard_map/ppermute | solution.py:260
  158.5 8.9 %collective-permute-start.44 = (bf16[32,2048]{1,0:T(8,128)(2,1)S(1)}, bf16[32,2048]{1,0:T(8,128)(2,1)S(1)}, u32[]{:S(2)}, u32[]{:S(2)}) collective-permute-start(bf16[32,2048]{1,0:T(8,128)(2,1)S(1)} %get-tuple-element.109), channel_id=1, source_target_pairs={{0,18},{1,19},{2,16},{3,17},{4,22},{5,23},{6,20},{7,21},{8,26},{9,... | collective-permute-start | bytes 393224 | tf_op jit(solution)/shard_map/ppermute | solution.py:260
  164.5 7.9 %collective-permute-start.71 = (bf16[32,2048]{1,0:T(8,128)(2,1)S(1)}, bf16[32,2048]{1,0:T(8,128)(2,1)S(1)}, u32[]{:S(2)}, u32[]{:S(2)}) collective-permute-start(bf16[32,2048]{1,0:T(8,128)(2,1)S(1)} %get-tuple-element.137), channel_id=1, source_target_pairs={{0,18},{1,19},{2,16},{3,17},{4,22},{5,23},{6,20},{7,21},{8,26},{9,... | collective-permute-start | bytes 393224 | tf_op jit(solution)/shard_map/ppermute | solution.py:260
  185.0 7.8 %collective-permute-start.52 = (bf16[32,2048]{1,0:T(8,128)(2,1)S(1)}, bf16[32,2048]{1,0:T(8,128)(2,1)S(1)}, u32[]{:S(2)}, u32[]{:S(2)}) collective-permute-start(bf16[32,2048]{1,0:T(8,128)(2,1)S(1)} %get-tuple-element.114), channel_id=1, source_target_pairs={{0,2},{1,3},{2,0},{3,1},{4,6},{5,7},{6,4},{7,5},{8,10},{9,11},{10,... | collective-permute-start | bytes 393224 | tf_op jit(solution)/shard_map/ppermute | solution.py:260
  194.9 8.3 %collective-permute-start.76 = (bf16[32,2048]{1,0:T(8,128)(2,1)S(1)}, bf16[32,2048]{1,0:T(8,128)(2,1)S(1)}, u32[]{:S(2)}, u32[]{:S(2)}) collective-permute-start(bf16[32,2048]{1,0:T(8,128)(2,1)S(1)} %get-tuple-element.198.refs_0_), channel_id=1, source_target_pairs={{0,2},{1,3},{2,0},{3,1},{4,6},{5,7},{6,4},{7,5},{8,10},{9,11},{10,... | collective-permute-start | bytes 393224 | tf_op jit(solution)/shard_map/ppermute | solution.py:260
  195.6 7.6 %collective-permute-start.77 = (bf16[32,2048]{1,0:T(8,128)(2,1)S(1)}, bf16[32,2048]{1,0:T(8,128)(2,1)S(1)}, u32[]{:S(2)}, u32[]{:S(2)}) collective-permute-start(bf16[32,2048]{1,0:T(8,128)(2,1)S(1)} %get-tuple-element.198.refs_0_), channel_id=1, source_target_pairs={{0,16},{1,17},{2,18},{3,19},{4,20},{5,21},{6,22},{7,23},{8,24},{9,... | collective-permute-start | bytes 393224 | tf_op jit(solution)/shard_map/ppermute | solution.py:260
  206.2 7.3 %collective-permute-start.79 = (bf16[32,2048]{1,0:T(8,128)(2,1)S(1)}, bf16[32,2048]{1,0:T(8,128)(2,1)S(1)}, u32[]{:S(2)}, u32[]{:S(2)}) collective-permute-start(bf16[32,2048]{1,0:T(8,128)(2,1)S(1)} %get-tuple-element.144), channel_id=1, source_target_pairs={{0,2},{1,3},{2,0},{3,1},{4,6},{5,7},{6,4},{7,5},{8,10},{9,11},{10,... | collective-permute-start | bytes 393224 | tf_op jit(solution)/shard_map/ppermute | solution.py:260
  288.9 7.4 %collective-permute-start.100 = (bf16[32,2048]{1,0:T(8,128)(2,1)S(1)}, bf16[32,2048]{1,0:T(8,128)(2,1)S(1)}, u32[]{:S(2)}, u32[]{:S(2)}) collective-permute-start(bf16[32,2048]{1,0:T(8,128)(2,1)S(1)} %get-tuple-element.156), channel_id=1, source_target_pairs={{0,2},{1,3},{2,0},{3,1},{4,6},{5,7},{6,4},{7,5},{8,10},{9,11},{10,... | collective-permute-start | bytes 393224 | tf_op jit(solution)/shard_map/ppermute | solution.py:260
  (78 other events, 494.7 us)
where the time goes:
time: 298 us
  starting transfers between devices  128 us (43%)
  waiting for transfers between devices  120 us (40%)
  Pallas kernels  39.2 us (13%)
  other arithmetic  8.01 us (3%)
    ppermute x101, starting transfers between devices, shifted(): return lax.ppermute(value, ('dp', 'pipe', 'expert'), pairs)  127 us
    ppermute x101, waiting for transfers between devices, shifted(): return lax.ppermute(value, ('dp', 'pipe', 'expert'), pairs)  119 us
    pallas_call x20, Pallas kernels, in_vmem(): pl.pallas_call(kernel, out_shape=outs, in_specs=specs or [VMEM] * len(ope...  39.2 us
  transfers between devices with their start and end apart: 105, of which 65 were waited for; matrix products, arithmetic and copies ran while one was open for 2% of the time, Pallas kernels for 7%

commit v1 on v0

--- a/solution.py
+++ b/solution.py
@@ -480,15 +480,8 @@
 
 
 def summed_over_owners(value):
-    dps, chips = lax.axis_size("dp"), lax.axis_size("expert") // 2
     value = value + swap_cores(value)
-    total = value
-    for step in range(1, chips):
-        total = total + shifted(value, 0, step, 0)
-    value = total
-    for step in range(1, dps):
-        total = total + shifted(value, step, 0, 0)
-    return total
+    return sum(spread(value))
 
 
 def dense_body(tokens, cotangent, owner_ids, gate_weights, norm_gain, w_gate, w_up, w_down):
@@ -534,14 +527,13 @@
                 here = behind
             here_blocks = spread(here)
             rate, normed, parts = forward_experts(tick, here_blocks, tables, gain, forward_weights)
-            parts = collect(parts)
-            out = lax.optimization_barrier(sum(p.astype(f32) for p in parts).astype(bf16))
             rates.append(rate)
             normeds.append(normed)
             ins.append(here)
-            outs.append(out)
             if tick + 1 < ticks:
-                behind = shifted(out, 0, 0, 1)
+                parts = collect(parts)
+                outs.append(lax.optimization_barrier(sum(p.astype(f32) for p in parts).astype(bf16)))
+                behind = shifted(outs[-1], 0, 0, 1)
         number = tick - (stages - 1)
         if number >= 0:
             first = number - (stages - 1)
@@ -553,9 +545,9 @@
             else:
                 grad = ahead
             grad_blocks = spread(grad)
-            gained, parts = backward_experts(first, picks, grad_blocks, rates, normeds, backward_weights)
-            parts = collect(parts)
-            normed_grad = sum(p.astype(f32) for p in parts)
+            gained, sums = backward_experts(first, picks, grad_blocks, rates, normeds, backward_weights)
+            sums = collect(sums)
+            normed_grad = sum(p.astype(f32) for p in sums)
             x = choose([ins[at] for at in picks]).astype(f32)
             scale = inverse_rms(x)
             weighted = gain * normed_grad
@@ -570,6 +562,9 @@
             grads.append(grad_x)
             if tick < last:
                 ahead = shifted(grad_x, 0, 0, -1)
+            if tick + 1 == ticks:
+                parts = collect(lax.optimization_barrier((parts, grad_x))[0])
+                outs.append(sum(p.astype(f32) for p in parts).astype(bf16))
     gain_grad = summed_over_owners(gain_sum) / gain
     segment_out = jnp.concatenate([choose([outs[m + s] for s in range(stages)]) for m in range(MICRO)])
     segment_grad = jnp.concatenate(

time: 298 us -> 281 us (0.943)
  waiting for transfers between devices: 120 us -> 102 us
    ppermute x101 -> x102, waiting for transfers between devices: 119 us -> 102 us  [shifted(): return lax.ppermute(value, ('dp', 'pipe', 'expert'), pairs)]
    ppermute x101 -> x102, starting transfers between devices: 127 us -> 128 us  [shifted(): return lax.ppermute(value, ('dp', 'pipe', 'expert'), pairs)]
  transfers between devices with their start and end apart: 105 -> 106, of which waited for: 65 -> 60; matrix products, arithmetic and copies ran while one was open for 2% -> 2% of each run, Pallas kernels for 7% -> 9%
where the time goes in v1:
time: 281 us
  starting transfers between devices  129 us (46%)
  waiting for transfers between devices  102 us (36%)
  Pallas kernels  39.5 us (14%)
  other arithmetic  8.01 us (3%)
    ppermute x102, starting transfers between devices, shifted(): return lax.ppermute(value, ('dp', 'pipe', 'expert'), pairs)  128 us
    ppermute x102, waiting for transfers between devices, shifted(): return lax.ppermute(value, ('dp', 'pipe', 'expert'), pairs)  102 us
    pallas_call x20, Pallas kernels, in_vmem(): pl.pallas_call(kernel, out_shape=outs, in_specs=specs or [VMEM] * len(ope...  39.5 us
  transfers between devices with their start and end apart: 106, of which 60 were waited for; matrix products, arithmetic and copies ran while one was open for 2% of the time, Pallas kernels for 9%

profile of v1, /device:TPU:0, one launch (start us, length us, event | category | flops | bytes accessed | tf_op | source)
XLA Modules:
  0.0 281.3 jit_solution(15815124286533344347)
XLA Ops:
  3.2 3.6 %collective-permute-start.3 = (bf16[128,8]{1,0:T(8,128)(2,1)S(1)}, bf16[128,8]{1,0:T(8,128)(2,1)S(1)}, u32[]{:S(2)}, u32[]{:S(2)}) collective-permute-start(bf16[128,8]{1,0:T(8,128)(2,1)S(1)} %copy.13.refs_4_), channel_id=1, source_target_pairs={{0,18},{1,19},{2,16},{3,17},{4,22},{5,23},{6,20},{7,21},{8,26},{9,... | collective-permute-start | bytes 6152 | tf_op jit(solution)/shard_map/ppermute | solution.py:260
  13.3 3.8 %shard_map.104 = (bf16[2048,768]{1,0:T(8,128)(2,1)S(1)}, bf16[2048,768]{1,0:T(8,128)(2,1)S(1)}, bf16[384,2048]{1,0:T(8,128)(2,1)S(1)}, bf16[384,2048]{1,0:T(8,128)(2,1)S(1)}) custom-call(bf16[2048,384]{1,0:T(8,128)(2,1)} %bitcast.27, bf16[2048,384]{1,0:T(8,128)(2,1)} %bitcast.29, bf16[384,2048]{1,0:T(8,128)(2,1)} %bitcast.31, bf16[2048,384]{1,0:T(8,128)(2,1)} %copy-done.2, ...), custom_call_target="tpu_custom_call" | custom-call | bytes 18874368 | tf_op jit(solution)/shard_map/pallas_call | solution.py:286
  23.3 2.7 collective-permute-done.11
  26.0 2.5 collective-permute-done.10
  30.3 5.1 %collective-permute-done.12 = bf16[32,2048]{1,0:T(8,128)(2,1)S(1)} collective-permute-done((bf16[32,2048]{1,0:T(8,128)(2,1)S(1)}, bf16[32,2048]{1,0:T(8,128)(2,1)S(1)}, u32[]{:S(2)}, u32[]{:S(2)}) %collective-permute-start.12) | collective-permute-done | bytes 131104 | tf_op jit(solution)/shard_map/ppermute | solution.py:260
  38.9 2.4 collective-permute-done.13.refs_1_
  53.6 6.8 %collective-permute-done.19 = bf16[32,2048]{1,0:T(8,128)(2,1)S(1)} collective-permute-done((bf16[32,2048]{1,0:T(8,128)(2,1)S(1)}, bf16[32,2048]{1,0:T(8,128)(2,1)S(1)}, u32[]{:S(2)}, u32[]{:S(2)}) %collective-permute-start.19) | collective-permute-done | bytes 131104 | tf_op jit(solution)/shard_map/ppermute | solution.py:260
  63.9 3.4 %collective-permute-done.20.refs_1_ = bf16[32,2048]{1,0:T(8,128)(2,1)S(1)} collective-permute-done((bf16[32,2048]{1,0:T(8,128)(2,1)S(1)}, bf16[32,2048]{1,0:T(8,128)(2,1)S(1)}, u32[]{:S(2)}, u32[]{:S(2)}) %collective-permute-start.20) | collective-permute-done | bytes 131104 | tf_op jit(solution)/shard_map/ppermute | solution.py:260
  67.3 2.5 collective-permute-done.21.refs_2_
  80.3 6.8 %collective-permute-done.26 = bf16[32,2048]{1,0:T(8,128)(2,1)S(1)} collective-permute-done((bf16[32,2048]{1,0:T(8,128)(2,1)S(1)}, bf16[32,2048]{1,0:T(8,128)(2,1)S(1)}, u32[]{:S(2)}, u32[]{:S(2)}) %collective-permute-start.26) | collective-permute-done | bytes 131104 | tf_op jit(solution)/shard_map/ppermute | solution.py:260
  104.1 2.4 shard_map.116
  112.9 3.3 %collective-permute-done.54 = bf16[32,2048]{1,0:T(8,128)(2,1)S(1)} collective-permute-done((bf16[32,2048]{1,0:T(8,128)(2,1)S(1)}, bf16[32,2048]{1,0:T(8,128)(2,1)S(1)}, u32[]{:S(2)}, u32[]{:S(2)}) %collective-permute-start.54) | collective-permute-done | bytes 131104 | tf_op jit(solution)/shard_map/ppermute | solution.py:260
  131.0 2.4 shard_map.117
  142.4 3.3 %collective-permute-start.64 = (bf16[32,2048]{1,0:T(8,128)(2,1)S(1)}, bf16[32,2048]{1,0:T(8,128)(2,1)S(1)}, u32[]{:S(2)}, u32[]{:S(2)}) collective-permute-start(bf16[32,2048]{1,0:T(8,128)(2,1)S(1)} %fusion.12), channel_id=1, source_target_pairs={{0,12},{1,13},{2,14},{3,15},{4,0},{5,1},{6,2},{7,3},{8,4},{9,5},{1... | collective-permute-start | bytes 393224 | tf_op jit(solution)/shard_map/ppermute | solution.py:260
  158.5 3.1 %collective-permute-start.44 = (bf16[32,2048]{1,0:T(8,128)(2,1)S(1)}, bf16[32,2048]{1,0:T(8,128)(2,1)S(1)}, u32[]{:S(2)}, u32[]{:S(2)}) collective-permute-start(bf16[32,2048]{1,0:T(8,128)(2,1)S(1)} %get-tuple-element.113), channel_id=1, source_target_pairs={{0,18},{1,19},{2,16},{3,17},{4,22},{5,23},{6,20},{7,21},{8,26},{9,... | collective-permute-start | bytes 393224 | tf_op jit(solution)/shard_map/ppermute | solution.py:260
  161.5 2.4 shard_map.118
  164.6 2.9 %collective-permute-start.68 = (bf16[32,2048]{1,0:T(8,128)(2,1)S(1)}, bf16[32,2048]{1,0:T(8,128)(2,1)S(1)}, u32[]{:S(2)}, u32[]{:S(2)}) collective-permute-start(bf16[32,2048]{1,0:T(8,128)(2,1)S(1)} %get-tuple-element.141), channel_id=1, source_target_pairs={{0,18},{1,19},{2,16},{3,17},{4,22},{5,23},{6,20},{7,21},{8,26},{9,... | collective-permute-start | bytes 393224 | tf_op jit(solution)/shard_map/ppermute | solution.py:260
  171.0 2.5 collective-permute-start.71
  183.9 3.9 %collective-permute-done.73.refs_2_ = bf16[32,2048]{1,0:T(8,128)(2,1)S(1)} collective-permute-done((bf16[32,2048]{1,0:T(8,128)(2,1)S(1)}, bf16[32,2048]{1,0:T(8,128)(2,1)S(1)}, u32[]{:S(2)}, u32[]{:S(2)}) %collective-permute-start.73) | collective-permute-done | bytes 131104 | tf_op jit(solution)/shard_map/ppermute | solution.py:260
  187.8 2.6 shard_map.119
  193.9 2.9 %collective-permute-done.77 = bf16[32,2048]{1,0:T(8,128)(2,1)S(1)} collective-permute-done((bf16[32,2048]{1,0:T(8,128)(2,1)S(1)}, bf16[32,2048]{1,0:T(8,128)(2,1)S(1)}, u32[]{:S(2)}, u32[]{:S(2)}) %collective-permute-start.77) | collective-permute-done | bytes 131104 | tf_op jit(solution)/shard_map/ppermute | solution.py:260
  199.6 3.1 %collective-permute-start.81 = (bf16[32,2048]{1,0:T(8,128)(2,1)S(1)}, bf16[32,2048]{1,0:T(8,128)(2,1)S(1)}, u32[]{:S(2)}, u32[]{:S(2)}) collective-permute-start(bf16[32,2048]{1,0:T(8,128)(2,1)S(1)} %fusion.26), channel_id=1, source_target_pairs={{0,12},{1,13},{2,14},{3,15},{4,0},{5,1},{6,2},{7,3},{8,4},{9,5},{1... | collective-permute-start | bytes 393224 | tf_op jit(solution)/shard_map/ppermute | solution.py:260
  202.7 2.5 collective-permute-done.81.refs_0_
  208.7 2.5 collective-permute-done.82.refs_1_
  212.5 2.4 shard_map.120
  223.3 4.1 %collective-permute-start.88 = (bf16[32,2048]{1,0:T(8,128)(2,1)S(1)}, bf16[32,2048]{1,0:T(8,128)(2,1)S(1)}, u32[]{:S(2)}, u32[]{:S(2)}) collective-permute-start(bf16[32,2048]{1,0:T(8,128)(2,1)S(1)} %fusion.33), channel_id=1, source_target_pairs={{0,12},{1,13},{2,14},{3,15},{4,0},{5,1},{6,2},{7,3},{8,4},{9,5},{1... | collective-permute-start | bytes 393224 | tf_op jit(solution)/shard_map/ppermute | solution.py:260
  227.4 2.5 collective-permute-done.88.refs_0_
  233.4 2.4 collective-permute-done.89.refs_1_
  237.5 2.4 shard_map.121
  248.6 4.3 %collective-permute-start.95 = (bf16[32,2048]{1,0:T(8,128)(2,1)S(1)}, bf16[32,2048]{1,0:T(8,128)(2,1)S(1)}, u32[]{:S(2)}, u32[]{:S(2)}) collective-permute-start(bf16[32,2048]{1,0:T(8,128)(2,1)S(1)} %fusion.40), channel_id=1, source_target_pairs={{0,12},{1,13},{2,14},{3,15},{4,0},{5,1},{6,2},{7,3},{8,4},{9,5},{1... | collective-permute-start | bytes 393224 | tf_op jit(solution)/shard_map/ppermute | solution.py:260
  252.9 2.5 collective-permute-done.95.refs_0_
  262.7 2.4 shard_map.122
  (261 shorter events, 178.0 us)
Async XLA Ops:
  0.6 10.0 %collective-permute-start.6 = (bf16[2048,384]{1,0:T(8,128)(2,1)}, bf16[2048,384]{1,0:T(8,128)(2,1)S(1)}, u32[]{:S(2)}, u32[]{:S(2)}) collective-permute-start(bf16[2048,384]{1,0:T(8,128)(2,1)} %bitcast.26), channel_id=1, source_target_pairs={{0,1},{1,0},{2,3},{3,2},{4,5},{5,4},{6,7},{7,6},{8,9},{9,8},{10,11... | collective-permute-start | bytes 4718600 | tf_op jit(solution)/shard_map/ppermute | solution.py:241
  1.2 11.0 %collective-permute-start.7 = (bf16[2048,384]{1,0:T(8,128)(2,1)}, bf16[2048,384]{1,0:T(8,128)(2,1)S(1)}, u32[]{:S(2)}, u32[]{:S(2)}) collective-permute-start(bf16[2048,384]{1,0:T(8,128)(2,1)} %bitcast.28), channel_id=1, source_target_pairs={{0,1},{1,0},{2,3},{3,2},{4,5},{5,4},{6,7},{7,6},{8,9},{9,8},{10,11... | collective-permute-start | bytes 4718600 | tf_op jit(solution)/shard_map/ppermute | solution.py:241
  1.3 11.4 %collective-permute-start.8 = (bf16[384,2048]{1,0:T(8,128)(2,1)}, bf16[384,2048]{1,0:T(8,128)(2,1)}, u32[]{:S(2)}, u32[]{:S(2)}) collective-permute-start(bf16[384,2048]{1,0:T(8,128)(2,1)} %bitcast.30), channel_id=1, source_target_pairs={{0,1},{1,0},{2,3},{3,2},{4,5},{5,4},{6,7},{7,6},{8,9},{9,8},{10,11... | collective-permute-start | bytes 4718600 | tf_op jit(solution)/shard_map/ppermute | solution.py:241
  7.7 9.8 %collective-permute-start = (bf16[32,2048]{1,0:T(8,128)(2,1)S(1)}, bf16[32,2048]{1,0:T(8,128)(2,1)S(1)}, u32[]{:S(2)}, u32[]{:S(2)}) collective-permute-start(bf16[32,2048]{1,0:T(8,128)(2,1)S(1)} %slice.27.refs_0_), channel_id=1, source_target_pairs={{0,18},{1,19},{2,16},{3,17},{4,22},{5,23},{6,20},{7,21},{8,26},{9,... | collective-permute-start | bytes 393224 | tf_op jit(solution)/shard_map/ppermute | solution.py:260
  8.7 8.8 %collective-permute-start.1 = (bf16[32,2048]{1,0:T(8,128)(2,1)S(1)}, bf16[32,2048]{1,0:T(8,128)(2,1)S(1)}, u32[]{:S(2)}, u32[]{:S(2)}) collective-permute-start(bf16[32,2048]{1,0:T(8,128)(2,1)S(1)} %slice.27.refs_0_), channel_id=1, source_target_pairs={{0,2},{1,3},{2,0},{3,1},{4,6},{5,7},{6,4},{7,5},{8,10},{9,11},{10,... | collective-permute-start | bytes 393224 | tf_op jit(solution)/shard_map/ppermute | solution.py:260
  20.8 7.6 %collective-permute-start.10 = (bf16[32,2048]{1,0:T(8,128)(2,1)S(1)}, bf16[32,2048]{1,0:T(8,128)(2,1)S(1)}, u32[]{:S(2)}, u32[]{:S(2)}) collective-permute-start(bf16[32,2048]{1,0:T(8,128)(2,1)S(1)} %get-tuple-element.94), channel_id=1, source_target_pairs={{0,2},{1,3},{2,0},{3,1},{4,6},{5,7},{6,4},{7,5},{8,10},{9,11},{10,... | collective-permute-start | bytes 393224 | tf_op jit(solution)/shard_map/ppermute | solution.py:260
  61.6 8.2 %collective-permute-start.21 = (bf16[32,2048]{1,0:T(8,128)(2,1)S(1)}, bf16[32,2048]{1,0:T(8,128)(2,1)S(1)}, u32[]{:S(2)}, u32[]{:S(2)}) collective-permute-start(bf16[32,2048]{1,0:T(8,128)(2,1)S(1)} %slice_select_fusion.4.refs_0_), channel_id=1, source_target_pairs={{0,2},{1,3},{2,0},{3,1},{4,6},{5,7},{6,4},{7,5},{8,10},{9,11},{10,... | collective-permute-start | bytes 393224 | tf_op jit(solution)/shard_map/ppermute | solution.py:260
  62.7 7.1 %collective-permute-start.22 = (bf16[32,2048]{1,0:T(8,128)(2,1)S(1)}, bf16[32,2048]{1,0:T(8,128)(2,1)S(1)}, u32[]{:S(2)}, u32[]{:S(2)}) collective-permute-start(bf16[32,2048]{1,0:T(8,128)(2,1)S(1)} %slice_select_fusion.4.refs_0_), channel_id=1, source_target_pairs={{0,16},{1,17},{2,18},{3,19},{4,20},{5,21},{6,22},{7,23},{8,24},{9,... | collective-permute-start | bytes 393224 | tf_op jit(solution)/shard_map/ppermute | solution.py:260
  90.6 8.5 %collective-permute-start.51 = (bf16[32,2048]{1,0:T(8,128)(2,1)S(1)}, bf16[32,2048]{1,0:T(8,128)(2,1)S(1)}, u32[]{:S(2)}, u32[]{:S(2)}) collective-permute-start(bf16[32,2048]{1,0:T(8,128)(2,1)S(1)} %slice.31.refs_0_), channel_id=1, source_target_pairs={{0,18},{1,19},{2,16},{3,17},{4,22},{5,23},{6,20},{7,21},{8,26},{9,... | collective-permute-start | bytes 393224 | tf_op jit(solution)/shard_map/ppermute | solution.py:260
  92.5 11.5 %collective-permute-start.52 = (bf16[32,2048]{1,0:T(8,128)(2,1)S(1)}, bf16[32,2048]{1,0:T(8,128)(2,1)S(1)}, u32[]{:S(2)}, u32[]{:S(2)}) collective-permute-start(bf16[32,2048]{1,0:T(8,128)(2,1)S(1)} %slice.31.refs_0_), channel_id=1, source_target_pairs={{0,2},{1,3},{2,0},{3,1},{4,6},{5,7},{6,4},{7,5},{8,10},{9,11},{10,... | collective-permute-start | bytes 393224 | tf_op jit(solution)/shard_map/ppermute | solution.py:260
  93.1 10.9 %collective-permute-start.53 = (bf16[32,2048]{1,0:T(8,128)(2,1)S(1)}, bf16[32,2048]{1,0:T(8,128)(2,1)S(1)}, u32[]{:S(2)}, u32[]{:S(2)}) collective-permute-start(bf16[32,2048]{1,0:T(8,128)(2,1)S(1)} %slice.31.refs_0_), channel_id=1, source_target_pairs={{0,16},{1,17},{2,18},{3,19},{4,20},{5,21},{6,22},{7,23},{8,24},{9,... | collective-permute-start | bytes 393224 | tf_op jit(solution)/shard_map/ppermute | solution.py:260
  96.7 12.1 %collective-permute-start.32 = (bf16[32,2048]{1,0:T(8,128)(2,1)S(1)}, bf16[32,2048]{1,0:T(8,128)(2,1)S(1)}, u32[]{:S(2)}, u32[]{:S(2)}) collective-permute-start(bf16[32,2048]{1,0:T(8,128)(2,1)S(1)} %get-tuple-element.107), channel_id=1, source_target_pairs={{0,16},{1,17},{2,18},{3,19},{4,20},{5,21},{6,22},{7,23},{8,24},{9,... | collective-permute-start | bytes 393224 | tf_op jit(solution)/shard_map/ppermute | solution.py:260
  97.8 12.2 %collective-permute-start.31 = (bf16[32,2048]{1,0:T(8,128)(2,1)S(1)}, bf16[32,2048]{1,0:T(8,128)(2,1)S(1)}, u32[]{:S(2)}, u32[]{:S(2)}) collective-permute-start(bf16[32,2048]{1,0:T(8,128)(2,1)S(1)} %get-tuple-element.106), channel_id=1, source_target_pairs={{0,2},{1,3},{2,0},{3,1},{4,6},{5,7},{6,4},{7,5},{8,10},{9,11},{10,... | collective-permute-start | bytes 393224 | tf_op jit(solution)/shard_map/ppermute | solution.py:260
  99.1 11.0 %collective-permute-start.30 = (bf16[32,2048]{1,0:T(8,128)(2,1)S(1)}, bf16[32,2048]{1,0:T(8,128)(2,1)S(1)}, u32[]{:S(2)}, u32[]{:S(2)}) collective-permute-start(bf16[32,2048]{1,0:T(8,128)(2,1)S(1)} %get-tuple-element.105), channel_id=1, source_target_pairs={{0,18},{1,19},{2,16},{3,17},{4,22},{5,23},{6,20},{7,21},{8,26},{9,... | collective-permute-start | bytes 393224 | tf_op jit(solution)/shard_map/ppermute | solution.py:260
  108.8 7.4 %collective-permute-start.54 = (bf16[32,2048]{1,0:T(8,128)(2,1)S(1)}, bf16[32,2048]{1,0:T(8,128)(2,1)S(1)}, u32[]{:S(2)}, u32[]{:S(2)}) collective-permute-start(bf16[32,2048]{1,0:T(8,128)(2,1)S(1)} %get-tuple-element.127), channel_id=1, source_target_pairs={{0,18},{1,19},{2,16},{3,17},{4,22},{5,23},{6,20},{7,21},{8,26},{9,... | collective-permute-start | bytes 393224 | tf_op jit(solution)/shard_map/ppermute | solution.py:260
  121.7 7.7 %collective-permute-start.58 = (bf16[32,2048]{1,0:T(8,128)(2,1)S(1)}, bf16[32,2048]{1,0:T(8,128)(2,1)S(1)}, u32[]{:S(2)}, u32[]{:S(2)}) collective-permute-start(bf16[32,2048]{1,0:T(8,128)(2,1)S(1)} %slice_select_fusion.refs_0_), channel_id=1, source_target_pairs={{0,18},{1,19},{2,16},{3,17},{4,22},{5,23},{6,20},{7,21},{8,26},{9,... | collective-permute-start | bytes 393224 | tf_op jit(solution)/shard_map/ppermute | solution.py:260
  123.2 7.8 %collective-permute-start.59 = (bf16[32,2048]{1,0:T(8,128)(2,1)S(1)}, bf16[32,2048]{1,0:T(8,128)(2,1)S(1)}, u32[]{:S(2)}, u32[]{:S(2)}) collective-permute-start(bf16[32,2048]{1,0:T(8,128)(2,1)S(1)} %slice_select_fusion.refs_0_), channel_id=1, source_target_pairs={{0,2},{1,3},{2,0},{3,1},{4,6},{5,7},{6,4},{7,5},{8,10},{9,11},{10,... | collective-permute-start | bytes 393224 | tf_op jit(solution)/shard_map/ppermute | solution.py:260
  127.4 8.0 %collective-permute-start.39 = (bf16[32,2048]{1,0:T(8,128)(2,1)S(1)}, bf16[32,2048]{1,0:T(8,128)(2,1)S(1)}, u32[]{:S(2)}, u32[]{:S(2)}) collective-permute-start(bf16[32,2048]{1,0:T(8,128)(2,1)S(1)} %get-tuple-element.111), channel_id=1, source_target_pairs={{0,16},{1,17},{2,18},{3,19},{4,20},{5,21},{6,22},{7,23},{8,24},{9,... | collective-permute-start | bytes 393224 | tf_op jit(solution)/shard_map/ppermute | solution.py:260
  128.3 9.4 %collective-permute-start.38 = (bf16[32,2048]{1,0:T(8,128)(2,1)S(1)}, bf16[32,2048]{1,0:T(8,128)(2,1)S(1)}, u32[]{:S(2)}, u32[]{:S(2)}) collective-permute-start(bf16[32,2048]{1,0:T(8,128)(2,1)S(1)} %get-tuple-element.110), channel_id=1, source_target_pairs={{0,2},{1,3},{2,0},{3,1},{4,6},{5,7},{6,4},{7,5},{8,10},{9,11},{10,... | collective-permute-start | bytes 393224 | tf_op jit(solution)/shard_map/ppermute | solution.py:260
  129.5 8.2 %collective-permute-start.37 = (bf16[32,2048]{1,0:T(8,128)(2,1)S(1)}, bf16[32,2048]{1,0:T(8,128)(2,1)S(1)}, u32[]{:S(2)}, u32[]{:S(2)}) collective-permute-start(bf16[32,2048]{1,0:T(8,128)(2,1)S(1)} %get-tuple-element.109), channel_id=1, source_target_pairs={{0,18},{1,19},{2,16},{3,17},{4,22},{5,23},{6,20},{7,21},{8,26},{9,... | collective-permute-start | bytes 393224 | tf_op jit(solution)/shard_map/ppermute | solution.py:260
  137.8 8.0 %collective-permute-start.40 = (bf16[32,2048]{1,0:T(8,128)(2,1)S(1)}, bf16[32,2048]{1,0:T(8,128)(2,1)S(1)}, u32[]{:S(2)}, u32[]{:S(2)}) collective-permute-start(bf16[32,2048]{1,0:T(8,128)(2,1)S(1)} %add_convert_fusion.2), channel_id=1, source_target_pairs={{0,4},{1,5},{2,6},{3,7},{4,8},{5,9},{6,10},{7,11},{8,12},{9,13},{1... | collective-permute-start | bytes 393224 | tf_op jit(solution)/shard_map/ppermute | solution.py:260
  147.1 8.7 %collective-permute-start.42 = (bf16[32,2048]{1,0:T(8,128)(2,1)S(1)}, bf16[32,2048]{1,0:T(8,128)(2,1)S(1)}, u32[]{:S(2)}, u32[]{:S(2)}) collective-permute-start(bf16[32,2048]{1,0:T(8,128)(2,1)S(1)} %collective-permute-done.40.refs_0_), channel_id=1, source_target_pairs={{0,2},{1,3},{2,0},{3,1},{4,6},{5,7},{6,4},{7,5},{8,10},{9,11},{10,... | collective-permute-start | bytes 393224 | tf_op jit(solution)/shard_map/ppermute | solution.py:260
  148.5 7.2 %collective-permute-start.43 = (bf16[32,2048]{1,0:T(8,128)(2,1)S(1)}, bf16[32,2048]{1,0:T(8,128)(2,1)S(1)}, u32[]{:S(2)}, u32[]{:S(2)}) collective-permute-start(bf16[32,2048]{1,0:T(8,128)(2,1)S(1)} %collective-permute-done.40.refs_0_), channel_id=1, source_target_pairs={{0,16},{1,17},{2,18},{3,19},{4,20},{5,21},{6,22},{7,23},{8,24},{9,... | collective-permute-start | bytes 393224 | tf_op jit(solution)/shard_map/ppermute | solution.py:260
  149.2 9.2 %collective-permute-start.65 = (bf16[32,2048]{1,0:T(8,128)(2,1)S(1)}, bf16[32,2048]{1,0:T(8,128)(2,1)S(1)}, u32[]{:S(2)}, u32[]{:S(2)}) collective-permute-start(bf16[32,2048]{1,0:T(8,128)(2,1)S(1)} %slice_select_fusion.1.refs_0_), channel_id=1, source_target_pairs={{0,18},{1,19},{2,16},{3,17},{4,22},{5,23},{6,20},{7,21},{8,26},{9,... | collective-permute-start | bytes 393224 | tf_op jit(solution)/shard_map/ppermute | solution.py:260
  150.7 10.9 %collective-permute-start.66 = (bf16[32,2048]{1,0:T(8,128)(2,1)S(1)}, bf16[32,2048]{1,0:T(8,128)(2,1)S(1)}, u32[]{:S(2)}, u32[]{:S(2)}) collective-permute-start(bf16[32,2048]{1,0:T(8,128)(2,1)S(1)} %slice_select_fusion.1.refs_0_), channel_id=1, source_target_pairs={{0,2},{1,3},{2,0},{3,1},{4,6},{5,7},{6,4},{7,5},{8,10},{9,11},{10,... | collective-permute-start | bytes 393224 | tf_op jit(solution)/shard_map/ppermute | solution.py:260
  152.6 9.0 %collective-permute-start.67 = (bf16[32,2048]{1,0:T(8,128)(2,1)S(1)}, bf16[32,2048]{1,0:T(8,128)(2,1)S(1)}, u32[]{:S(2)}, u32[]{:S(2)}) collective-permute-start(bf16[32,2048]{1,0:T(8,128)(2,1)S(1)} %slice_select_fusion.1.refs_0_), channel_id=1, source_target_pairs={{0,16},{1,17},{2,18},{3,19},{4,20},{5,21},{6,22},{7,23},{8,24},{9,... | collective-permute-start | bytes 393224 | tf_op jit(solution)/shard_map/ppermute | solution.py:260
  158.0 9.4 %collective-permute-start.45 = (bf16[32,2048]{1,0:T(8,128)(2,1)S(1)}, bf16[32,2048]{1,0:T(8,128)(2,1)S(1)}, u32[]{:S(2)}, u32[]{:S(2)}) collective-permute-start(bf16[32,2048]{1,0:T(8,128)(2,1)S(1)} %get-tuple-element.114), channel_id=1, source_target_pairs={{0,2},{1,3},{2,0},{3,1},{4,6},{5,7},{6,4},{7,5},{8,10},{9,11},{10,... | collective-permute-start | bytes 393224 | tf_op jit(solution)/shard_map/ppermute | solution.py:260
  158.5 9.0 %collective-permute-start.44 = (bf16[32,2048]{1,0:T(8,128)(2,1)S(1)}, bf16[32,2048]{1,0:T(8,128)(2,1)S(1)}, u32[]{:S(2)}, u32[]{:S(2)}) collective-permute-start(bf16[32,2048]{1,0:T(8,128)(2,1)S(1)} %get-tuple-element.113), channel_id=1, source_target_pairs={{0,18},{1,19},{2,16},{3,17},{4,22},{5,23},{6,20},{7,21},{8,26},{9,... | collective-permute-start | bytes 393224 | tf_op jit(solution)/shard_map/ppermute | solution.py:260
  179.0 8.8 %collective-permute-start.73 = (bf16[32,2048]{1,0:T(8,128)(2,1)S(1)}, bf16[32,2048]{1,0:T(8,128)(2,1)S(1)}, u32[]{:S(2)}, u32[]{:S(2)}) collective-permute-start(bf16[32,2048]{1,0:T(8,128)(2,1)S(1)} %slice_select_fusion.2.refs_0_), channel_id=1, source_target_pairs={{0,2},{1,3},{2,0},{3,1},{4,6},{5,7},{6,4},{7,5},{8,10},{9,11},{10,... | collective-permute-start | bytes 393224 | tf_op jit(solution)/shard_map/ppermute | solution.py:260
  180.3 7.4 %collective-permute-start.74 = (bf16[32,2048]{1,0:T(8,128)(2,1)S(1)}, bf16[32,2048]{1,0:T(8,128)(2,1)S(1)}, u32[]{:S(2)}, u32[]{:S(2)}) collective-permute-start(bf16[32,2048]{1,0:T(8,128)(2,1)S(1)} %slice_select_fusion.2.refs_0_), channel_id=1, source_target_pairs={{0,16},{1,17},{2,18},{3,19},{4,20},{5,21},{6,22},{7,23},{8,24},{9,... | collective-permute-start | bytes 393224 | tf_op jit(solution)/shard_map/ppermute | solution.py:260
  191.0 8.1 %collective-permute-start.76 = (bf16[32,2048]{1,0:T(8,128)(2,1)S(1)}, bf16[32,2048]{1,0:T(8,128)(2,1)S(1)}, u32[]{:S(2)}, u32[]{:S(2)}) collective-permute-start(bf16[32,2048]{1,0:T(8,128)(2,1)S(1)} %get-tuple-element.148), channel_id=1, source_target_pairs={{0,2},{1,3},{2,0},{3,1},{4,6},{5,7},{6,4},{7,5},{8,10},{9,11},{10,... | collective-permute-start | bytes 393224 | tf_op jit(solution)/shard_map/ppermute | solution.py:260
  272.6 7.1 %collective-permute-start.100 = (bf16[32,2048]{1,0:T(8,128)(2,1)S(1)}, bf16[32,2048]{1,0:T(8,128)(2,1)S(1)}, u32[]{:S(2)}, u32[]{:S(2)}) collective-permute-start(bf16[32,2048]{1,0:T(8,128)(2,1)S(1)} %get-tuple-element.164), channel_id=1, source_target_pairs={{0,2},{1,3},{2,0},{3,1},{4,6},{5,7},{6,4},{7,5},{8,10},{9,11},{10,... | collective-permute-start | bytes 393224 | tf_op jit(solution)/shard_map/ppermute | solution.py:260
  (79 other events, 497.2 us)

commit v2 on v1

--- a/solution.py
+++ b/solution.py
@@ -241,23 +241,19 @@
     return lax.ppermute(value, "expert", [(e, e ^ 1) for e in range(count)])
 
 
-def device_number(dp, pipe, expert):
-    return (dp * lax.axis_size("pipe") + pipe) * lax.axis_size("expert") + expert
-
-
-def shifted(value, dp_step, chip_step, pipe_step):
-    dps, pipes, experts = (lax.axis_size(name) for name in ("dp", "pipe", "expert"))
+def shifted(value, dp_step, chip_step):
+    dps, experts = (lax.axis_size(name) for name in ("dp", "expert"))
     pairs = []
     for dp in range(dps):
-        for pipe in range(pipes):
-            for expert in range(experts):
-                target = device_number(
-                    (dp + dp_step) % dps,
-                    (pipe + pipe_step) % pipes,
-                    (expert + 2 * chip_step) % experts,
-                )
-                pairs.append((device_number(dp, pipe, expert), target))
-    return lax.ppermute(value, ("dp", "pipe", "expert"), pairs)
+        for expert in range(experts):
+            target = (dp + dp_step) % dps * experts + (expert + 2 * chip_step) % experts
+            pairs.append((dp * experts + expert, target))
+    return lax.ppermute(value, ("dp", "expert"), pairs)
+
+
+def hopped(value, step):
+    stages = lax.axis_size("pipe")
+    return lax.ppermute(value, "pipe", [(s, (s + step) % stages) for s in range(stages)])
 
 
 def chip_steps():
@@ -267,17 +263,22 @@
 
 
 def spread(rows):
-    return [rows] + [shifted(rows, d, c, 0) for d, c in chip_steps()]
+    return [rows] + [shifted(rows, d, c) for d, c in chip_steps()]
+
+
+def returned(blocks, which):
+    dps, chips = lax.axis_size("dp"), lax.axis_size("expert") // 2
+    dp, chip = chip_steps()[which - 1]
+    return shifted(blocks[which], -dp % dps, -chip % chips)
 
 
 def collect(blocks):
-    dps, chips = lax.axis_size("dp"), lax.axis_size("expert") // 2
-    back = [shifted(block, -d % dps, -c % chips, 0) for block, (d, c) in zip(blocks[1:], chip_steps())]
-    return [blocks[0]] + back
+    return [blocks[0]] + [returned(blocks, which) for which in range(1, len(blocks))]
 
 
 VMEM = pl.BlockSpec(memory_space=pltpu.VMEM)
 CHUNK = 256
+LANES = 128
 HALVES = 2
 
 
@@ -313,13 +314,41 @@
 def loaded(own, pair):
     gate, _, down = own
     joint, down = pltpu.VMEM((gate.shape[0], 2 * gate.shape[1]), gate.dtype), pltpu.VMEM(down.shape, down.dtype)
-    specs = [pl.BlockSpec(memory_space=pltpu.HBM)] * 6
+    specs = [pl.BlockSpec(memory_space=pltpu.HBM)] * 3 + [pl.BlockSpec(memory_space=pl.ANY)] * 3
     scratch = [pltpu.SemaphoreType.DMA((6,))]
     return in_vmem(load_kernel, [joint, joint, down, down], scratch, 0, *own, *pair, specs=specs)
 
 
 def stage_kernel(out_ref):
     out_ref[...] = jnp.full(out_ref.shape, lax.axis_index("pipe"), jnp.int32)
+
+
+def first_rows_kernel(token_ref, id_ref, gate_ref, out_ref, copied, sem):
+    rows, width = copied.shape
+    copy = pltpu.make_async_copy(token_ref.at[pl.ds(0, rows), :], copied, sem)
+    copy.start()
+    owners = lax.axis_size("dp") * lax.axis_size("expert")
+    column = lax.broadcasted_iota(jnp.int32, (rows, out_ref.shape[1] - width), 1)
+    table = jnp.zeros(column.shape, jnp.float32)
+    for micro in range(MICRO):
+        window = slice(micro * rows, (micro + 1) * rows)
+        gates = gate_ref[window, :].astype(jnp.float32)
+        for slot in range(id_ref.shape[1]):
+            place = micro * owners + id_ref[window, slot:slot + 1]
+            table = table + jnp.where(column == place, gates[:, slot:slot + 1], 0.0)
+    out_ref[:, width:] = table.astype(jnp.bfloat16)
+    copy.wait()
+    out_ref[:, :width] = copied[...]
+
+
+def first_rows(tokens, ids, gates):
+    rows, width = tokens.shape[0] // MICRO, tokens.shape[1]
+    owners = lax.axis_size("dp") * lax.axis_size("expert")
+    extra = -(-MICRO * owners // LANES) * LANES
+    outs = [jax.ShapeDtypeStruct((rows, width + extra), tokens.dtype)]
+    scratch = [pltpu.VMEM((rows, width), tokens.dtype), pltpu.SemaphoreType.DMA]
+    specs = [pl.BlockSpec(memory_space=pl.ANY), VMEM, VMEM]
+    return in_vmem(first_rows_kernel, outs, scratch, 0, tokens, ids, gates, specs=specs)[0]
 
 
 def turn_kernel(in_ref, out_ref):
@@ -356,20 +385,20 @@
     row_refs, table_refs, refs = refs[:blocks], refs[blocks:2 * blocks], refs[2 * blocks:]
     gain_ref, *weight_refs = refs[:5]
     rate_ref, flat_ref, own_ref, *part_refs, pre, hidden = refs[5:]
-    rows, width = row_refs[0].shape
+    rows, width = own_ref.shape
     ff = weight_refs[2].shape[0]
     gain = gain_ref[...]
     for k, row_ref in enumerate(row_refs):
-        x = row_ref[...].astype(jnp.float32)
+        x = row_ref[:, :width].astype(jnp.float32)
         flat_ref[k * rows:(k + 1) * rows, :] = (x * inverse_rms(x) * gain).astype(jnp.bfloat16)
     micro = tick - lax.axis_index("pipe")
     is_valid = (micro >= 0) & (micro < MICRO)
-    first = pl.multiple_of(jnp.clip(micro, 0, MICRO - 1) * rows, rows)
-    routed = jnp.concatenate([ref[pl.ds(first, rows), :] for ref in table_refs], axis=0).astype(jnp.float32)
-    number = lax.broadcasted_iota(jnp.int32, routed.shape, 1)
-    me = owner_number()
+    routed = jnp.concatenate([ref[:, width:] for ref in table_refs], axis=0).astype(jnp.float32)
+    column = lax.broadcasted_iota(jnp.int32, routed.shape, 1)
+    me, owners = owner_number(), lax.axis_size("dp") * lax.axis_size("expert")
     for e, owner in enumerate((me, me ^ 1)):
-        weight = jnp.sum(jnp.where((number == owner) & is_valid, routed, 0.0), axis=1, keepdims=True)
+        is_routed = (column == micro * owners + owner) & is_valid
+        weight = jnp.sum(jnp.where(is_routed, routed, 0.0), axis=1, keepdims=True)
         for start in range(0, 2 * ff, CHUNK):
             pre[:, start:start + CHUNK] = jnp.dot(
                 flat_ref[...], weight_refs[e][:, start:start + CHUNK], preferred_element_type=jnp.float32
@@ -442,7 +471,7 @@
 
 
 def forward_experts(tick, row_blocks, tables, gain, weights):
-    blocks, (rows, width) = len(row_blocks), row_blocks[0].shape
+    blocks, rows, width = len(row_blocks), row_blocks[0].shape[0], gain.shape[1]
     total, ff = blocks * rows, weights[2].shape[0]
     outs = [
         jax.ShapeDtypeStruct((total, 4 * ff), jnp.float32),
@@ -487,7 +516,6 @@
 def dense_body(tokens, cotangent, owner_ids, gate_weights, norm_gain, w_gate, w_up, w_down):
     f32, bf16 = jnp.float32, jnp.bfloat16
     stages = lax.axis_size("pipe")
-    owners = lax.axis_size("dp") * lax.axis_size("expert")
     tok_rows, width = tokens.shape
     rows = tok_rows // MICRO
     gain = norm_gain[0][None, :]
@@ -496,15 +524,10 @@
 
     own = [pltpu.with_memory_space_constraint(w[0, 0], pltpu.HBM) for w in (w_gate, w_up, w_down)]
     theirs = [swap_cores(w) for w in own]
-    theirs = [pltpu.with_memory_space_constraint(w, pltpu.HBM) for w in theirs]
     forward_weights = loaded(own, theirs)
     backward_weights = []
     for number, part in enumerate(forward_weights):
         backward_weights.append(turned(part))
-
-    onehot = owner_ids[0][:, :, None] == jnp.arange(owners, dtype=jnp.int32)
-    table = jnp.sum(jnp.where(onehot, gate_weights[0].astype(f32)[:, :, None], 0.0), axis=1).astype(bf16)
-    tables = spread(table)
 
     def choose(values):
         found = values[0]
@@ -520,20 +543,22 @@
     for tick in range(last + 1):
         if tick < ticks:
             if tick == 0:
-                here = tokens[:rows]
+                here = first_rows(tokens, owner_ids[0], gate_weights[0])
             elif tick < MICRO:
                 here = jnp.where(stage == 0, tokens[tick * rows:(tick + 1) * rows], behind)
             else:
                 here = behind
             here_blocks = spread(here)
+            if tick == 0:
+                tables = here_blocks
             rate, normed, parts = forward_experts(tick, here_blocks, tables, gain, forward_weights)
             rates.append(rate)
             normeds.append(normed)
-            ins.append(here)
+            ins.append(here[:, :width])
             if tick + 1 < ticks:
                 parts = collect(parts)
                 outs.append(lax.optimization_barrier(sum(p.astype(f32) for p in parts).astype(bf16)))
-                behind = shifted(outs[-1], 0, 0, 1)
+                behind = hopped(outs[-1], 1)
         number = tick - (stages - 1)
         if number >= 0:
             first = number - (stages - 1)
@@ -561,10 +586,12 @@
                 grad_x = lax.optimization_barrier(grad_x)
             grads.append(grad_x)
             if tick < last:
-                ahead = shifted(grad_x, 0, 0, -1)
+                ahead = hopped(grad_x, -1)
             if tick + 1 == ticks:
-                parts = collect(lax.optimization_barrier((parts, grad_x))[0])
-                outs.append(sum(p.astype(f32) for p in parts).astype(bf16))
+                waiting, kept = parts, parts[:1]
+            while tick + 1 >= ticks and len(kept) < len(waiting) and (tick - ticks + 2 >= len(kept) or tick + 1 == last):
+                kept.append(returned(lax.optimization_barrier((waiting, grad_x))[0], len(kept)))
+    outs.append(sum(part.astype(f32) for part in kept).astype(bf16))
     gain_grad = summed_over_owners(gain_sum) / gain
     segment_out = jnp.concatenate([choose([outs[m + s] for s in range(stages)]) for m in range(MICRO)])
     segment_grad = jnp.concatenate(

time: 281 us -> 282 us (level)
  waiting for transfers between devices: 102 us -> 97.1 us
  starting transfers between devices: 129 us -> 133 us
    ppermute x102 -> x99, waiting for transfers between devices: 102 us -> 97 us  [the longest x87 68.5 us: shifted(): return lax.ppermute(value, ('dp', 'expert'), pairs)]
    ppermute x102 -> x99, starting transfers between devices: 128 us -> 131 us  [the longest x87 103 us: shifted(): return lax.ppermute(value, ('dp', 'expert'), pairs)]
    unnamed x10 -> x14, local copies, waits for them, and re-layouts: 0.53 us -> 4.03 us
    pallas_call x20 -> x21, Pallas kernels: 39.5 us -> 39.8 us  [in_vmem(): pl.pallas_call(kernel, out_shape=outs, in_specs=specs or [VMEM] * len(ope...]
  transfers between devices with their start and end apart: 106 -> 103, of which waited for: 60 -> 57; matrix products, arithmetic and copies ran while one was open for 2% -> 2% of each run, Pallas kernels for 9% -> 9%
where the time goes in v2:
time: 282 us; the launch traced here: 281 us
  starting transfers between devices  133 us (47%)
  waiting for transfers between devices  97.1 us (34%)
  Pallas kernels  39.8 us (14%)
  other arithmetic  6.67 us (2%)
  local copies, waits for them, and re-layouts  4.04 us (1%)
    ppermute x87, starting transfers between devices, shifted(): return lax.ppermute(value, ('dp', 'expert'), pairs)  103 us
    ppermute x87, waiting for transfers between devices, shifted(): return lax.ppermute(value, ('dp', 'expert'), pairs)  68.5 us
    pallas_call x21, Pallas kernels, in_vmem(): pl.pallas_call(kernel, out_shape=outs, in_specs=specs or [VMEM] * len(ope...  39.8 us
    ppermute x12, waiting for transfers between devices, hopped(): lax.ppermute(value, 'pipe', [(s, (s + step) % stages) for s in range(stag...  28.4 us
    ppermute x12, starting transfers between devices, hopped(): lax.ppermute(value, 'pipe', [(s, (s + step) % stages) for s in range(stag...  28.4 us
  transfers between devices with their start and end apart: 103, of which 57 were waited for; matrix products, arithmetic and copies ran while one was open for 2% of the time, Pallas kernels for 9%

profile of v2, /device:TPU:0, one launch (start us, length us, event | category | flops | bytes accessed | tf_op | source)
XLA Modules:
  0.0 281.3 jit_solution(12991923296764657777)
XLA Ops:
  4.7 3.6 %collective-permute-start = (bf16[32,2176]{1,0:T(8,128)(2,1)S(1)}, bf16[32,2176]{1,0:T(8,128)(2,1)S(1)}, u32[]{:S(2)}, u32[]{:S(2)}) collective-permute-start(bf16[32,2176]{1,0:T(8,128)(2,1)S(1)} %shard_map.104.refs_0_.refs_4_), channel_id=1, source_target_pairs={{0,18},{1,19},{2,16},{3,17},{16,2},{17,3},{18,0},{19,1},{4,22},{5,... | collective-permute-start | bytes 417800 | tf_op jit(solution)/shard_map/ppermute | solution.py:251
  10.4 3.8 %shard_map.105 = (bf16[2048,768]{1,0:T(8,128)(2,1)S(1)}, bf16[2048,768]{1,0:T(8,128)(2,1)S(1)}, bf16[384,2048]{1,0:T(8,128)(2,1)S(1)}, bf16[384,2048]{1,0:T(8,128)(2,1)S(1)}) custom-call(bf16[2048,384]{1,0:T(8,128)(2,1)} %bitcast.27, bf16[2048,384]{1,0:T(8,128)(2,1)} %bitcast.29, bf16[384,2048]{1,0:T(8,128)(2,1)} %bitcast.31, bf16[2048,384]{1,0:T(8,128)(2,1)} %copy-done.3, ...), custom_call_target="tpu_custom_call" | custom-call | bytes 18874368 | tf_op jit(solution)/shard_map/pallas_call | solution.py:287
  23.5 4.0 %collective-permute-done.7 = bf16[32,2048]{1,0:T(8,128)(2,1)S(1)} collective-permute-done((bf16[32,2048]{1,0:T(8,128)(2,1)S(1)}, bf16[32,2048]{1,0:T(8,128)(2,1)S(1)}, u32[]{:S(2)}, u32[]{:S(2)}) %collective-permute-start.7) | collective-permute-done | bytes 131104 | tf_op jit(solution)/shard_map/ppermute | solution.py:251
  29.3 5.1 %collective-permute-done.9 = bf16[32,2048]{1,0:T(8,128)(2,1)S(1)} collective-permute-done((bf16[32,2048]{1,0:T(8,128)(2,1)S(1)}, bf16[32,2048]{1,0:T(8,128)(2,1)S(1)}, u32[]{:S(2)}, u32[]{:S(2)}) %collective-permute-start.9) | collective-permute-done | bytes 131104 | tf_op jit(solution)/shard_map/ppermute | solution.py:256
  37.9 2.5 collective-permute-done.10.refs_1_
  52.0 6.8 %collective-permute-done.16 = bf16[32,2048]{1,0:T(8,128)(2,1)S(1)} collective-permute-done((bf16[32,2048]{1,0:T(8,128)(2,1)S(1)}, bf16[32,2048]{1,0:T(8,128)(2,1)S(1)}, u32[]{:S(2)}, u32[]{:S(2)}) %collective-permute-start.16) | collective-permute-done | bytes 131104 | tf_op jit(solution)/shard_map/ppermute | solution.py:256
  62.3 3.1 %collective-permute-done.17.refs_1_ = bf16[32,2048]{1,0:T(8,128)(2,1)S(1)} collective-permute-done((bf16[32,2048]{1,0:T(8,128)(2,1)S(1)}, bf16[32,2048]{1,0:T(8,128)(2,1)S(1)}, u32[]{:S(2)}, u32[]{:S(2)}) %collective-permute-start.17) | collective-permute-done | bytes 131104 | tf_op jit(solution)/shard_map/ppermute | solution.py:251
  65.4 2.4 collective-permute-done.18.refs_2_
  78.3 6.8 %collective-permute-done.23 = bf16[32,2048]{1,0:T(8,128)(2,1)S(1)} collective-permute-done((bf16[32,2048]{1,0:T(8,128)(2,1)S(1)}, bf16[32,2048]{1,0:T(8,128)(2,1)S(1)}, u32[]{:S(2)}, u32[]{:S(2)}) %collective-permute-start.23) | collective-permute-done | bytes 131104 | tf_op jit(solution)/shard_map/ppermute | solution.py:256
  102.2 2.4 shard_map.117
  108.5 2.4 collective-permute-done.53
  129.0 2.4 shard_map.118
  135.9 2.5 collective-permute-start.37
  138.4 2.6 collective-permute-done.58
  157.0 2.4 shard_map.119
  163.0 3.9 %collective-permute-start.44 = (bf16[32,2048]{1,0:T(8,128)(2,1)S(1)}, bf16[32,2048]{1,0:T(8,128)(2,1)S(1)}, u32[]{:S(2)}, u32[]{:S(2)}) collective-permute-start(bf16[32,2048]{1,0:T(8,128)(2,1)S(1)} %add_convert_fusion.1), channel_id=1, source_target_pairs={{0,4},{4,8},{8,12},{12,0},{1,5},{5,9},{9,13},{13,1},{2,6},{6,10},{... | collective-permute-start | bytes 393224 | tf_op jit(solution)/shard_map/ppermute | solution.py:256
  168.0 5.7 %collective-permute-start.68 = (bf16[32,2048]{1,0:T(8,128)(2,1)S(1)}, bf16[32,2048]{1,0:T(8,128)(2,1)S(1)}, u32[]{:S(2)}, u32[]{:S(2)}) collective-permute-start(bf16[32,2048]{1,0:T(8,128)(2,1)S(1)} %fusion.19), channel_id=1, source_target_pairs={{0,12},{4,0},{8,4},{12,8},{1,13},{5,1},{9,5},{13,9},{2,14},{6,2},{... | collective-permute-start | bytes 393224 | tf_op jit(solution)/shard_map/ppermute | solution.py:256
  186.8 2.6 shard_map.120
  193.0 2.3 collective-permute-done.74
  195.2 3.2 %collective-permute-done.73 = bf16[32,2048]{1,0:T(8,128)(2,1)S(1)} collective-permute-done((bf16[32,2048]{1,0:T(8,128)(2,1)S(1)}, bf16[32,2048]{1,0:T(8,128)(2,1)S(1)}, u32[]{:S(2)}, u32[]{:S(2)}) %collective-permute-start.73) | collective-permute-done | bytes 131104 | tf_op jit(solution)/shard_map/ppermute | solution.py:251
  198.9 4.1 %collective-permute-start.76 = (bf16[32,2048]{1,0:T(8,128)(2,1)S(1)}, bf16[32,2048]{1,0:T(8,128)(2,1)S(1)}, u32[]{:S(2)}, u32[]{:S(2)}) collective-permute-start(bf16[32,2048]{1,0:T(8,128)(2,1)S(1)} %fusion.26), channel_id=1, source_target_pairs={{0,12},{4,0},{8,4},{12,8},{1,13},{5,1},{9,5},{13,9},{2,14},{6,2},{... | collective-permute-start | bytes 393224 | tf_op jit(solution)/shard_map/ppermute | solution.py:256
  203.0 2.5 collective-permute-done.76.refs_0_
  209.0 2.5 collective-permute-done.77.refs_1_
  212.8 2.4 shard_map.121
  223.6 4.3 %collective-permute-start.84 = (bf16[32,2048]{1,0:T(8,128)(2,1)S(1)}, bf16[32,2048]{1,0:T(8,128)(2,1)S(1)}, u32[]{:S(2)}, u32[]{:S(2)}) collective-permute-start(bf16[32,2048]{1,0:T(8,128)(2,1)S(1)} %fusion.33), channel_id=1, source_target_pairs={{0,12},{4,0},{8,4},{12,8},{1,13},{5,1},{9,5},{13,9},{2,14},{6,2},{... | collective-permute-start | bytes 393224 | tf_op jit(solution)/shard_map/ppermute | solution.py:256
  227.9 2.5 collective-permute-done.84.refs_0_
  233.9 2.5 collective-permute-done.85.refs_1_
  238.1 2.4 shard_map.122
  248.9 4.3 %collective-permute-start.92 = (bf16[32,2048]{1,0:T(8,128)(2,1)S(1)}, bf16[32,2048]{1,0:T(8,128)(2,1)S(1)}, u32[]{:S(2)}, u32[]{:S(2)}) collective-permute-start(bf16[32,2048]{1,0:T(8,128)(2,1)S(1)} %fusion.40), channel_id=1, source_target_pairs={{0,12},{4,0},{8,4},{12,8},{1,13},{5,1},{9,5},{13,9},{2,14},{6,2},{... | collective-permute-start | bytes 393224 | tf_op jit(solution)/shard_map/ppermute | solution.py:256
  253.2 2.5 collective-permute-done.92.refs_0_
  263.0 2.4 shard_map.123
  277.3 2.5 collective-permute-done.97
  (256 shorter events, 175.3 us)
Async XLA Ops:
  0.6 8.2 %collective-permute-start.3 = (bf16[2048,384]{1,0:T(8,128)(2,1)}, bf16[2048,384]{1,0:T(8,128)(2,1)S(1)}, u32[]{:S(2)}, u32[]{:S(2)}) collective-permute-start(bf16[2048,384]{1,0:T(8,128)(2,1)} %bitcast.26), channel_id=1, source_target_pairs={{0,1},{1,0},{2,3},{3,2},{4,5},{5,4},{6,7},{7,6},{8,9},{9,8},{10,11... | collective-permute-start | bytes 4718600 | tf_op jit(solution)/shard_map/ppermute | solution.py:241
  1.2 7.7 %collective-permute-start.4 = (bf16[2048,384]{1,0:T(8,128)(2,1)}, bf16[2048,384]{1,0:T(8,128)(2,1)S(1)}, u32[]{:S(2)}, u32[]{:S(2)}) collective-permute-start(bf16[2048,384]{1,0:T(8,128)(2,1)} %bitcast.28), channel_id=1, source_target_pairs={{0,1},{1,0},{2,3},{3,2},{4,5},{5,4},{6,7},{7,6},{8,9},{9,8},{10,11... | collective-permute-start | bytes 4718600 | tf_op jit(solution)/shard_map/ppermute | solution.py:241
  1.3 7.8 %collective-permute-start.5 = (bf16[384,2048]{1,0:T(8,128)(2,1)}, bf16[384,2048]{1,0:T(8,128)(2,1)}, u32[]{:S(2)}, u32[]{:S(2)}) collective-permute-start(bf16[384,2048]{1,0:T(8,128)(2,1)} %bitcast.30), channel_id=1, source_target_pairs={{0,1},{1,0},{2,3},{3,2},{4,5},{5,4},{6,7},{7,6},{8,9},{9,8},{10,11... | collective-permute-start | bytes 4718600 | tf_op jit(solution)/shard_map/ppermute | solution.py:241
  4.7 9.5 %collective-permute-start = (bf16[32,2176]{1,0:T(8,128)(2,1)S(1)}, bf16[32,2176]{1,0:T(8,128)(2,1)S(1)}, u32[]{:S(2)}, u32[]{:S(2)}) collective-permute-start(bf16[32,2176]{1,0:T(8,128)(2,1)S(1)} %shard_map.104.refs_0_.refs_4_), channel_id=1, source_target_pairs={{0,18},{1,19},{2,16},{3,17},{16,2},{17,3},{18,0},{19,1},{4,22},{5,... | collective-permute-start | bytes 417800 | tf_op jit(solution)/shard_map/ppermute | solution.py:251
  19.6 7.9 %collective-permute-start.7 = (bf16[32,2048]{1,0:T(8,128)(2,1)S(1)}, bf16[32,2048]{1,0:T(8,128)(2,1)S(1)}, u32[]{:S(2)}, u32[]{:S(2)}) collective-permute-start(bf16[32,2048]{1,0:T(8,128)(2,1)S(1)} %get-tuple-element.93), channel_id=1, source_target_pairs={{0,2},{1,3},{2,0},{3,1},{16,18},{17,19},{18,16},{19,17},{4,6},{5,7... | collective-permute-start | bytes 393224 | tf_op jit(solution)/shard_map/ppermute | solution.py:251
  60.3 7.5 %collective-permute-start.18 = (bf16[32,2048]{1,0:T(8,128)(2,1)S(1)}, bf16[32,2048]{1,0:T(8,128)(2,1)S(1)}, u32[]{:S(2)}, u32[]{:S(2)}) collective-permute-start(bf16[32,2048]{1,0:T(8,128)(2,1)S(1)} %slice_select_fusion.4.refs_0_), channel_id=1, source_target_pairs={{0,2},{1,3},{2,0},{3,1},{16,18},{17,19},{18,16},{19,17},{4,6},{5,7... | collective-permute-start | bytes 393224 | tf_op jit(solution)/shard_map/ppermute | solution.py:251
  88.7 8.3 %collective-permute-start.48 = (bf16[32,2048]{1,0:T(8,128)(2,1)S(1)}, bf16[32,2048]{1,0:T(8,128)(2,1)S(1)}, u32[]{:S(2)}, u32[]{:S(2)}) collective-permute-start(bf16[32,2048]{1,0:T(8,128)(2,1)S(1)} %slice.30.refs_0_), channel_id=1, source_target_pairs={{0,18},{1,19},{2,16},{3,17},{16,2},{17,3},{18,0},{19,1},{4,22},{5,... | collective-permute-start | bytes 393224 | tf_op jit(solution)/shard_map/ppermute | solution.py:251
  90.0 12.1 %collective-permute-start.49 = (bf16[32,2048]{1,0:T(8,128)(2,1)S(1)}, bf16[32,2048]{1,0:T(8,128)(2,1)S(1)}, u32[]{:S(2)}, u32[]{:S(2)}) collective-permute-start(bf16[32,2048]{1,0:T(8,128)(2,1)S(1)} %slice.30.refs_0_), channel_id=1, source_target_pairs={{0,2},{1,3},{2,0},{3,1},{16,18},{17,19},{18,16},{19,17},{4,6},{5,7... | collective-permute-start | bytes 393224 | tf_op jit(solution)/shard_map/ppermute | solution.py:251
  91.3 10.9 %collective-permute-start.50 = (bf16[32,2048]{1,0:T(8,128)(2,1)S(1)}, bf16[32,2048]{1,0:T(8,128)(2,1)S(1)}, u32[]{:S(2)}, u32[]{:S(2)}) collective-permute-start(bf16[32,2048]{1,0:T(8,128)(2,1)S(1)} %slice.30.refs_0_), channel_id=1, source_target_pairs={{0,16},{1,17},{2,18},{3,19},{16,0},{17,1},{18,2},{19,3},{4,20},{5,... | collective-permute-start | bytes 393224 | tf_op jit(solution)/shard_map/ppermute | solution.py:251
  94.8 11.9 %collective-permute-start.29 = (bf16[32,2048]{1,0:T(8,128)(2,1)S(1)}, bf16[32,2048]{1,0:T(8,128)(2,1)S(1)}, u32[]{:S(2)}, u32[]{:S(2)}) collective-permute-start(bf16[32,2048]{1,0:T(8,128)(2,1)S(1)} %get-tuple-element.106), channel_id=1, source_target_pairs={{0,16},{1,17},{2,18},{3,19},{16,0},{17,1},{18,2},{19,3},{4,20},{5,... | collective-permute-start | bytes 393224 | tf_op jit(solution)/shard_map/ppermute | solution.py:251
  95.9 12.3 %collective-permute-start.28 = (bf16[32,2048]{1,0:T(8,128)(2,1)S(1)}, bf16[32,2048]{1,0:T(8,128)(2,1)S(1)}, u32[]{:S(2)}, u32[]{:S(2)}) collective-permute-start(bf16[32,2048]{1,0:T(8,128)(2,1)S(1)} %get-tuple-element.105), channel_id=1, source_target_pairs={{0,2},{1,3},{2,0},{3,1},{16,18},{17,19},{18,16},{19,17},{4,6},{5,7... | collective-permute-start | bytes 393224 | tf_op jit(solution)/shard_map/ppermute | solution.py:251
  97.0 11.1 %collective-permute-start.27 = (bf16[32,2048]{1,0:T(8,128)(2,1)S(1)}, bf16[32,2048]{1,0:T(8,128)(2,1)S(1)}, u32[]{:S(2)}, u32[]{:S(2)}) collective-permute-start(bf16[32,2048]{1,0:T(8,128)(2,1)S(1)} %get-tuple-element.104), channel_id=1, source_target_pairs={{0,18},{1,19},{2,16},{3,17},{16,2},{17,3},{18,0},{19,1},{4,22},{5,... | collective-permute-start | bytes 393224 | tf_op jit(solution)/shard_map/ppermute | solution.py:251
  106.8 7.4 %collective-permute-start.51 = (bf16[32,2048]{1,0:T(8,128)(2,1)S(1)}, bf16[32,2048]{1,0:T(8,128)(2,1)S(1)}, u32[]{:S(2)}, u32[]{:S(2)}) collective-permute-start(bf16[32,2048]{1,0:T(8,128)(2,1)S(1)} %get-tuple-element.126), channel_id=1, source_target_pairs={{0,18},{1,19},{2,16},{3,17},{16,2},{17,3},{18,0},{19,1},{4,22},{5,... | collective-permute-start | bytes 393224 | tf_op jit(solution)/shard_map/ppermute | solution.py:251
  119.7 7.8 %collective-permute-start.55 = (bf16[32,2048]{1,0:T(8,128)(2,1)S(1)}, bf16[32,2048]{1,0:T(8,128)(2,1)S(1)}, u32[]{:S(2)}, u32[]{:S(2)}) collective-permute-start(bf16[32,2048]{1,0:T(8,128)(2,1)S(1)} %slice_select_fusion.refs_0_), channel_id=1, source_target_pairs={{0,18},{1,19},{2,16},{3,17},{16,2},{17,3},{18,0},{19,1},{4,22},{5,... | collective-permute-start | bytes 393224 | tf_op jit(solution)/shard_map/ppermute | solution.py:251
  121.1 7.9 %collective-permute-start.56 = (bf16[32,2048]{1,0:T(8,128)(2,1)S(1)}, bf16[32,2048]{1,0:T(8,128)(2,1)S(1)}, u32[]{:S(2)}, u32[]{:S(2)}) collective-permute-start(bf16[32,2048]{1,0:T(8,128)(2,1)S(1)} %slice_select_fusion.refs_0_), channel_id=1, source_target_pairs={{0,2},{1,3},{2,0},{3,1},{16,18},{17,19},{18,16},{19,17},{4,6},{5,7... | collective-permute-start | bytes 393224 | tf_op jit(solution)/shard_map/ppermute | solution.py:251
  125.4 8.0 %collective-permute-start.36 = (bf16[32,2048]{1,0:T(8,128)(2,1)S(1)}, bf16[32,2048]{1,0:T(8,128)(2,1)S(1)}, u32[]{:S(2)}, u32[]{:S(2)}) collective-permute-start(bf16[32,2048]{1,0:T(8,128)(2,1)S(1)} %get-tuple-element.110), channel_id=1, source_target_pairs={{0,16},{1,17},{2,18},{3,19},{16,0},{17,1},{18,2},{19,3},{4,20},{5,... | collective-permute-start | bytes 393224 | tf_op jit(solution)/shard_map/ppermute | solution.py:251
  126.6 9.3 %collective-permute-start.35 = (bf16[32,2048]{1,0:T(8,128)(2,1)S(1)}, bf16[32,2048]{1,0:T(8,128)(2,1)S(1)}, u32[]{:S(2)}, u32[]{:S(2)}) collective-permute-start(bf16[32,2048]{1,0:T(8,128)(2,1)S(1)} %get-tuple-element.109), channel_id=1, source_target_pairs={{0,2},{1,3},{2,0},{3,1},{16,18},{17,19},{18,16},{19,17},{4,6},{5,7... | collective-permute-start | bytes 393224 | tf_op jit(solution)/shard_map/ppermute | solution.py:251
  127.5 8.4 %collective-permute-start.34 = (bf16[32,2048]{1,0:T(8,128)(2,1)S(1)}, bf16[32,2048]{1,0:T(8,128)(2,1)S(1)}, u32[]{:S(2)}, u32[]{:S(2)}) collective-permute-start(bf16[32,2048]{1,0:T(8,128)(2,1)S(1)} %get-tuple-element.108), channel_id=1, source_target_pairs={{0,18},{1,19},{2,16},{3,17},{16,2},{17,3},{18,0},{19,1},{4,22},{5,... | collective-permute-start | bytes 393224 | tf_op jit(solution)/shard_map/ppermute | solution.py:251
  133.4 7.7 %collective-permute-start.58 = (bf16[32,2048]{1,0:T(8,128)(2,1)S(1)}, bf16[32,2048]{1,0:T(8,128)(2,1)S(1)}, u32[]{:S(2)}, u32[]{:S(2)}) collective-permute-start(bf16[32,2048]{1,0:T(8,128)(2,1)S(1)} %get-tuple-element.134), channel_id=1, source_target_pairs={{0,18},{1,19},{2,16},{3,17},{16,2},{17,3},{18,0},{19,1},{4,22},{5,... | collective-permute-start | bytes 393224 | tf_op jit(solution)/shard_map/ppermute | solution.py:251
  135.9 7.3 %collective-permute-start.37 = (bf16[32,2048]{1,0:T(8,128)(2,1)S(1)}, bf16[32,2048]{1,0:T(8,128)(2,1)S(1)}, u32[]{:S(2)}, u32[]{:S(2)}) collective-permute-start(bf16[32,2048]{1,0:T(8,128)(2,1)S(1)} %add_convert_fusion.2), channel_id=1, source_target_pairs={{0,4},{4,8},{8,12},{12,0},{1,5},{5,9},{9,13},{13,1},{2,6},{6,10},{... | collective-permute-start | bytes 393224 | tf_op jit(solution)/shard_map/ppermute | solution.py:256
  146.9 7.9 %collective-permute-start.62 = (bf16[32,2048]{1,0:T(8,128)(2,1)S(1)}, bf16[32,2048]{1,0:T(8,128)(2,1)S(1)}, u32[]{:S(2)}, u32[]{:S(2)}) collective-permute-start(bf16[32,2048]{1,0:T(8,128)(2,1)S(1)} %slice_select_fusion.1.refs_0_), channel_id=1, source_target_pairs={{0,18},{1,19},{2,16},{3,17},{16,2},{17,3},{18,0},{19,1},{4,22},{5,... | collective-permute-start | bytes 393224 | tf_op jit(solution)/shard_map/ppermute | solution.py:251
  148.5 8.4 %collective-permute-start.63 = (bf16[32,2048]{1,0:T(8,128)(2,1)S(1)}, bf16[32,2048]{1,0:T(8,128)(2,1)S(1)}, u32[]{:S(2)}, u32[]{:S(2)}) collective-permute-start(bf16[32,2048]{1,0:T(8,128)(2,1)S(1)} %slice_select_fusion.1.refs_0_), channel_id=1, source_target_pairs={{0,2},{1,3},{2,0},{3,1},{16,18},{17,19},{18,16},{19,17},{4,6},{5,7... | collective-permute-start | bytes 393224 | tf_op jit(solution)/shard_map/ppermute | solution.py:251
  152.7 8.9 %collective-permute-start.43 = (bf16[32,2048]{1,0:T(8,128)(2,1)S(1)}, bf16[32,2048]{1,0:T(8,128)(2,1)S(1)}, u32[]{:S(2)}, u32[]{:S(2)}) collective-permute-start(bf16[32,2048]{1,0:T(8,128)(2,1)S(1)} %get-tuple-element.114), channel_id=1, source_target_pairs={{0,16},{1,17},{2,18},{3,19},{16,0},{17,1},{18,2},{19,3},{4,20},{5,... | collective-permute-start | bytes 393224 | tf_op jit(solution)/shard_map/ppermute | solution.py:251
  154.2 8.8 %collective-permute-start.42 = (bf16[32,2048]{1,0:T(8,128)(2,1)S(1)}, bf16[32,2048]{1,0:T(8,128)(2,1)S(1)}, u32[]{:S(2)}, u32[]{:S(2)}) collective-permute-start(bf16[32,2048]{1,0:T(8,128)(2,1)S(1)} %get-tuple-element.113), channel_id=1, source_target_pairs={{0,2},{1,3},{2,0},{3,1},{16,18},{17,19},{18,16},{19,17},{4,6},{5,7... | collective-permute-start | bytes 393224 | tf_op jit(solution)/shard_map/ppermute | solution.py:251
  154.9 8.1 %collective-permute-start.41 = (bf16[32,2048]{1,0:T(8,128)(2,1)S(1)}, bf16[32,2048]{1,0:T(8,128)(2,1)S(1)}, u32[]{:S(2)}, u32[]{:S(2)}) collective-permute-start(bf16[32,2048]{1,0:T(8,128)(2,1)S(1)} %get-tuple-element.112), channel_id=1, source_target_pairs={{0,18},{1,19},{2,16},{3,17},{16,2},{17,3},{18,0},{19,1},{4,22},{5,... | collective-permute-start | bytes 393224 | tf_op jit(solution)/shard_map/ppermute | solution.py:251
  159.4 7.5 %collective-permute-start.67 = (bf16[32,2048]{1,0:T(8,128)(2,1)S(1)}, bf16[32,2048]{1,0:T(8,128)(2,1)S(1)}, u32[]{:S(2)}, u32[]{:S(2)}) collective-permute-start(bf16[32,2048]{1,0:T(8,128)(2,1)S(1)} %get-tuple-element.142), channel_id=1, source_target_pairs={{0,16},{1,17},{2,18},{3,19},{16,0},{17,1},{18,2},{19,3},{4,20},{5,... | collective-permute-start | bytes 393224 | tf_op jit(solution)/shard_map/ppermute | solution.py:251
  163.0 10.6 %collective-permute-start.44 = (bf16[32,2048]{1,0:T(8,128)(2,1)S(1)}, bf16[32,2048]{1,0:T(8,128)(2,1)S(1)}, u32[]{:S(2)}, u32[]{:S(2)}) collective-permute-start(bf16[32,2048]{1,0:T(8,128)(2,1)S(1)} %add_convert_fusion.1), channel_id=1, source_target_pairs={{0,4},{4,8},{8,12},{12,0},{1,5},{5,9},{9,13},{13,1},{2,6},{6,10},{... | collective-permute-start | bytes 393224 | tf_op jit(solution)/shard_map/ppermute | solution.py:256
  168.0 9.8 %collective-permute-start.68 = (bf16[32,2048]{1,0:T(8,128)(2,1)S(1)}, bf16[32,2048]{1,0:T(8,128)(2,1)S(1)}, u32[]{:S(2)}, u32[]{:S(2)}) collective-permute-start(bf16[32,2048]{1,0:T(8,128)(2,1)S(1)} %fusion.19), channel_id=1, source_target_pairs={{0,12},{4,0},{8,4},{12,8},{1,13},{5,1},{9,5},{13,9},{2,14},{6,2},{... | collective-permute-start | bytes 393224 | tf_op jit(solution)/shard_map/ppermute | solution.py:256
  177.8 7.4 %collective-permute-start.69 = (bf16[32,2048]{1,0:T(8,128)(2,1)S(1)}, bf16[32,2048]{1,0:T(8,128)(2,1)S(1)}, u32[]{:S(2)}, u32[]{:S(2)}) collective-permute-start(bf16[32,2048]{1,0:T(8,128)(2,1)S(1)} %slice_select_fusion.2.refs_0_), channel_id=1, source_target_pairs={{0,18},{1,19},{2,16},{3,17},{16,2},{17,3},{18,0},{19,1},{4,22},{5,... | collective-permute-start | bytes 393224 | tf_op jit(solution)/shard_map/ppermute | solution.py:251
  179.0 7.8 %collective-permute-start.70 = (bf16[32,2048]{1,0:T(8,128)(2,1)S(1)}, bf16[32,2048]{1,0:T(8,128)(2,1)S(1)}, u32[]{:S(2)}, u32[]{:S(2)}) collective-permute-start(bf16[32,2048]{1,0:T(8,128)(2,1)S(1)} %slice_select_fusion.2.refs_0_), channel_id=1, source_target_pairs={{0,2},{1,3},{2,0},{3,1},{16,18},{17,19},{18,16},{19,17},{4,6},{5,7... | collective-permute-start | bytes 393224 | tf_op jit(solution)/shard_map/ppermute | solution.py:251
  190.8 7.6 %collective-permute-start.73 = (bf16[32,2048]{1,0:T(8,128)(2,1)S(1)}, bf16[32,2048]{1,0:T(8,128)(2,1)S(1)}, u32[]{:S(2)}, u32[]{:S(2)}) collective-permute-start(bf16[32,2048]{1,0:T(8,128)(2,1)S(1)} %get-tuple-element.147), channel_id=1, source_target_pairs={{0,2},{1,3},{2,0},{3,1},{16,18},{17,19},{18,16},{19,17},{4,6},{5,7... | collective-permute-start | bytes 393224 | tf_op jit(solution)/shard_map/ppermute | solution.py:251
  272.2 7.6 %collective-permute-start.97 = (bf16[32,2048]{1,0:T(8,128)(2,1)S(1)}, bf16[32,2048]{1,0:T(8,128)(2,1)S(1)}, u32[]{:S(2)}, u32[]{:S(2)}) collective-permute-start(bf16[32,2048]{1,0:T(8,128)(2,1)S(1)} %get-tuple-element.162), channel_id=1, source_target_pairs={{0,2},{1,3},{2,0},{3,1},{16,18},{17,19},{18,16},{19,17},{4,6},{5,7... | collective-permute-start | bytes 393224 | tf_op jit(solution)/shard_map/ppermute | solution.py:251
  (77 other events, 484.9 us)

commit v3 on v2

--- a/solution.py
+++ b/solution.py
@@ -295,47 +295,47 @@
     )(*operands)
 
 
-def load_kernel(*refs):
-    own, pair, outs, sems = refs[:3], refs[3:6], refs[6:10], refs[10]
-    ff = own[0].shape[1]
-    copies = []
-    for e, (gate_ref, up_ref, down_ref) in enumerate((own, pair)):
-        copies += [
-            pltpu.make_async_copy(gate_ref, outs[e].at[:, :ff], sems.at[3 * e]),
-            pltpu.make_async_copy(up_ref, outs[e].at[:, ff:], sems.at[3 * e + 1]),
-            pltpu.make_async_copy(down_ref, outs[2 + e], sems.at[3 * e + 2]),
-        ]
+def load_kernel(gate_ref, up_ref, down_ref, joint_out, down_out, sems):
+    ff = gate_ref.shape[1]
+    copies = [
+        pltpu.make_async_copy(gate_ref, joint_out.at[:, :ff], sems.at[0]),
+        pltpu.make_async_copy(up_ref, joint_out.at[:, ff:], sems.at[1]),
+        pltpu.make_async_copy(down_ref, down_out, sems.at[2]),
+    ]
     for copy in copies:
         copy.start()
     for copy in copies:
         copy.wait()
 
 
-def loaded(own, pair):
-    gate, _, down = own
-    joint, down = pltpu.VMEM((gate.shape[0], 2 * gate.shape[1]), gate.dtype), pltpu.VMEM(down.shape, down.dtype)
-    specs = [pl.BlockSpec(memory_space=pltpu.HBM)] * 3 + [pl.BlockSpec(memory_space=pl.ANY)] * 3
-    scratch = [pltpu.SemaphoreType.DMA((6,))]
-    return in_vmem(load_kernel, [joint, joint, down, down], scratch, 0, *own, *pair, specs=specs)
+def loaded(gate, up, down):
+    outs = [pltpu.VMEM((gate.shape[0], 2 * gate.shape[1]), gate.dtype), pltpu.VMEM(down.shape, down.dtype)]
+    specs = [pl.BlockSpec(memory_space=pl.ANY)] * 3
+    return in_vmem(load_kernel, outs, [pltpu.SemaphoreType.DMA((3,))], 0, gate, up, down, specs=specs)
 
 
 def stage_kernel(out_ref):
     out_ref[...] = jnp.full(out_ref.shape, lax.axis_index("pipe"), jnp.int32)
 
 
-def first_rows_kernel(token_ref, id_ref, gate_ref, out_ref, copied, sem):
+def first_rows_kernel(token_ref, id_hbm, gate_hbm, out_ref, copied, id_ref, gate_ref, sems):
     rows, width = copied.shape
-    copy = pltpu.make_async_copy(token_ref.at[pl.ds(0, rows), :], copied, sem)
-    copy.start()
+    copy = pltpu.make_async_copy(token_ref.at[pl.ds(0, rows), :], copied, sems.at[0])
+    id_copy = pltpu.make_async_copy(id_hbm, id_ref, sems.at[1])
+    gate_copy = pltpu.make_async_copy(gate_hbm, gate_ref, sems.at[2])
+    for each in (id_copy, gate_copy, copy):
+        each.start()
     owners = lax.axis_size("dp") * lax.axis_size("expert")
     column = lax.broadcasted_iota(jnp.int32, (rows, out_ref.shape[1] - width), 1)
     table = jnp.zeros(column.shape, jnp.float32)
+    id_copy.wait()
+    gate_copy.wait()
+    ids, gates = id_ref[...].T, gate_ref[...].astype(jnp.float32).T
     for micro in range(MICRO):
         window = slice(micro * rows, (micro + 1) * rows)
-        gates = gate_ref[window, :].astype(jnp.float32)
-        for slot in range(id_ref.shape[1]):
-            place = micro * owners + id_ref[window, slot:slot + 1]
-            table = table + jnp.where(column == place, gates[:, slot:slot + 1], 0.0)
+        for slot in range(ids.shape[1]):
+            place = micro * owners + ids[window, slot:slot + 1]
+            table = table + jnp.where(column == place, gates[window, slot:slot + 1], 0.0)
     out_ref[:, width:] = table.astype(jnp.bfloat16)
     copy.wait()
     out_ref[:, :width] = copied[...]
@@ -346,8 +346,10 @@
     owners = lax.axis_size("dp") * lax.axis_size("expert")
     extra = -(-MICRO * owners // LANES) * LANES
     outs = [jax.ShapeDtypeStruct((rows, width + extra), tokens.dtype)]
-    scratch = [pltpu.VMEM((rows, width), tokens.dtype), pltpu.SemaphoreType.DMA]
-    specs = [pl.BlockSpec(memory_space=pl.ANY), VMEM, VMEM]
+    scratch = [pltpu.VMEM((rows, width), tokens.dtype), pltpu.VMEM(ids.shape, ids.dtype)]
+    scratch += [pltpu.VMEM(gates.shape, gates.dtype), pltpu.SemaphoreType.DMA((3,))]
+    specs = [pl.BlockSpec(memory_space=pl.ANY)] * 3
+    tokens, ids, gates = (pltpu.with_memory_space_constraint(value, pltpu.HBM) for value in (tokens, ids, gates))
     return in_vmem(first_rows_kernel, outs, scratch, 0, tokens, ids, gates, specs=specs)[0]
 
 
@@ -524,7 +526,9 @@
 
     own = [pltpu.with_memory_space_constraint(w[0, 0], pltpu.HBM) for w in (w_gate, w_up, w_down)]
     theirs = [swap_cores(w) for w in own]
-    forward_weights = loaded(own, theirs)
+    joint, down = loaded(*own)
+    pair_joint, pair_down = loaded(*[pltpu.with_memory_space_constraint(w, pltpu.VMEM) for w in theirs])
+    forward_weights = (joint, pair_joint, down, pair_down)
     backward_weights = []
     for number, part in enumerate(forward_weights):
         backward_weights.append(turned(part))
@@ -541,9 +545,11 @@
     behind = ahead = None
     last = ticks + stages - 2
     for tick in range(last + 1):
+        if tick == stages - 1:
+            grad_blocks = spread(lax.optimization_barrier((cotangent[:rows], *outs[-1:]))[0])
         if tick < ticks:
             if tick == 0:
-                here = first_rows(tokens, owner_ids[0], gate_weights[0])
+                here = first_rows(tokens, owner_ids[0].T, gate_weights[0].T)
             elif tick < MICRO:
                 here = jnp.where(stage == 0, tokens[tick * rows:(tick + 1) * rows], behind)
             else:
@@ -569,7 +575,8 @@
                 grad = jnp.where(stage == stages - 1, cotangent[number * rows:(number + 1) * rows], ahead)
             else:
                 grad = ahead
-            grad_blocks = spread(grad)
+            if number:
+                grad_blocks = spread(grad)
             gained, sums = backward_experts(first, picks, grad_blocks, rates, normeds, backward_weights)
             sums = collect(sums)
             normed_grad = sum(p.astype(f32) for p in sums)

time: 282 us -> 279 us (0.989)
  waiting for transfers between devices: 97.1 us -> 107 us
  starting transfers between devices: 133 us -> 124 us
  local copies, waits for them, and re-layouts: 4.04 us -> 0.03 us
    ppermute x12, starting transfers between devices: 28.4 us -> 19.7 us  [hopped(): lax.ppermute(value, 'pipe', [(s, (s + step) % stages) for s in range(stag...]
    ppermute x87, waiting for transfers between devices: 68.5 us -> 74.5 us  [shifted(): return lax.ppermute(value, ('dp', 'expert'), pairs)]
    ppermute x12, waiting for transfers between devices: 28.4 us -> 32.5 us  [hopped(): lax.ppermute(value, 'pipe', [(s, (s + step) % stages) for s in range(stag...]
    unnamed x14 -> x6, local copies, waits for them, and re-layouts: 4.03 us -> 0.02 us
    pallas_call x21 -> x22, Pallas kernels: 39.8 us -> 39.8 us  [in_vmem(): pl.pallas_call(kernel, out_shape=outs, in_specs=specs or [VMEM] * len(ope...]
  transfers between devices with their start and end apart: 103 -> 103, of which waited for: 57 -> 60; matrix products, arithmetic and copies ran while one was open for 2% -> 1% of each run, Pallas kernels for 9% -> 9%
where the time goes in v3:
time: 279 us
  starting transfers between devices  124 us (44%)
  waiting for transfers between devices  107 us (38%)
  Pallas kernels  39.8 us (14%)
  other arithmetic  6.65 us (2%)
    ppermute x87, starting transfers between devices, shifted(): return lax.ppermute(value, ('dp', 'expert'), pairs)  103 us
    ppermute x87, waiting for transfers between devices, shifted(): return lax.ppermute(value, ('dp', 'expert'), pairs)  74.5 us
    pallas_call x22, Pallas kernels, in_vmem(): pl.pallas_call(kernel, out_shape=outs, in_specs=specs or [VMEM] * len(ope...  39.8 us
    ppermute x12, waiting for transfers between devices, hopped(): lax.ppermute(value, 'pipe', [(s, (s + step) % stages) for s in range(stag...  32.5 us
    ppermute x12, starting transfers between devices, hopped(): lax.ppermute(value, 'pipe', [(s, (s + step) % stages) for s in range(stag...  19.7 us
  transfers between devices with their start and end apart: 103, of which 60 were waited for; matrix products, arithmetic and copies ran while one was open for 1% of the time, Pallas kernels for 9%

profile of v3, /device:TPU:0, one launch (start us, length us, event | category | flops | bytes accessed | tf_op | source)
XLA Modules:
  0.0 279.0 jit_solution(11616257970229042017)
XLA Ops:
  2.8 3.6 %collective-permute-start = (bf16[32,2176]{1,0:T(8,128)(2,1)S(1)}, bf16[32,2176]{1,0:T(8,128)(2,1)S(1)}, u32[]{:S(2)}, u32[]{:S(2)}) collective-permute-start(bf16[32,2176]{1,0:T(8,128)(2,1)S(1)} %shard_map.104.refs_0_.refs_4_), channel_id=1, source_target_pairs={{0,18},{1,19},{2,16},{3,17},{16,2},{17,3},{18,0},{19,1},{4,22},{5,... | collective-permute-start | bytes 417800 | tf_op jit(solution)/shard_map/ppermute | solution.py:251
  7.3 2.4 shard_map.105
  10.9 2.7 collective-permute-done.1.refs_2_.refs_6_
  21.5 4.0 %collective-permute-done.7 = bf16[32,2048]{1,0:T(8,128)(2,1)S(1)} collective-permute-done((bf16[32,2048]{1,0:T(8,128)(2,1)S(1)}, bf16[32,2048]{1,0:T(8,128)(2,1)S(1)}, u32[]{:S(2)}, u32[]{:S(2)}) %collective-permute-start.7) | collective-permute-done | bytes 131104 | tf_op jit(solution)/shard_map/ppermute | solution.py:251
  27.3 5.1 %collective-permute-done.9 = bf16[32,2048]{1,0:T(8,128)(2,1)S(1)} collective-permute-done((bf16[32,2048]{1,0:T(8,128)(2,1)S(1)}, bf16[32,2048]{1,0:T(8,128)(2,1)S(1)}, u32[]{:S(2)}, u32[]{:S(2)}) %collective-permute-start.9) | collective-permute-done | bytes 131104 | tf_op jit(solution)/shard_map/ppermute | solution.py:256
  36.0 2.5 collective-permute-done.10.refs_1_
  50.0 6.8 %collective-permute-done.16 = bf16[32,2048]{1,0:T(8,128)(2,1)S(1)} collective-permute-done((bf16[32,2048]{1,0:T(8,128)(2,1)S(1)}, bf16[32,2048]{1,0:T(8,128)(2,1)S(1)}, u32[]{:S(2)}, u32[]{:S(2)}) %collective-permute-start.16) | collective-permute-done | bytes 131104 | tf_op jit(solution)/shard_map/ppermute | solution.py:256
  60.4 3.1 %collective-permute-done.17.refs_1_ = bf16[32,2048]{1,0:T(8,128)(2,1)S(1)} collective-permute-done((bf16[32,2048]{1,0:T(8,128)(2,1)S(1)}, bf16[32,2048]{1,0:T(8,128)(2,1)S(1)}, u32[]{:S(2)}, u32[]{:S(2)}) %collective-permute-start.17) | collective-permute-done | bytes 131104 | tf_op jit(solution)/shard_map/ppermute | solution.py:251
  63.5 2.4 collective-permute-done.18.refs_2_
  76.4 6.8 %collective-permute-done.23 = bf16[32,2048]{1,0:T(8,128)(2,1)S(1)} collective-permute-done((bf16[32,2048]{1,0:T(8,128)(2,1)S(1)}, bf16[32,2048]{1,0:T(8,128)(2,1)S(1)}, u32[]{:S(2)}, u32[]{:S(2)}) %collective-permute-start.23) | collective-permute-done | bytes 131104 | tf_op jit(solution)/shard_map/ppermute | solution.py:256
  100.2 2.6 shard_map.118
  106.5 2.7 collective-permute-done.53
  127.3 2.4 shard_map.119
  134.4 2.8 collective-permute-start.37
  137.2 2.3 collective-permute-done.58
  144.9 2.8 collective-permute-done.61
  158.1 2.4 shard_map.120
  166.7 3.1 %collective-permute-done.65 = bf16[32,2048]{1,0:T(8,128)(2,1)S(1)} collective-permute-done((bf16[32,2048]{1,0:T(8,128)(2,1)S(1)}, bf16[32,2048]{1,0:T(8,128)(2,1)S(1)}, u32[]{:S(2)}, u32[]{:S(2)}) %collective-permute-start.65) | collective-permute-done | bytes 131104 | tf_op jit(solution)/shard_map/ppermute | solution.py:251
  184.6 2.4 shard_map.121
  192.8 3.1 %collective-permute-done.73 = bf16[32,2048]{1,0:T(8,128)(2,1)S(1)} collective-permute-done((bf16[32,2048]{1,0:T(8,128)(2,1)S(1)}, bf16[32,2048]{1,0:T(8,128)(2,1)S(1)}, u32[]{:S(2)}, u32[]{:S(2)}) %collective-permute-start.73) | collective-permute-done | bytes 131104 | tf_op jit(solution)/shard_map/ppermute | solution.py:251
  196.4 4.0 %collective-permute-start.76 = (bf16[32,2048]{1,0:T(8,128)(2,1)S(1)}, bf16[32,2048]{1,0:T(8,128)(2,1)S(1)}, u32[]{:S(2)}, u32[]{:S(2)}) collective-permute-start(bf16[32,2048]{1,0:T(8,128)(2,1)S(1)} %fusion.26), channel_id=1, source_target_pairs={{0,12},{4,0},{8,4},{12,8},{1,13},{5,1},{9,5},{13,9},{2,14},{6,2},{... | collective-permute-start | bytes 393224 | tf_op jit(solution)/shard_map/ppermute | solution.py:256
  200.4 2.5 collective-permute-done.76.refs_0_
  206.4 2.5 collective-permute-done.77.refs_1_
  210.3 2.4 shard_map.122
  221.2 4.2 %collective-permute-start.84 = (bf16[32,2048]{1,0:T(8,128)(2,1)S(1)}, bf16[32,2048]{1,0:T(8,128)(2,1)S(1)}, u32[]{:S(2)}, u32[]{:S(2)}) collective-permute-start(bf16[32,2048]{1,0:T(8,128)(2,1)S(1)} %fusion.33), channel_id=1, source_target_pairs={{0,12},{4,0},{8,4},{12,8},{1,13},{5,1},{9,5},{13,9},{2,14},{6,2},{... | collective-permute-start | bytes 393224 | tf_op jit(solution)/shard_map/ppermute | solution.py:256
  225.4 2.5 collective-permute-done.84.refs_0_
  231.4 2.5 collective-permute-done.85.refs_1_
  235.6 2.4 shard_map.123
  246.3 4.3 %collective-permute-start.92 = (bf16[32,2048]{1,0:T(8,128)(2,1)S(1)}, bf16[32,2048]{1,0:T(8,128)(2,1)S(1)}, u32[]{:S(2)}, u32[]{:S(2)}) collective-permute-start(bf16[32,2048]{1,0:T(8,128)(2,1)S(1)} %fusion.40), channel_id=1, source_target_pairs={{0,12},{4,0},{8,4},{12,8},{1,13},{5,1},{9,5},{13,9},{2,14},{6,2},{... | collective-permute-start | bytes 393224 | tf_op jit(solution)/shard_map/ppermute | solution.py:256
  250.6 2.5 collective-permute-done.92.refs_0_
  260.4 2.6 shard_map.124
  274.6 2.9 %collective-permute-done.97 = bf16[32,2048]{1,0:T(8,128)(2,1)S(1)} collective-permute-done((bf16[32,2048]{1,0:T(8,128)(2,1)S(1)}, bf16[32,2048]{1,0:T(8,128)(2,1)S(1)}, u32[]{:S(2)}, u32[]{:S(2)}) %collective-permute-start.97) | collective-permute-done | bytes 131104 | tf_op jit(solution)/shard_map/ppermute | solution.py:251
  (249 shorter events, 176.9 us)
Async XLA Ops:
  1.2 8.5 %collective-permute-start.4 = (bf16[2048,384]{1,0:T(8,128)(2,1)}, bf16[2048,384]{1,0:T(8,128)(2,1)S(1)}, u32[]{:S(2)}, u32[]{:S(2)}) collective-permute-start(bf16[2048,384]{1,0:T(8,128)(2,1)} %bitcast.30), channel_id=1, source_target_pairs={{0,1},{1,0},{2,3},{3,2},{4,5},{5,4},{6,7},{7,6},{8,9},{9,8},{10,11... | collective-permute-start | bytes 4718600 | tf_op jit(solution)/shard_map/ppermute | solution.py:241
  1.3 8.4 %collective-permute-start.5 = (bf16[384,2048]{1,0:T(8,128)(2,1)}, bf16[384,2048]{1,0:T(8,128)(2,1)S(1)}, u32[]{:S(2)}, u32[]{:S(2)}) collective-permute-start(bf16[384,2048]{1,0:T(8,128)(2,1)} %bitcast.32), channel_id=1, source_target_pairs={{0,1},{1,0},{2,3},{3,2},{4,5},{5,4},{6,7},{7,6},{8,9},{9,8},{10,11... | collective-permute-start | bytes 4718600 | tf_op jit(solution)/shard_map/ppermute | solution.py:241
  2.8 8.1 %collective-permute-start = (bf16[32,2176]{1,0:T(8,128)(2,1)S(1)}, bf16[32,2176]{1,0:T(8,128)(2,1)S(1)}, u32[]{:S(2)}, u32[]{:S(2)}) collective-permute-start(bf16[32,2176]{1,0:T(8,128)(2,1)S(1)} %shard_map.104.refs_0_.refs_4_), channel_id=1, source_target_pairs={{0,18},{1,19},{2,16},{3,17},{16,2},{17,3},{18,0},{19,1},{4,22},{5,... | collective-permute-start | bytes 417800 | tf_op jit(solution)/shard_map/ppermute | solution.py:251
  17.7 7.9 %collective-permute-start.7 = (bf16[32,2048]{1,0:T(8,128)(2,1)S(1)}, bf16[32,2048]{1,0:T(8,128)(2,1)S(1)}, u32[]{:S(2)}, u32[]{:S(2)}) collective-permute-start(bf16[32,2048]{1,0:T(8,128)(2,1)S(1)} %get-tuple-element.94), channel_id=1, source_target_pairs={{0,2},{1,3},{2,0},{3,1},{16,18},{17,19},{18,16},{19,17},{4,6},{5,7... | collective-permute-start | bytes 393224 | tf_op jit(solution)/shard_map/ppermute | solution.py:251
  58.3 7.5 %collective-permute-start.18 = (bf16[32,2048]{1,0:T(8,128)(2,1)S(1)}, bf16[32,2048]{1,0:T(8,128)(2,1)S(1)}, u32[]{:S(2)}, u32[]{:S(2)}) collective-permute-start(bf16[32,2048]{1,0:T(8,128)(2,1)S(1)} %slice_select_fusion.4.refs_0_), channel_id=1, source_target_pairs={{0,2},{1,3},{2,0},{3,1},{16,18},{17,19},{18,16},{19,17},{4,6},{5,7... | collective-permute-start | bytes 393224 | tf_op jit(solution)/shard_map/ppermute | solution.py:251
  86.7 8.4 %collective-permute-start.48 = (bf16[32,2048]{1,0:T(8,128)(2,1)S(1)}, bf16[32,2048]{1,0:T(8,128)(2,1)S(1)}, u32[]{:S(2)}, u32[]{:S(2)}) collective-permute-start(bf16[32,2048]{1,0:T(8,128)(2,1)S(1)} %slice.31.refs_0_), channel_id=1, source_target_pairs={{0,18},{1,19},{2,16},{3,17},{16,2},{17,3},{18,0},{19,1},{4,22},{5,... | collective-permute-start | bytes 393224 | tf_op jit(solution)/shard_map/ppermute | solution.py:251
  88.1 12.1 %collective-permute-start.49 = (bf16[32,2048]{1,0:T(8,128)(2,1)S(1)}, bf16[32,2048]{1,0:T(8,128)(2,1)S(1)}, u32[]{:S(2)}, u32[]{:S(2)}) collective-permute-start(bf16[32,2048]{1,0:T(8,128)(2,1)S(1)} %slice.31.refs_0_), channel_id=1, source_target_pairs={{0,2},{1,3},{2,0},{3,1},{16,18},{17,19},{18,16},{19,17},{4,6},{5,7... | collective-permute-start | bytes 393224 | tf_op jit(solution)/shard_map/ppermute | solution.py:251
  89.3 10.9 %collective-permute-start.50 = (bf16[32,2048]{1,0:T(8,128)(2,1)S(1)}, bf16[32,2048]{1,0:T(8,128)(2,1)S(1)}, u32[]{:S(2)}, u32[]{:S(2)}) collective-permute-start(bf16[32,2048]{1,0:T(8,128)(2,1)S(1)} %slice.31.refs_0_), channel_id=1, source_target_pairs={{0,16},{1,17},{2,18},{3,19},{16,0},{17,1},{18,2},{19,3},{4,20},{5,... | collective-permute-start | bytes 393224 | tf_op jit(solution)/shard_map/ppermute | solution.py:251
  92.9 12.1 %collective-permute-start.29 = (bf16[32,2048]{1,0:T(8,128)(2,1)S(1)}, bf16[32,2048]{1,0:T(8,128)(2,1)S(1)}, u32[]{:S(2)}, u32[]{:S(2)}) collective-permute-start(bf16[32,2048]{1,0:T(8,128)(2,1)S(1)} %get-tuple-element.107), channel_id=1, source_target_pairs={{0,16},{1,17},{2,18},{3,19},{16,0},{17,1},{18,2},{19,3},{4,20},{5,... | collective-permute-start | bytes 393224 | tf_op jit(solution)/shard_map/ppermute | solution.py:251
  93.9 12.5 %collective-permute-start.28 = (bf16[32,2048]{1,0:T(8,128)(2,1)S(1)}, bf16[32,2048]{1,0:T(8,128)(2,1)S(1)}, u32[]{:S(2)}, u32[]{:S(2)}) collective-permute-start(bf16[32,2048]{1,0:T(8,128)(2,1)S(1)} %get-tuple-element.106), channel_id=1, source_target_pairs={{0,2},{1,3},{2,0},{3,1},{16,18},{17,19},{18,16},{19,17},{4,6},{5,7... | collective-permute-start | bytes 393224 | tf_op jit(solution)/shard_map/ppermute | solution.py:251
  95.1 11.3 %collective-permute-start.27 = (bf16[32,2048]{1,0:T(8,128)(2,1)S(1)}, bf16[32,2048]{1,0:T(8,128)(2,1)S(1)}, u32[]{:S(2)}, u32[]{:S(2)}) collective-permute-start(bf16[32,2048]{1,0:T(8,128)(2,1)S(1)} %get-tuple-element.105), channel_id=1, source_target_pairs={{0,18},{1,19},{2,16},{3,17},{16,2},{17,3},{18,0},{19,1},{4,22},{5,... | collective-permute-start | bytes 393224 | tf_op jit(solution)/shard_map/ppermute | solution.py:251
  105.0 7.4 %collective-permute-start.51 = (bf16[32,2048]{1,0:T(8,128)(2,1)S(1)}, bf16[32,2048]{1,0:T(8,128)(2,1)S(1)}, u32[]{:S(2)}, u32[]{:S(2)}) collective-permute-start(bf16[32,2048]{1,0:T(8,128)(2,1)S(1)} %get-tuple-element.128), channel_id=1, source_target_pairs={{0,18},{1,19},{2,16},{3,17},{16,2},{17,3},{18,0},{19,1},{4,22},{5,... | collective-permute-start | bytes 393224 | tf_op jit(solution)/shard_map/ppermute | solution.py:251
  117.9 8.1 %collective-permute-start.55 = (bf16[32,2048]{1,0:T(8,128)(2,1)S(1)}, bf16[32,2048]{1,0:T(8,128)(2,1)S(1)}, u32[]{:S(2)}, u32[]{:S(2)}) collective-permute-start(bf16[32,2048]{1,0:T(8,128)(2,1)S(1)} %slice_select_fusion.refs_0_), channel_id=1, source_target_pairs={{0,18},{1,19},{2,16},{3,17},{16,2},{17,3},{18,0},{19,1},{4,22},{5,... | collective-permute-start | bytes 393224 | tf_op jit(solution)/shard_map/ppermute | solution.py:251
  119.5 7.8 %collective-permute-start.56 = (bf16[32,2048]{1,0:T(8,128)(2,1)S(1)}, bf16[32,2048]{1,0:T(8,128)(2,1)S(1)}, u32[]{:S(2)}, u32[]{:S(2)}) collective-permute-start(bf16[32,2048]{1,0:T(8,128)(2,1)S(1)} %slice_select_fusion.refs_0_), channel_id=1, source_target_pairs={{0,2},{1,3},{2,0},{3,1},{16,18},{17,19},{18,16},{19,17},{4,6},{5,7... | collective-permute-start | bytes 393224 | tf_op jit(solution)/shard_map/ppermute | solution.py:251
  123.8 8.2 %collective-permute-start.36 = (bf16[32,2048]{1,0:T(8,128)(2,1)S(1)}, bf16[32,2048]{1,0:T(8,128)(2,1)S(1)}, u32[]{:S(2)}, u32[]{:S(2)}) collective-permute-start(bf16[32,2048]{1,0:T(8,128)(2,1)S(1)} %get-tuple-element.111), channel_id=1, source_target_pairs={{0,16},{1,17},{2,18},{3,19},{16,0},{17,1},{18,2},{19,3},{4,20},{5,... | collective-permute-start | bytes 393224 | tf_op jit(solution)/shard_map/ppermute | solution.py:251
  125.2 9.2 %collective-permute-start.35 = (bf16[32,2048]{1,0:T(8,128)(2,1)S(1)}, bf16[32,2048]{1,0:T(8,128)(2,1)S(1)}, u32[]{:S(2)}, u32[]{:S(2)}) collective-permute-start(bf16[32,2048]{1,0:T(8,128)(2,1)S(1)} %get-tuple-element.110), channel_id=1, source_target_pairs={{0,2},{1,3},{2,0},{3,1},{16,18},{17,19},{18,16},{19,17},{4,6},{5,7... | collective-permute-start | bytes 393224 | tf_op jit(solution)/shard_map/ppermute | solution.py:251
  126.1 8.3 %collective-permute-start.34 = (bf16[32,2048]{1,0:T(8,128)(2,1)S(1)}, bf16[32,2048]{1,0:T(8,128)(2,1)S(1)}, u32[]{:S(2)}, u32[]{:S(2)}) collective-permute-start(bf16[32,2048]{1,0:T(8,128)(2,1)S(1)} %get-tuple-element.109), channel_id=1, source_target_pairs={{0,18},{1,19},{2,16},{3,17},{16,2},{17,3},{18,0},{19,1},{4,22},{5,... | collective-permute-start | bytes 393224 | tf_op jit(solution)/shard_map/ppermute | solution.py:251
  129.7 7.5 %collective-permute-start.60 = (bf16[32,2048]{1,0:T(8,128)(2,1)S(1)}, bf16[32,2048]{1,0:T(8,128)(2,1)S(1)}, u32[]{:S(2)}, u32[]{:S(2)}) collective-permute-start(bf16[32,2048]{1,0:T(8,128)(2,1)S(1)} %get-tuple-element.138), channel_id=1, source_target_pairs={{0,16},{1,17},{2,18},{3,19},{16,0},{17,1},{18,2},{19,3},{4,20},{5,... | collective-permute-start | bytes 393224 | tf_op jit(solution)/shard_map/ppermute | solution.py:251
  132.0 7.5 %collective-permute-start.58 = (bf16[32,2048]{1,0:T(8,128)(2,1)S(1)}, bf16[32,2048]{1,0:T(8,128)(2,1)S(1)}, u32[]{:S(2)}, u32[]{:S(2)}) collective-permute-start(bf16[32,2048]{1,0:T(8,128)(2,1)S(1)} %get-tuple-element.136), channel_id=1, source_target_pairs={{0,18},{1,19},{2,16},{3,17},{16,2},{17,3},{18,0},{19,1},{4,22},{5,... | collective-permute-start | bytes 393224 | tf_op jit(solution)/shard_map/ppermute | solution.py:251
  139.9 7.8 %collective-permute-start.61 = (bf16[32,2048]{1,0:T(8,128)(2,1)S(1)}, bf16[32,2048]{1,0:T(8,128)(2,1)S(1)}, u32[]{:S(2)}, u32[]{:S(2)}) collective-permute-start(bf16[32,2048]{1,0:T(8,128)(2,1)S(1)} %fusion.12), channel_id=1, source_target_pairs={{0,12},{4,0},{8,4},{12,8},{1,13},{5,1},{9,5},{13,9},{2,14},{6,2},{... | collective-permute-start | bytes 393224 | tf_op jit(solution)/shard_map/ppermute | solution.py:256
  141.4 8.7 %collective-permute-start.38 = (bf16[32,2048]{1,0:T(8,128)(2,1)S(1)}, bf16[32,2048]{1,0:T(8,128)(2,1)S(1)}, u32[]{:S(2)}, u32[]{:S(2)}) collective-permute-start(bf16[32,2048]{1,0:T(8,128)(2,1)S(1)} %collective-permute-done.37.refs_0_), channel_id=1, source_target_pairs={{0,18},{1,19},{2,16},{3,17},{16,2},{17,3},{18,0},{19,1},{4,22},{5,... | collective-permute-start | bytes 393224 | tf_op jit(solution)/shard_map/ppermute | solution.py:251
  142.8 8.5 %collective-permute-start.39 = (bf16[32,2048]{1,0:T(8,128)(2,1)S(1)}, bf16[32,2048]{1,0:T(8,128)(2,1)S(1)}, u32[]{:S(2)}, u32[]{:S(2)}) collective-permute-start(bf16[32,2048]{1,0:T(8,128)(2,1)S(1)} %collective-permute-done.37.refs_0_), channel_id=1, source_target_pairs={{0,2},{1,3},{2,0},{3,1},{16,18},{17,19},{18,16},{19,17},{4,6},{5,7... | collective-permute-start | bytes 393224 | tf_op jit(solution)/shard_map/ppermute | solution.py:251
  143.8 7.5 %collective-permute-start.40 = (bf16[32,2048]{1,0:T(8,128)(2,1)S(1)}, bf16[32,2048]{1,0:T(8,128)(2,1)S(1)}, u32[]{:S(2)}, u32[]{:S(2)}) collective-permute-start(bf16[32,2048]{1,0:T(8,128)(2,1)S(1)} %collective-permute-done.37.refs_0_), channel_id=1, source_target_pairs={{0,16},{1,17},{2,18},{3,19},{16,0},{17,1},{18,2},{19,3},{4,20},{5,... | collective-permute-start | bytes 393224 | tf_op jit(solution)/shard_map/ppermute | solution.py:251
  147.7 7.7 %collective-permute-start.62 = (bf16[32,2048]{1,0:T(8,128)(2,1)S(1)}, bf16[32,2048]{1,0:T(8,128)(2,1)S(1)}, u32[]{:S(2)}, u32[]{:S(2)}) collective-permute-start(bf16[32,2048]{1,0:T(8,128)(2,1)S(1)} %slice_select_fusion.1.refs_0_), channel_id=1, source_target_pairs={{0,18},{1,19},{2,16},{3,17},{16,2},{17,3},{18,0},{19,1},{4,22},{5,... | collective-permute-start | bytes 393224 | tf_op jit(solution)/shard_map/ppermute | solution.py:251
  149.2 9.0 %collective-permute-start.63 = (bf16[32,2048]{1,0:T(8,128)(2,1)S(1)}, bf16[32,2048]{1,0:T(8,128)(2,1)S(1)}, u32[]{:S(2)}, u32[]{:S(2)}) collective-permute-start(bf16[32,2048]{1,0:T(8,128)(2,1)S(1)} %slice_select_fusion.1.refs_0_), channel_id=1, source_target_pairs={{0,2},{1,3},{2,0},{3,1},{16,18},{17,19},{18,16},{19,17},{4,6},{5,7... | collective-permute-start | bytes 393224 | tf_op jit(solution)/shard_map/ppermute | solution.py:251
  150.1 8.0 %collective-permute-start.64 = (bf16[32,2048]{1,0:T(8,128)(2,1)S(1)}, bf16[32,2048]{1,0:T(8,128)(2,1)S(1)}, u32[]{:S(2)}, u32[]{:S(2)}) collective-permute-start(bf16[32,2048]{1,0:T(8,128)(2,1)S(1)} %slice_select_fusion.1.refs_0_), channel_id=1, source_target_pairs={{0,16},{1,17},{2,18},{3,19},{16,0},{17,1},{18,2},{19,3},{4,20},{5,... | collective-permute-start | bytes 393224 | tf_op jit(solution)/shard_map/ppermute | solution.py:251
  153.5 9.1 %collective-permute-start.43 = (bf16[32,2048]{1,0:T(8,128)(2,1)S(1)}, bf16[32,2048]{1,0:T(8,128)(2,1)S(1)}, u32[]{:S(2)}, u32[]{:S(2)}) collective-permute-start(bf16[32,2048]{1,0:T(8,128)(2,1)S(1)} %get-tuple-element.115), channel_id=1, source_target_pairs={{0,16},{1,17},{2,18},{3,19},{16,0},{17,1},{18,2},{19,3},{4,20},{5,... | collective-permute-start | bytes 393224 | tf_op jit(solution)/shard_map/ppermute | solution.py:251
  154.4 9.7 %collective-permute-start.42 = (bf16[32,2048]{1,0:T(8,128)(2,1)S(1)}, bf16[32,2048]{1,0:T(8,128)(2,1)S(1)}, u32[]{:S(2)}, u32[]{:S(2)}) collective-permute-start(bf16[32,2048]{1,0:T(8,128)(2,1)S(1)} %get-tuple-element.114), channel_id=1, source_target_pairs={{0,2},{1,3},{2,0},{3,1},{16,18},{17,19},{18,16},{19,17},{4,6},{5,7... | collective-permute-start | bytes 393224 | tf_op jit(solution)/shard_map/ppermute | solution.py:251
  155.5 8.6 %collective-permute-start.41 = (bf16[32,2048]{1,0:T(8,128)(2,1)S(1)}, bf16[32,2048]{1,0:T(8,128)(2,1)S(1)}, u32[]{:S(2)}, u32[]{:S(2)}) collective-permute-start(bf16[32,2048]{1,0:T(8,128)(2,1)S(1)} %get-tuple-element.113), channel_id=1, source_target_pairs={{0,18},{1,19},{2,16},{3,17},{16,2},{17,3},{18,0},{19,1},{4,22},{5,... | collective-permute-start | bytes 393224 | tf_op jit(solution)/shard_map/ppermute | solution.py:251
  171.0 8.2 %collective-permute-start.45 = (bf16[32,2048]{1,0:T(8,128)(2,1)S(1)}, bf16[32,2048]{1,0:T(8,128)(2,1)S(1)}, u32[]{:S(2)}, u32[]{:S(2)}) collective-permute-start(bf16[32,2048]{1,0:T(8,128)(2,1)S(1)} %collective-permute-done.44.refs_0_), channel_id=1, source_target_pairs={{0,18},{1,19},{2,16},{3,17},{16,2},{17,3},{18,0},{19,1},{4,22},{5,... | collective-permute-start | bytes 393224 | tf_op jit(solution)/shard_map/ppermute | solution.py:251
  188.4 7.5 %collective-permute-start.73 = (bf16[32,2048]{1,0:T(8,128)(2,1)S(1)}, bf16[32,2048]{1,0:T(8,128)(2,1)S(1)}, u32[]{:S(2)}, u32[]{:S(2)}) collective-permute-start(bf16[32,2048]{1,0:T(8,128)(2,1)S(1)} %get-tuple-element.149), channel_id=1, source_target_pairs={{0,2},{1,3},{2,0},{3,1},{16,18},{17,19},{18,16},{19,17},{4,6},{5,7... | collective-permute-start | bytes 393224 | tf_op jit(solution)/shard_map/ppermute | solution.py:251
  269.9 7.6 %collective-permute-start.97 = (bf16[32,2048]{1,0:T(8,128)(2,1)S(1)}, bf16[32,2048]{1,0:T(8,128)(2,1)S(1)}, u32[]{:S(2)}, u32[]{:S(2)}) collective-permute-start(bf16[32,2048]{1,0:T(8,128)(2,1)S(1)} %get-tuple-element.164), channel_id=1, source_target_pairs={{0,2},{1,3},{2,0},{3,1},{16,18},{17,19},{18,16},{19,17},{4,6},{5,7... | collective-permute-start | bytes 393224 | tf_op jit(solution)/shard_map/ppermute | solution.py:251
  (74 other events, 479.6 us)

commit v4 on v3

--- a/solution.py
+++ b/solution.py
@@ -9,6 +9,7 @@
 
 MICRO = 4
 LIMIT = 12 * 1024 * 1024
+DP, PIPE, EXPERT = "dp", "pipe", "expert"
 
 
 epsilon = 1e-06
@@ -49,22 +50,22 @@
 
 def send_rows(row_block, pair_block):
     got_rows, got_pairs = (
-        lax.all_to_all(row_block, ("dp", "expert"), split_axis=0, concat_axis=0, tiled=True),
-        lax.all_to_all(pair_block, ("dp", "expert"), split_axis=0, concat_axis=0, tiled=True),
+        lax.all_to_all(row_block, (DP, EXPERT), split_axis=0, concat_axis=0, tiled=True),
+        lax.all_to_all(pair_block, (DP, EXPERT), split_axis=0, concat_axis=0, tiled=True),
     )
     return (got_rows, got_pairs)
 
 
 def return_rows(row_block):
-    return lax.all_to_all(row_block, ("dp", "expert"), split_axis=0, concat_axis=0, tiled=True)
+    return lax.all_to_all(row_block, (DP, EXPERT), split_axis=0, concat_axis=0, tiled=True)
 
 
 def send_grads(row_block):
-    return lax.all_to_all(row_block, ("dp", "expert"), split_axis=0, concat_axis=0, tiled=True)
+    return lax.all_to_all(row_block, (DP, EXPERT), split_axis=0, concat_axis=0, tiled=True)
 
 
 def return_grads(row_block):
-    return lax.all_to_all(row_block, ("dp", "expert"), split_axis=0, concat_axis=0, tiled=True)
+    return lax.all_to_all(row_block, (DP, EXPERT), split_axis=0, concat_axis=0, tiled=True)
 
 
 def expert_forward(flat_rows, flat_pairs, joint_mats, down_mats):
@@ -96,9 +97,9 @@
 
 
 def slot_body(tokens, cotangent, owner_ids, gate_weights, norm_gain, w_gate, w_up, w_down):
-    segments = lax.axis_size("pipe")
-    segment_index = lax.axis_index("pipe")
-    owners = lax.axis_size("dp") * lax.axis_size("expert")
+    segments = lax.axis_size(PIPE)
+    segment_index = lax.axis_index(PIPE)
+    owners = lax.axis_size(DP) * lax.axis_size(EXPERT)
     tok_rows = tokens.shape[0]
     width = tokens.shape[1]
     micro_rows = tok_rows // MICRO
@@ -177,7 +178,7 @@
         kept_joint = lax.dynamic_update_index_in_dim(kept_joint, joint_pre, f_pick, 0)
         kept_pairs = lax.dynamic_update_index_in_dim(kept_pairs, flat_pairs, f_pick, 0)
         if tick_num + 1 < ticks:
-            incoming = from_behind(layer_out, "pipe", 1)
+            incoming = from_behind(layer_out, PIPE, 1)
     incoming = jnp.zeros((micro_rows, width), jnp.bfloat16)
     for tick_num in range(ticks):
         backward_is_valid, backward_slot_pick, backward_start_row = timing(
@@ -229,35 +230,35 @@
         grad_outs = lax.dynamic_update_index_in_dim(grad_outs, grad_bf, b_pick, 0)
         gain_sum = gain_sum + gain_term
         if tick_num + 1 < ticks:
-            incoming = from_behind(grad_bf, "pipe", -1)
-    gain_grad = lax.psum(gain_sum, ("dp", "expert"))
+            incoming = from_behind(grad_bf, PIPE, -1)
+    gain_grad = lax.psum(gain_sum, (DP, EXPERT))
     segment_out = layer_outs[:MICRO].reshape(1, tok_rows, width)
     segment_grad = grad_outs[:MICRO].reshape(1, tok_rows, width)
     return (segment_out, segment_grad, gain_grad.reshape(1, width))
 
 
 def swap_cores(value):
-    count = lax.axis_size("expert")
-    return lax.ppermute(value, "expert", [(e, e ^ 1) for e in range(count)])
+    count = lax.axis_size(EXPERT)
+    return lax.ppermute(value, EXPERT, [(e, e ^ 1) for e in range(count)])
 
 
 def shifted(value, dp_step, chip_step):
-    dps, experts = (lax.axis_size(name) for name in ("dp", "expert"))
+    dps, experts = (lax.axis_size(name) for name in (DP, EXPERT))
     pairs = []
     for dp in range(dps):
         for expert in range(experts):
             target = (dp + dp_step) % dps * experts + (expert + 2 * chip_step) % experts
             pairs.append((dp * experts + expert, target))
-    return lax.ppermute(value, ("dp", "expert"), pairs)
+    return lax.ppermute(value, (DP, EXPERT), pairs)
 
 
 def hopped(value, step):
-    stages = lax.axis_size("pipe")
-    return lax.ppermute(value, "pipe", [(s, (s + step) % stages) for s in range(stages)])
+    stages = lax.axis_size(PIPE)
+    return lax.ppermute(value, PIPE, [(s, (s + step) % stages) for s in range(stages)])
 
 
 def chip_steps():
-    dps, chips = lax.axis_size("dp"), lax.axis_size("expert") // 2
+    dps, chips = lax.axis_size(DP), lax.axis_size(EXPERT) // 2
     steps = [(d, c) for d in range(dps) for c in range(chips)]
     return sorted(steps[1:], key=lambda step: -(step[0] + step[1]))
 
@@ -267,7 +268,7 @@
 
 
 def returned(blocks, which):
-    dps, chips = lax.axis_size("dp"), lax.axis_size("expert") // 2
+    dps, chips = lax.axis_size(DP), lax.axis_size(EXPERT) // 2
     dp, chip = chip_steps()[which - 1]
     return shifted(blocks[which], -dp % dps, -chip % chips)
 
@@ -315,7 +316,7 @@
 
 
 def stage_kernel(out_ref):
-    out_ref[...] = jnp.full(out_ref.shape, lax.axis_index("pipe"), jnp.int32)
+    out_ref[...] = jnp.full(out_ref.shape, lax.axis_index(PIPE), jnp.int32)
 
 
 def first_rows_kernel(token_ref, id_hbm, gate_hbm, out_ref, copied, id_ref, gate_ref, sems):
@@ -325,7 +326,7 @@
     gate_copy = pltpu.make_async_copy(gate_hbm, gate_ref, sems.at[2])
     for each in (id_copy, gate_copy, copy):
         each.start()
-    owners = lax.axis_size("dp") * lax.axis_size("expert")
+    owners = lax.axis_size(DP) * lax.axis_size(EXPERT)
     column = lax.broadcasted_iota(jnp.int32, (rows, out_ref.shape[1] - width), 1)
     table = jnp.zeros(column.shape, jnp.float32)
     id_copy.wait()
@@ -343,7 +344,7 @@
 
 def first_rows(tokens, ids, gates):
     rows, width = tokens.shape[0] // MICRO, tokens.shape[1]
-    owners = lax.axis_size("dp") * lax.axis_size("expert")
+    owners = lax.axis_size(DP) * lax.axis_size(EXPERT)
     extra = -(-MICRO * owners // LANES) * LANES
     outs = [jax.ShapeDtypeStruct((rows, width + extra), tokens.dtype)]
     scratch = [pltpu.VMEM((rows, width), tokens.dtype), pltpu.VMEM(ids.shape, ids.dtype)]
@@ -380,7 +381,7 @@
 
 
 def owner_number():
-    return lax.axis_index("dp") * lax.axis_size("expert") + lax.axis_index("expert")
+    return lax.axis_index(DP) * lax.axis_size(EXPERT) + lax.axis_index(EXPERT)
 
 
 def forward_kernel(blocks, tick, *refs):
@@ -393,11 +394,11 @@
     for k, row_ref in enumerate(row_refs):
         x = row_ref[:, :width].astype(jnp.float32)
         flat_ref[k * rows:(k + 1) * rows, :] = (x * inverse_rms(x) * gain).astype(jnp.bfloat16)
-    micro = tick - lax.axis_index("pipe")
+    micro = tick - lax.axis_index(PIPE)
     is_valid = (micro >= 0) & (micro < MICRO)
     routed = jnp.concatenate([ref[:, width:] for ref in table_refs], axis=0).astype(jnp.float32)
     column = lax.broadcasted_iota(jnp.int32, routed.shape, 1)
-    me, owners = owner_number(), lax.axis_size("dp") * lax.axis_size("expert")
+    me, owners = owner_number(), lax.axis_size(DP) * lax.axis_size(EXPERT)
     for e, owner in enumerate((me, me ^ 1)):
         is_routed = (column == micro * owners + owner) & is_valid
         weight = jnp.sum(jnp.where(is_routed, routed, 0.0), axis=1, keepdims=True)
@@ -429,7 +430,7 @@
     weight_refs, (gain_ref, own_ref, *part_refs, flat, rate, normed, hidden, sems) = refs[:4], refs[4:]
     rows, width = row_refs[0].shape
     ff = weight_refs[2].shape[1]
-    stage = lax.axis_index("pipe")
+    stage = lax.axis_index(PIPE)
 
     def copies(at):
         return (
@@ -517,7 +518,7 @@
 
 def dense_body(tokens, cotangent, owner_ids, gate_weights, norm_gain, w_gate, w_up, w_down):
     f32, bf16 = jnp.float32, jnp.bfloat16
-    stages = lax.axis_size("pipe")
+    stages = lax.axis_size(PIPE)
     tok_rows, width = tokens.shape
     rows = tok_rows // MICRO
     gain = norm_gain[0][None, :]
@@ -608,26 +609,26 @@
 
 
 def body(tokens, cotangent, owner_ids, *rest):
-    owners = lax.axis_size("dp") * lax.axis_size("expert")
-    routed_densely = owners <= 2 * owner_ids.shape[2] and lax.axis_size("expert") % 2 == 0
+    owners = lax.axis_size(DP) * lax.axis_size(EXPERT)
+    routed_densely = owners <= 2 * owner_ids.shape[2] and lax.axis_size(EXPERT) % 2 == 0
     plan = dense_body if routed_densely else slot_body
     return plan(tokens, cotangent, owner_ids, *rest)
 
 
 def solution(mesh):
     in_specs = (
-        P(("dp", "expert"), None),
-        P(("dp", "expert"), None),
-        P("pipe", ("dp", "expert"), None),
-        P("pipe", ("dp", "expert"), None),
-        P("pipe", None),
-        P("pipe", ("dp", "expert"), None, None),
-        P("pipe", ("dp", "expert"), None, None),
-        P("pipe", ("dp", "expert"), None, None),
+        P((DP, EXPERT), None),
+        P((DP, EXPERT), None),
+        P(PIPE, (DP, EXPERT), None),
+        P(PIPE, (DP, EXPERT), None),
+        P(PIPE, None),
+        P(PIPE, (DP, EXPERT), None, None),
+        P(PIPE, (DP, EXPERT), None, None),
+        P(PIPE, (DP, EXPERT), None, None),
     )
     out_specs = (
-        P("pipe", ("dp", "expert"), None),
-        P("pipe", ("dp", "expert"), None),
-        P("pipe", None),
+        P(PIPE, (DP, EXPERT), None),
+        P(PIPE, (DP, EXPERT), None),
+        P(PIPE, None),
     )
     return jax.shard_map(body, mesh=mesh, in_specs=in_specs, out_specs=out_specs, check_vma=False)

time: 279 us -> 279 us (level)
  no operation moved by 1% of the time
where the time goes in v4:
time: 279 us
  starting transfers between devices  124 us (44%)
  waiting for transfers between devices  107 us (38%)
  Pallas kernels  39.8 us (14%)
  other arithmetic  6.65 us (2%)
    ppermute x87, starting transfers between devices, shifted(): return lax.ppermute(value, (DP, EXPERT), pairs)  103 us
    ppermute x87, waiting for transfers between devices, shifted(): return lax.ppermute(value, (DP, EXPERT), pairs)  74.5 us
    pallas_call x22, Pallas kernels, in_vmem(): pl.pallas_call(kernel, out_shape=outs, in_specs=specs or [VMEM] * len(ope...  39.8 us
    ppermute x12, waiting for transfers between devices, hopped(): lax.ppermute(value, PIPE, [(s, (s + step) % stages) for s in range(stages)])  32.5 us
    ppermute x12, starting transfers between devices, hopped(): lax.ppermute(value, PIPE, [(s, (s + step) % stages) for s in range(stages)])  19.7 us
  transfers between devices with their start and end apart: 103, of which 60 were waited for; matrix products, arithmetic and copies ran while one was open for 1% of the time, Pallas kernels for 9%

profile of v4, /device:TPU:0, one launch (start us, length us, event | category | flops | bytes accessed | tf_op | source)
XLA Modules:
  0.0 279.0 jit_solution(11616257970229042017)
XLA Ops:
  2.8 3.6 %collective-permute-start = (bf16[32,2176]{1,0:T(8,128)(2,1)S(1)}, bf16[32,2176]{1,0:T(8,128)(2,1)S(1)}, u32[]{:S(2)}, u32[]{:S(2)}) collective-permute-start(bf16[32,2176]{1,0:T(8,128)(2,1)S(1)} %shard_map.104.refs_0_.refs_4_), channel_id=1, source_target_pairs={{0,18},{1,19},{2,16},{3,17},{16,2},{17,3},{18,0},{19,1},{4,22},{5,... | collective-permute-start | bytes 417800 | tf_op jit(solution)/shard_map/ppermute | solution.py:252
  7.3 2.4 shard_map.105
  10.9 2.7 collective-permute-done.1.refs_2_.refs_6_
  21.5 4.0 %collective-permute-done.7 = bf16[32,2048]{1,0:T(8,128)(2,1)S(1)} collective-permute-done((bf16[32,2048]{1,0:T(8,128)(2,1)S(1)}, bf16[32,2048]{1,0:T(8,128)(2,1)S(1)}, u32[]{:S(2)}, u32[]{:S(2)}) %collective-permute-start.7) | collective-permute-done | bytes 131104 | tf_op jit(solution)/shard_map/ppermute | solution.py:252
  27.3 5.1 %collective-permute-done.9 = bf16[32,2048]{1,0:T(8,128)(2,1)S(1)} collective-permute-done((bf16[32,2048]{1,0:T(8,128)(2,1)S(1)}, bf16[32,2048]{1,0:T(8,128)(2,1)S(1)}, u32[]{:S(2)}, u32[]{:S(2)}) %collective-permute-start.9) | collective-permute-done | bytes 131104 | tf_op jit(solution)/shard_map/ppermute | solution.py:257
  36.0 2.5 collective-permute-done.10.refs_1_
  50.0 6.8 %collective-permute-done.16 = bf16[32,2048]{1,0:T(8,128)(2,1)S(1)} collective-permute-done((bf16[32,2048]{1,0:T(8,128)(2,1)S(1)}, bf16[32,2048]{1,0:T(8,128)(2,1)S(1)}, u32[]{:S(2)}, u32[]{:S(2)}) %collective-permute-start.16) | collective-permute-done | bytes 131104 | tf_op jit(solution)/shard_map/ppermute | solution.py:257
  60.4 3.1 %collective-permute-done.17.refs_1_ = bf16[32,2048]{1,0:T(8,128)(2,1)S(1)} collective-permute-done((bf16[32,2048]{1,0:T(8,128)(2,1)S(1)}, bf16[32,2048]{1,0:T(8,128)(2,1)S(1)}, u32[]{:S(2)}, u32[]{:S(2)}) %collective-permute-start.17) | collective-permute-done | bytes 131104 | tf_op jit(solution)/shard_map/ppermute | solution.py:252
  63.5 2.4 collective-permute-done.18.refs_2_
  76.4 6.8 %collective-permute-done.23 = bf16[32,2048]{1,0:T(8,128)(2,1)S(1)} collective-permute-done((bf16[32,2048]{1,0:T(8,128)(2,1)S(1)}, bf16[32,2048]{1,0:T(8,128)(2,1)S(1)}, u32[]{:S(2)}, u32[]{:S(2)}) %collective-permute-start.23) | collective-permute-done | bytes 131104 | tf_op jit(solution)/shard_map/ppermute | solution.py:257
  100.2 2.6 shard_map.118
  106.5 2.7 collective-permute-done.53
  127.3 2.4 shard_map.119
  134.4 2.8 collective-permute-start.37
  137.2 2.3 collective-permute-done.58
  144.9 2.8 collective-permute-done.61
  158.1 2.4 shard_map.120
  166.7 3.1 %collective-permute-done.65 = bf16[32,2048]{1,0:T(8,128)(2,1)S(1)} collective-permute-done((bf16[32,2048]{1,0:T(8,128)(2,1)S(1)}, bf16[32,2048]{1,0:T(8,128)(2,1)S(1)}, u32[]{:S(2)}, u32[]{:S(2)}) %collective-permute-start.65) | collective-permute-done | bytes 131104 | tf_op jit(solution)/shard_map/ppermute | solution.py:252
  184.6 2.4 shard_map.121
  192.8 3.1 %collective-permute-done.73 = bf16[32,2048]{1,0:T(8,128)(2,1)S(1)} collective-permute-done((bf16[32,2048]{1,0:T(8,128)(2,1)S(1)}, bf16[32,2048]{1,0:T(8,128)(2,1)S(1)}, u32[]{:S(2)}, u32[]{:S(2)}) %collective-permute-start.73) | collective-permute-done | bytes 131104 | tf_op jit(solution)/shard_map/ppermute | solution.py:252
  196.4 4.0 %collective-permute-start.76 = (bf16[32,2048]{1,0:T(8,128)(2,1)S(1)}, bf16[32,2048]{1,0:T(8,128)(2,1)S(1)}, u32[]{:S(2)}, u32[]{:S(2)}) collective-permute-start(bf16[32,2048]{1,0:T(8,128)(2,1)S(1)} %fusion.26), channel_id=1, source_target_pairs={{0,12},{4,0},{8,4},{12,8},{1,13},{5,1},{9,5},{13,9},{2,14},{6,2},{... | collective-permute-start | bytes 393224 | tf_op jit(solution)/shard_map/ppermute | solution.py:257
  200.4 2.5 collective-permute-done.76.refs_0_
  206.4 2.5 collective-permute-done.77.refs_1_
  210.3 2.4 shard_map.122
  221.2 4.2 %collective-permute-start.84 = (bf16[32,2048]{1,0:T(8,128)(2,1)S(1)}, bf16[32,2048]{1,0:T(8,128)(2,1)S(1)}, u32[]{:S(2)}, u32[]{:S(2)}) collective-permute-start(bf16[32,2048]{1,0:T(8,128)(2,1)S(1)} %fusion.33), channel_id=1, source_target_pairs={{0,12},{4,0},{8,4},{12,8},{1,13},{5,1},{9,5},{13,9},{2,14},{6,2},{... | collective-permute-start | bytes 393224 | tf_op jit(solution)/shard_map/ppermute | solution.py:257
  225.4 2.5 collective-permute-done.84.refs_0_
  231.4 2.5 collective-permute-done.85.refs_1_
  235.6 2.4 shard_map.123
  246.3 4.3 %collective-permute-start.92 = (bf16[32,2048]{1,0:T(8,128)(2,1)S(1)}, bf16[32,2048]{1,0:T(8,128)(2,1)S(1)}, u32[]{:S(2)}, u32[]{:S(2)}) collective-permute-start(bf16[32,2048]{1,0:T(8,128)(2,1)S(1)} %fusion.40), channel_id=1, source_target_pairs={{0,12},{4,0},{8,4},{12,8},{1,13},{5,1},{9,5},{13,9},{2,14},{6,2},{... | collective-permute-start | bytes 393224 | tf_op jit(solution)/shard_map/ppermute | solution.py:257
  250.6 2.5 collective-permute-done.92.refs_0_
  260.4 2.6 shard_map.124
  274.6 2.9 %collective-permute-done.97 = bf16[32,2048]{1,0:T(8,128)(2,1)S(1)} collective-permute-done((bf16[32,2048]{1,0:T(8,128)(2,1)S(1)}, bf16[32,2048]{1,0:T(8,128)(2,1)S(1)}, u32[]{:S(2)}, u32[]{:S(2)}) %collective-permute-start.97) | collective-permute-done | bytes 131104 | tf_op jit(solution)/shard_map/ppermute | solution.py:252
  (249 shorter events, 176.9 us)
Async XLA Ops:
  1.2 8.5 %collective-permute-start.4 = (bf16[2048,384]{1,0:T(8,128)(2,1)}, bf16[2048,384]{1,0:T(8,128)(2,1)S(1)}, u32[]{:S(2)}, u32[]{:S(2)}) collective-permute-start(bf16[2048,384]{1,0:T(8,128)(2,1)} %bitcast.30), channel_id=1, source_target_pairs={{0,1},{1,0},{2,3},{3,2},{4,5},{5,4},{6,7},{7,6},{8,9},{9,8},{10,11... | collective-permute-start | bytes 4718600 | tf_op jit(solution)/shard_map/ppermute | solution.py:242
  1.3 8.4 %collective-permute-start.5 = (bf16[384,2048]{1,0:T(8,128)(2,1)}, bf16[384,2048]{1,0:T(8,128)(2,1)S(1)}, u32[]{:S(2)}, u32[]{:S(2)}) collective-permute-start(bf16[384,2048]{1,0:T(8,128)(2,1)} %bitcast.32), channel_id=1, source_target_pairs={{0,1},{1,0},{2,3},{3,2},{4,5},{5,4},{6,7},{7,6},{8,9},{9,8},{10,11... | collective-permute-start | bytes 4718600 | tf_op jit(solution)/shard_map/ppermute | solution.py:242
  2.8 8.1 %collective-permute-start = (bf16[32,2176]{1,0:T(8,128)(2,1)S(1)}, bf16[32,2176]{1,0:T(8,128)(2,1)S(1)}, u32[]{:S(2)}, u32[]{:S(2)}) collective-permute-start(bf16[32,2176]{1,0:T(8,128)(2,1)S(1)} %shard_map.104.refs_0_.refs_4_), channel_id=1, source_target_pairs={{0,18},{1,19},{2,16},{3,17},{16,2},{17,3},{18,0},{19,1},{4,22},{5,... | collective-permute-start | bytes 417800 | tf_op jit(solution)/shard_map/ppermute | solution.py:252
  17.7 7.9 %collective-permute-start.7 = (bf16[32,2048]{1,0:T(8,128)(2,1)S(1)}, bf16[32,2048]{1,0:T(8,128)(2,1)S(1)}, u32[]{:S(2)}, u32[]{:S(2)}) collective-permute-start(bf16[32,2048]{1,0:T(8,128)(2,1)S(1)} %get-tuple-element.94), channel_id=1, source_target_pairs={{0,2},{1,3},{2,0},{3,1},{16,18},{17,19},{18,16},{19,17},{4,6},{5,7... | collective-permute-start | bytes 393224 | tf_op jit(solution)/shard_map/ppermute | solution.py:252
  58.3 7.5 %collective-permute-start.18 = (bf16[32,2048]{1,0:T(8,128)(2,1)S(1)}, bf16[32,2048]{1,0:T(8,128)(2,1)S(1)}, u32[]{:S(2)}, u32[]{:S(2)}) collective-permute-start(bf16[32,2048]{1,0:T(8,128)(2,1)S(1)} %slice_select_fusion.4.refs_0_), channel_id=1, source_target_pairs={{0,2},{1,3},{2,0},{3,1},{16,18},{17,19},{18,16},{19,17},{4,6},{5,7... | collective-permute-start | bytes 393224 | tf_op jit(solution)/shard_map/ppermute | solution.py:252
  86.7 8.4 %collective-permute-start.48 = (bf16[32,2048]{1,0:T(8,128)(2,1)S(1)}, bf16[32,2048]{1,0:T(8,128)(2,1)S(1)}, u32[]{:S(2)}, u32[]{:S(2)}) collective-permute-start(bf16[32,2048]{1,0:T(8,128)(2,1)S(1)} %slice.31.refs_0_), channel_id=1, source_target_pairs={{0,18},{1,19},{2,16},{3,17},{16,2},{17,3},{18,0},{19,1},{4,22},{5,... | collective-permute-start | bytes 393224 | tf_op jit(solution)/shard_map/ppermute | solution.py:252
  88.1 12.1 %collective-permute-start.49 = (bf16[32,2048]{1,0:T(8,128)(2,1)S(1)}, bf16[32,2048]{1,0:T(8,128)(2,1)S(1)}, u32[]{:S(2)}, u32[]{:S(2)}) collective-permute-start(bf16[32,2048]{1,0:T(8,128)(2,1)S(1)} %slice.31.refs_0_), channel_id=1, source_target_pairs={{0,2},{1,3},{2,0},{3,1},{16,18},{17,19},{18,16},{19,17},{4,6},{5,7... | collective-permute-start | bytes 393224 | tf_op jit(solution)/shard_map/ppermute | solution.py:252
  89.3 10.9 %collective-permute-start.50 = (bf16[32,2048]{1,0:T(8,128)(2,1)S(1)}, bf16[32,2048]{1,0:T(8,128)(2,1)S(1)}, u32[]{:S(2)}, u32[]{:S(2)}) collective-permute-start(bf16[32,2048]{1,0:T(8,128)(2,1)S(1)} %slice.31.refs_0_), channel_id=1, source_target_pairs={{0,16},{1,17},{2,18},{3,19},{16,0},{17,1},{18,2},{19,3},{4,20},{5,... | collective-permute-start | bytes 393224 | tf_op jit(solution)/shard_map/ppermute | solution.py:252
  92.9 12.1 %collective-permute-start.29 = (bf16[32,2048]{1,0:T(8,128)(2,1)S(1)}, bf16[32,2048]{1,0:T(8,128)(2,1)S(1)}, u32[]{:S(2)}, u32[]{:S(2)}) collective-permute-start(bf16[32,2048]{1,0:T(8,128)(2,1)S(1)} %get-tuple-element.107), channel_id=1, source_target_pairs={{0,16},{1,17},{2,18},{3,19},{16,0},{17,1},{18,2},{19,3},{4,20},{5,... | collective-permute-start | bytes 393224 | tf_op jit(solution)/shard_map/ppermute | solution.py:252
  93.9 12.5 %collective-permute-start.28 = (bf16[32,2048]{1,0:T(8,128)(2,1)S(1)}, bf16[32,2048]{1,0:T(8,128)(2,1)S(1)}, u32[]{:S(2)}, u32[]{:S(2)}) collective-permute-start(bf16[32,2048]{1,0:T(8,128)(2,1)S(1)} %get-tuple-element.106), channel_id=1, source_target_pairs={{0,2},{1,3},{2,0},{3,1},{16,18},{17,19},{18,16},{19,17},{4,6},{5,7... | collective-permute-start | bytes 393224 | tf_op jit(solution)/shard_map/ppermute | solution.py:252
  95.1 11.3 %collective-permute-start.27 = (bf16[32,2048]{1,0:T(8,128)(2,1)S(1)}, bf16[32,2048]{1,0:T(8,128)(2,1)S(1)}, u32[]{:S(2)}, u32[]{:S(2)}) collective-permute-start(bf16[32,2048]{1,0:T(8,128)(2,1)S(1)} %get-tuple-element.105), channel_id=1, source_target_pairs={{0,18},{1,19},{2,16},{3,17},{16,2},{17,3},{18,0},{19,1},{4,22},{5,... | collective-permute-start | bytes 393224 | tf_op jit(solution)/shard_map/ppermute | solution.py:252
  105.0 7.4 %collective-permute-start.51 = (bf16[32,2048]{1,0:T(8,128)(2,1)S(1)}, bf16[32,2048]{1,0:T(8,128)(2,1)S(1)}, u32[]{:S(2)}, u32[]{:S(2)}) collective-permute-start(bf16[32,2048]{1,0:T(8,128)(2,1)S(1)} %get-tuple-element.128), channel_id=1, source_target_pairs={{0,18},{1,19},{2,16},{3,17},{16,2},{17,3},{18,0},{19,1},{4,22},{5,... | collective-permute-start | bytes 393224 | tf_op jit(solution)/shard_map/ppermute | solution.py:252
  117.9 8.1 %collective-permute-start.55 = (bf16[32,2048]{1,0:T(8,128)(2,1)S(1)}, bf16[32,2048]{1,0:T(8,128)(2,1)S(1)}, u32[]{:S(2)}, u32[]{:S(2)}) collective-permute-start(bf16[32,2048]{1,0:T(8,128)(2,1)S(1)} %slice_select_fusion.refs_0_), channel_id=1, source_target_pairs={{0,18},{1,19},{2,16},{3,17},{16,2},{17,3},{18,0},{19,1},{4,22},{5,... | collective-permute-start | bytes 393224 | tf_op jit(solution)/shard_map/ppermute | solution.py:252
  119.5 7.8 %collective-permute-start.56 = (bf16[32,2048]{1,0:T(8,128)(2,1)S(1)}, bf16[32,2048]{1,0:T(8,128)(2,1)S(1)}, u32[]{:S(2)}, u32[]{:S(2)}) collective-permute-start(bf16[32,2048]{1,0:T(8,128)(2,1)S(1)} %slice_select_fusion.refs_0_), channel_id=1, source_target_pairs={{0,2},{1,3},{2,0},{3,1},{16,18},{17,19},{18,16},{19,17},{4,6},{5,7... | collective-permute-start | bytes 393224 | tf_op jit(solution)/shard_map/ppermute | solution.py:252
  123.8 8.2 %collective-permute-start.36 = (bf16[32,2048]{1,0:T(8,128)(2,1)S(1)}, bf16[32,2048]{1,0:T(8,128)(2,1)S(1)}, u32[]{:S(2)}, u32[]{:S(2)}) collective-permute-start(bf16[32,2048]{1,0:T(8,128)(2,1)S(1)} %get-tuple-element.111), channel_id=1, source_target_pairs={{0,16},{1,17},{2,18},{3,19},{16,0},{17,1},{18,2},{19,3},{4,20},{5,... | collective-permute-start | bytes 393224 | tf_op jit(solution)/shard_map/ppermute | solution.py:252
  125.2 9.2 %collective-permute-start.35 = (bf16[32,2048]{1,0:T(8,128)(2,1)S(1)}, bf16[32,2048]{1,0:T(8,128)(2,1)S(1)}, u32[]{:S(2)}, u32[]{:S(2)}) collective-permute-start(bf16[32,2048]{1,0:T(8,128)(2,1)S(1)} %get-tuple-element.110), channel_id=1, source_target_pairs={{0,2},{1,3},{2,0},{3,1},{16,18},{17,19},{18,16},{19,17},{4,6},{5,7... | collective-permute-start | bytes 393224 | tf_op jit(solution)/shard_map/ppermute | solution.py:252
  126.1 8.3 %collective-permute-start.34 = (bf16[32,2048]{1,0:T(8,128)(2,1)S(1)}, bf16[32,2048]{1,0:T(8,128)(2,1)S(1)}, u32[]{:S(2)}, u32[]{:S(2)}) collective-permute-start(bf16[32,2048]{1,0:T(8,128)(2,1)S(1)} %get-tuple-element.109), channel_id=1, source_target_pairs={{0,18},{1,19},{2,16},{3,17},{16,2},{17,3},{18,0},{19,1},{4,22},{5,... | collective-permute-start | bytes 393224 | tf_op jit(solution)/shard_map/ppermute | solution.py:252
  129.7 7.5 %collective-permute-start.60 = (bf16[32,2048]{1,0:T(8,128)(2,1)S(1)}, bf16[32,2048]{1,0:T(8,128)(2,1)S(1)}, u32[]{:S(2)}, u32[]{:S(2)}) collective-permute-start(bf16[32,2048]{1,0:T(8,128)(2,1)S(1)} %get-tuple-element.138), channel_id=1, source_target_pairs={{0,16},{1,17},{2,18},{3,19},{16,0},{17,1},{18,2},{19,3},{4,20},{5,... | collective-permute-start | bytes 393224 | tf_op jit(solution)/shard_map/ppermute | solution.py:252
  132.0 7.5 %collective-permute-start.58 = (bf16[32,2048]{1,0:T(8,128)(2,1)S(1)}, bf16[32,2048]{1,0:T(8,128)(2,1)S(1)}, u32[]{:S(2)}, u32[]{:S(2)}) collective-permute-start(bf16[32,2048]{1,0:T(8,128)(2,1)S(1)} %get-tuple-element.136), channel_id=1, source_target_pairs={{0,18},{1,19},{2,16},{3,17},{16,2},{17,3},{18,0},{19,1},{4,22},{5,... | collective-permute-start | bytes 393224 | tf_op jit(solution)/shard_map/ppermute | solution.py:252
  139.9 7.8 %collective-permute-start.61 = (bf16[32,2048]{1,0:T(8,128)(2,1)S(1)}, bf16[32,2048]{1,0:T(8,128)(2,1)S(1)}, u32[]{:S(2)}, u32[]{:S(2)}) collective-permute-start(bf16[32,2048]{1,0:T(8,128)(2,1)S(1)} %fusion.12), channel_id=1, source_target_pairs={{0,12},{4,0},{8,4},{12,8},{1,13},{5,1},{9,5},{13,9},{2,14},{6,2},{... | collective-permute-start | bytes 393224 | tf_op jit(solution)/shard_map/ppermute | solution.py:257
  141.4 8.7 %collective-permute-start.38 = (bf16[32,2048]{1,0:T(8,128)(2,1)S(1)}, bf16[32,2048]{1,0:T(8,128)(2,1)S(1)}, u32[]{:S(2)}, u32[]{:S(2)}) collective-permute-start(bf16[32,2048]{1,0:T(8,128)(2,1)S(1)} %collective-permute-done.37.refs_0_), channel_id=1, source_target_pairs={{0,18},{1,19},{2,16},{3,17},{16,2},{17,3},{18,0},{19,1},{4,22},{5,... | collective-permute-start | bytes 393224 | tf_op jit(solution)/shard_map/ppermute | solution.py:252
  142.8 8.5 %collective-permute-start.39 = (bf16[32,2048]{1,0:T(8,128)(2,1)S(1)}, bf16[32,2048]{1,0:T(8,128)(2,1)S(1)}, u32[]{:S(2)}, u32[]{:S(2)}) collective-permute-start(bf16[32,2048]{1,0:T(8,128)(2,1)S(1)} %collective-permute-done.37.refs_0_), channel_id=1, source_target_pairs={{0,2},{1,3},{2,0},{3,1},{16,18},{17,19},{18,16},{19,17},{4,6},{5,7... | collective-permute-start | bytes 393224 | tf_op jit(solution)/shard_map/ppermute | solution.py:252
  143.8 7.5 %collective-permute-start.40 = (bf16[32,2048]{1,0:T(8,128)(2,1)S(1)}, bf16[32,2048]{1,0:T(8,128)(2,1)S(1)}, u32[]{:S(2)}, u32[]{:S(2)}) collective-permute-start(bf16[32,2048]{1,0:T(8,128)(2,1)S(1)} %collective-permute-done.37.refs_0_), channel_id=1, source_target_pairs={{0,16},{1,17},{2,18},{3,19},{16,0},{17,1},{18,2},{19,3},{4,20},{5,... | collective-permute-start | bytes 393224 | tf_op jit(solution)/shard_map/ppermute | solution.py:252
  147.7 7.7 %collective-permute-start.62 = (bf16[32,2048]{1,0:T(8,128)(2,1)S(1)}, bf16[32,2048]{1,0:T(8,128)(2,1)S(1)}, u32[]{:S(2)}, u32[]{:S(2)}) collective-permute-start(bf16[32,2048]{1,0:T(8,128)(2,1)S(1)} %slice_select_fusion.1.refs_0_), channel_id=1, source_target_pairs={{0,18},{1,19},{2,16},{3,17},{16,2},{17,3},{18,0},{19,1},{4,22},{5,... | collective-permute-start | bytes 393224 | tf_op jit(solution)/shard_map/ppermute | solution.py:252
  149.2 9.0 %collective-permute-start.63 = (bf16[32,2048]{1,0:T(8,128)(2,1)S(1)}, bf16[32,2048]{1,0:T(8,128)(2,1)S(1)}, u32[]{:S(2)}, u32[]{:S(2)}) collective-permute-start(bf16[32,2048]{1,0:T(8,128)(2,1)S(1)} %slice_select_fusion.1.refs_0_), channel_id=1, source_target_pairs={{0,2},{1,3},{2,0},{3,1},{16,18},{17,19},{18,16},{19,17},{4,6},{5,7... | collective-permute-start | bytes 393224 | tf_op jit(solution)/shard_map/ppermute | solution.py:252
  150.1 8.0 %collective-permute-start.64 = (bf16[32,2048]{1,0:T(8,128)(2,1)S(1)}, bf16[32,2048]{1,0:T(8,128)(2,1)S(1)}, u32[]{:S(2)}, u32[]{:S(2)}) collective-permute-start(bf16[32,2048]{1,0:T(8,128)(2,1)S(1)} %slice_select_fusion.1.refs_0_), channel_id=1, source_target_pairs={{0,16},{1,17},{2,18},{3,19},{16,0},{17,1},{18,2},{19,3},{4,20},{5,... | collective-permute-start | bytes 393224 | tf_op jit(solution)/shard_map/ppermute | solution.py:252
  153.5 9.1 %collective-permute-start.43 = (bf16[32,2048]{1,0:T(8,128)(2,1)S(1)}, bf16[32,2048]{1,0:T(8,128)(2,1)S(1)}, u32[]{:S(2)}, u32[]{:S(2)}) collective-permute-start(bf16[32,2048]{1,0:T(8,128)(2,1)S(1)} %get-tuple-element.115), channel_id=1, source_target_pairs={{0,16},{1,17},{2,18},{3,19},{16,0},{17,1},{18,2},{19,3},{4,20},{5,... | collective-permute-start | bytes 393224 | tf_op jit(solution)/shard_map/ppermute | solution.py:252
  154.4 9.7 %collective-permute-start.42 = (bf16[32,2048]{1,0:T(8,128)(2,1)S(1)}, bf16[32,2048]{1,0:T(8,128)(2,1)S(1)}, u32[]{:S(2)}, u32[]{:S(2)}) collective-permute-start(bf16[32,2048]{1,0:T(8,128)(2,1)S(1)} %get-tuple-element.114), channel_id=1, source_target_pairs={{0,2},{1,3},{2,0},{3,1},{16,18},{17,19},{18,16},{19,17},{4,6},{5,7... | collective-permute-start | bytes 393224 | tf_op jit(solution)/shard_map/ppermute | solution.py:252
  155.5 8.6 %collective-permute-start.41 = (bf16[32,2048]{1,0:T(8,128)(2,1)S(1)}, bf16[32,2048]{1,0:T(8,128)(2,1)S(1)}, u32[]{:S(2)}, u32[]{:S(2)}) collective-permute-start(bf16[32,2048]{1,0:T(8,128)(2,1)S(1)} %get-tuple-element.113), channel_id=1, source_target_pairs={{0,18},{1,19},{2,16},{3,17},{16,2},{17,3},{18,0},{19,1},{4,22},{5,... | collective-permute-start | bytes 393224 | tf_op jit(solution)/shard_map/ppermute | solution.py:252
  171.0 8.2 %collective-permute-start.45 = (bf16[32,2048]{1,0:T(8,128)(2,1)S(1)}, bf16[32,2048]{1,0:T(8,128)(2,1)S(1)}, u32[]{:S(2)}, u32[]{:S(2)}) collective-permute-start(bf16[32,2048]{1,0:T(8,128)(2,1)S(1)} %collective-permute-done.44.refs_0_), channel_id=1, source_target_pairs={{0,18},{1,19},{2,16},{3,17},{16,2},{17,3},{18,0},{19,1},{4,22},{5,... | collective-permute-start | bytes 393224 | tf_op jit(solution)/shard_map/ppermute | solution.py:252
  188.4 7.5 %collective-permute-start.73 = (bf16[32,2048]{1,0:T(8,128)(2,1)S(1)}, bf16[32,2048]{1,0:T(8,128)(2,1)S(1)}, u32[]{:S(2)}, u32[]{:S(2)}) collective-permute-start(bf16[32,2048]{1,0:T(8,128)(2,1)S(1)} %get-tuple-element.149), channel_id=1, source_target_pairs={{0,2},{1,3},{2,0},{3,1},{16,18},{17,19},{18,16},{19,17},{4,6},{5,7... | collective-permute-start | bytes 393224 | tf_op jit(solution)/shard_map/ppermute | solution.py:252
  269.9 7.6 %collective-permute-start.97 = (bf16[32,2048]{1,0:T(8,128)(2,1)S(1)}, bf16[32,2048]{1,0:T(8,128)(2,1)S(1)}, u32[]{:S(2)}, u32[]{:S(2)}) collective-permute-start(bf16[32,2048]{1,0:T(8,128)(2,1)S(1)} %get-tuple-element.164), channel_id=1, source_target_pairs={{0,2},{1,3},{2,0},{3,1},{16,18},{17,19},{18,16},{19,17},{4,6},{5,7... | collective-permute-start | bytes 393224 | tf_op jit(solution)/shard_map/ppermute | solution.py:252
  (74 other events, 479.6 us)

commit v5 on v4

--- a/solution.py
+++ b/solution.py
@@ -602,9 +602,9 @@
     outs.append(sum(part.astype(f32) for part in kept).astype(bf16))
     gain_grad = summed_over_owners(gain_sum) / gain
     segment_out = jnp.concatenate([choose([outs[m + s] for s in range(stages)]) for m in range(MICRO)])
-    segment_grad = jnp.concatenate(
-        [choose([grads[m + stages - 1 - s] for s in range(stages)]) for m in range(MICRO)]
-    )
+    grad_parts = [choose([grads[m + stages - 1 - s] for s in range(stages)]) for m in range(MICRO)]
+    settled = lax.optimization_barrier(jnp.concatenate([*grad_parts[:-1], jnp.zeros_like(grad_parts[-1])]))
+    segment_grad = lax.dynamic_update_slice_in_dim(settled, grad_parts[-1], tok_rows - rows, 0)
     return (segment_out[None], segment_grad[None], gain_grad)
 
 

time: 279 us -> 282 us (1.011)
  waiting for transfers between devices: 107 us -> 110 us
    ppermute x87, waiting for transfers between devices: 74.5 us -> 80.8 us  [shifted(): return lax.ppermute(value, (DP, EXPERT), pairs)]
    ppermute x12, waiting for transfers between devices: 32.5 us -> 28.5 us  [hopped(): lax.ppermute(value, PIPE, [(s, (s + step) % stages) for s in range(stages)])]
  transfers between devices with their start and end apart: 103 -> 103, of which waited for: 60 -> 62; matrix products, arithmetic and copies ran while one was open for 1% -> 1% of each run, Pallas kernels for 9% -> 8%
where the time goes in v5:
time: 282 us
  starting transfers between devices  124 us (44%)
  waiting for transfers between devices  110 us (39%)
  Pallas kernels  39.7 us (14%)
  other arithmetic  6 us (2%)
    ppermute x87, starting transfers between devices, shifted(): return lax.ppermute(value, (DP, EXPERT), pairs)  104 us
    ppermute x87, waiting for transfers between devices, shifted(): return lax.ppermute(value, (DP, EXPERT), pairs)  80.8 us
    pallas_call x22, Pallas kernels, in_vmem(): pl.pallas_call(kernel, out_shape=outs, in_specs=specs or [VMEM] * len(ope...  39.7 us
    ppermute x12, waiting for transfers between devices, hopped(): lax.ppermute(value, PIPE, [(s, (s + step) % stages) for s in range(stages)])  28.5 us
    ppermute x12, starting transfers between devices, hopped(): lax.ppermute(value, PIPE, [(s, (s + step) % stages) for s in range(stages)])  19.1 us
  transfers between devices with their start and end apart: 103, of which 62 were waited for; matrix products, arithmetic and copies ran while one was open for 1% of the time, Pallas kernels for 8%

profile of v5, /device:TPU:0, one launch (start us, length us, event | category | flops | bytes accessed | tf_op | source)
XLA Modules:
  0.0 282.2 jit_solution(14531398121906710272)
XLA Ops:
  2.8 3.6 %collective-permute-start = (bf16[32,2176]{1,0:T(8,128)(2,1)S(1)}, bf16[32,2176]{1,0:T(8,128)(2,1)S(1)}, u32[]{:S(2)}, u32[]{:S(2)}) collective-permute-start(bf16[32,2176]{1,0:T(8,128)(2,1)S(1)} %shard_map.104.refs_0_.refs_4_), channel_id=1, source_target_pairs={{0,18},{1,19},{2,16},{3,17},{16,2},{17,3},{18,0},{19,1},{4,22},{5,... | collective-permute-start | bytes 417800 | tf_op jit(solution)/shard_map/ppermute | solution.py:252
  7.3 2.4 shard_map.105
  10.9 2.7 collective-permute-done.1.refs_2_.refs_6_
  19.6 3.8 %collective-permute-done.6 = bf16[32,2048]{1,0:T(8,128)(2,1)S(1)} collective-permute-done((bf16[32,2048]{1,0:T(8,128)(2,1)S(1)}, bf16[32,2048]{1,0:T(8,128)(2,1)S(1)}, u32[]{:S(2)}, u32[]{:S(2)}) %collective-permute-start.6) | collective-permute-done | bytes 131104 | tf_op jit(solution)/shard_map/ppermute | solution.py:252
  27.1 5.5 %collective-permute-done.9 = bf16[32,2048]{1,0:T(8,128)(2,1)S(1)} collective-permute-done((bf16[32,2048]{1,0:T(8,128)(2,1)S(1)}, bf16[32,2048]{1,0:T(8,128)(2,1)S(1)}, u32[]{:S(2)}, u32[]{:S(2)}) %collective-permute-start.9) | collective-permute-done | bytes 131104 | tf_op jit(solution)/shard_map/ppermute | solution.py:257
  36.2 3.4 %collective-permute-done.10.refs_1_ = bf16[32,2048]{1,0:T(8,128)(2,1)S(1)} collective-permute-done((bf16[32,2048]{1,0:T(8,128)(2,1)S(1)}, bf16[32,2048]{1,0:T(8,128)(2,1)S(1)}, u32[]{:S(2)}, u32[]{:S(2)}) %collective-permute-start.10) | collective-permute-done | bytes 131104 | tf_op jit(solution)/shard_map/ppermute | solution.py:252
  46.8 3.7 %collective-permute-done.13 = bf16[32,2048]{1,0:T(8,128)(2,1)S(1)} collective-permute-done((bf16[32,2048]{1,0:T(8,128)(2,1)S(1)}, bf16[32,2048]{1,0:T(8,128)(2,1)S(1)}, u32[]{:S(2)}, u32[]{:S(2)}) %collective-permute-start.13) | collective-permute-done | bytes 131104 | tf_op jit(solution)/shard_map/ppermute | solution.py:252
  52.0 6.8 %collective-permute-done.16 = bf16[32,2048]{1,0:T(8,128)(2,1)S(1)} collective-permute-done((bf16[32,2048]{1,0:T(8,128)(2,1)S(1)}, bf16[32,2048]{1,0:T(8,128)(2,1)S(1)}, u32[]{:S(2)}, u32[]{:S(2)}) %collective-permute-start.16) | collective-permute-done | bytes 131104 | tf_op jit(solution)/shard_map/ppermute | solution.py:257
  62.4 3.2 %collective-permute-done.17.refs_1_ = bf16[32,2048]{1,0:T(8,128)(2,1)S(1)} collective-permute-done((bf16[32,2048]{1,0:T(8,128)(2,1)S(1)}, bf16[32,2048]{1,0:T(8,128)(2,1)S(1)}, u32[]{:S(2)}, u32[]{:S(2)}) %collective-permute-start.17) | collective-permute-done | bytes 131104 | tf_op jit(solution)/shard_map/ppermute | solution.py:252
  72.9 3.3 %collective-permute-done.20 = bf16[32,2048]{1,0:T(8,128)(2,1)S(1)} collective-permute-done((bf16[32,2048]{1,0:T(8,128)(2,1)S(1)}, bf16[32,2048]{1,0:T(8,128)(2,1)S(1)}, u32[]{:S(2)}, u32[]{:S(2)}) %collective-permute-start.20) | collective-permute-done | bytes 131104 | tf_op jit(solution)/shard_map/ppermute | solution.py:252
  77.9 6.8 %collective-permute-done.23 = bf16[32,2048]{1,0:T(8,128)(2,1)S(1)} collective-permute-done((bf16[32,2048]{1,0:T(8,128)(2,1)S(1)}, bf16[32,2048]{1,0:T(8,128)(2,1)S(1)}, u32[]{:S(2)}, u32[]{:S(2)}) %collective-permute-start.23) | collective-permute-done | bytes 131104 | tf_op jit(solution)/shard_map/ppermute | solution.py:257
  104.8 2.6 shard_map.118
  113.4 3.3 %collective-permute-done.52 = bf16[32,2048]{1,0:T(8,128)(2,1)S(1)} collective-permute-done((bf16[32,2048]{1,0:T(8,128)(2,1)S(1)}, bf16[32,2048]{1,0:T(8,128)(2,1)S(1)}, u32[]{:S(2)}, u32[]{:S(2)}) %collective-permute-start.52) | collective-permute-done | bytes 131104 | tf_op jit(solution)/shard_map/ppermute | solution.py:252
  125.9 2.7 collective-permute-done.32.refs_2_
  141.6 2.5 collective-permute-done.58
  144.1 2.9 %collective-permute-done.59 = bf16[32,2048]{1,0:T(8,128)(2,1)S(1)} collective-permute-done((bf16[32,2048]{1,0:T(8,128)(2,1)S(1)}, bf16[32,2048]{1,0:T(8,128)(2,1)S(1)}, u32[]{:S(2)}, u32[]{:S(2)}) %collective-permute-start.59) | collective-permute-done | bytes 131104 | tf_op jit(solution)/shard_map/ppermute | solution.py:252
  163.9 2.4 shard_map.120
  188.7 2.4 shard_map.121
  194.6 2.5 collective-permute-done.72
  199.1 3.2 %collective-permute-start.76 = (bf16[32,2048]{1,0:T(8,128)(2,1)S(1)}, bf16[32,2048]{1,0:T(8,128)(2,1)S(1)}, u32[]{:S(2)}, u32[]{:S(2)}) collective-permute-start(bf16[32,2048]{1,0:T(8,128)(2,1)S(1)} %fusion.26), channel_id=1, source_target_pairs={{0,12},{4,0},{8,4},{12,8},{1,13},{5,1},{9,5},{13,9},{2,14},{6,2},{... | collective-permute-start | bytes 393224 | tf_op jit(solution)/shard_map/ppermute | solution.py:257
  202.3 2.5 collective-permute-done.76.refs_0_
  208.3 2.5 collective-permute-done.77.refs_1_
  212.1 2.4 shard_map.122
  218.0 2.5 collective-permute-done.80
  222.6 4.3 %collective-permute-start.84 = (bf16[32,2048]{1,0:T(8,128)(2,1)S(1)}, bf16[32,2048]{1,0:T(8,128)(2,1)S(1)}, u32[]{:S(2)}, u32[]{:S(2)}) collective-permute-start(bf16[32,2048]{1,0:T(8,128)(2,1)S(1)} %fusion.33), channel_id=1, source_target_pairs={{0,12},{4,0},{8,4},{12,8},{1,13},{5,1},{9,5},{13,9},{2,14},{6,2},{... | collective-permute-start | bytes 393224 | tf_op jit(solution)/shard_map/ppermute | solution.py:257
  226.9 2.5 collective-permute-done.84.refs_0_
  232.9 3.6 %collective-permute-done.85.refs_1_ = bf16[32,2048]{1,0:T(8,128)(2,1)S(1)} collective-permute-done((bf16[32,2048]{1,0:T(8,128)(2,1)S(1)}, bf16[32,2048]{1,0:T(8,128)(2,1)S(1)}, u32[]{:S(2)}, u32[]{:S(2)}) %collective-permute-start.85) | collective-permute-done | bytes 131104 | tf_op jit(solution)/shard_map/ppermute | solution.py:252
  236.5 2.5 collective-permute-done.86.refs_2_
  239.0 2.4 shard_map.123
  249.3 4.7 %collective-permute-start.92 = (bf16[32,2048]{1,0:T(8,128)(2,1)S(1)}, bf16[32,2048]{1,0:T(8,128)(2,1)S(1)}, u32[]{:S(2)}, u32[]{:S(2)}) collective-permute-start(bf16[32,2048]{1,0:T(8,128)(2,1)S(1)} %fusion.40), channel_id=1, source_target_pairs={{0,12},{4,0},{8,4},{12,8},{1,13},{5,1},{9,5},{13,9},{2,14},{6,2},{... | collective-permute-start | bytes 393224 | tf_op jit(solution)/shard_map/ppermute | solution.py:257
  264.0 2.6 shard_map.124
  276.5 3.0 %collective-permute-done.96 = bf16[32,2048]{1,0:T(8,128)(2,1)S(1)} collective-permute-done((bf16[32,2048]{1,0:T(8,128)(2,1)S(1)}, bf16[32,2048]{1,0:T(8,128)(2,1)S(1)}, u32[]{:S(2)}, u32[]{:S(2)}) %collective-permute-start.96) | collective-permute-done | bytes 131104 | tf_op jit(solution)/shard_map/ppermute | solution.py:252
  (253 shorter events, 176.1 us)
Async XLA Ops:
  1.2 8.5 %collective-permute-start.4 = (bf16[2048,384]{1,0:T(8,128)(2,1)}, bf16[2048,384]{1,0:T(8,128)(2,1)S(1)}, u32[]{:S(2)}, u32[]{:S(2)}) collective-permute-start(bf16[2048,384]{1,0:T(8,128)(2,1)} %bitcast.31), channel_id=1, source_target_pairs={{0,1},{1,0},{2,3},{3,2},{4,5},{5,4},{6,7},{7,6},{8,9},{9,8},{10,11... | collective-permute-start | bytes 4718600 | tf_op jit(solution)/shard_map/ppermute | solution.py:242
  1.3 8.4 %collective-permute-start.5 = (bf16[384,2048]{1,0:T(8,128)(2,1)}, bf16[384,2048]{1,0:T(8,128)(2,1)S(1)}, u32[]{:S(2)}, u32[]{:S(2)}) collective-permute-start(bf16[384,2048]{1,0:T(8,128)(2,1)} %bitcast.33), channel_id=1, source_target_pairs={{0,1},{1,0},{2,3},{3,2},{4,5},{5,4},{6,7},{7,6},{8,9},{9,8},{10,11... | collective-permute-start | bytes 4718600 | tf_op jit(solution)/shard_map/ppermute | solution.py:242
  2.8 8.1 %collective-permute-start = (bf16[32,2176]{1,0:T(8,128)(2,1)S(1)}, bf16[32,2176]{1,0:T(8,128)(2,1)S(1)}, u32[]{:S(2)}, u32[]{:S(2)}) collective-permute-start(bf16[32,2176]{1,0:T(8,128)(2,1)S(1)} %shard_map.104.refs_0_.refs_4_), channel_id=1, source_target_pairs={{0,18},{1,19},{2,16},{3,17},{16,2},{17,3},{18,0},{19,1},{4,22},{5,... | collective-permute-start | bytes 417800 | tf_op jit(solution)/shard_map/ppermute | solution.py:252
  86.3 9.0 %collective-permute-start.25 = (bf16[32,2048]{1,0:T(8,128)(2,1)S(1)}, bf16[32,2048]{1,0:T(8,128)(2,1)S(1)}, u32[]{:S(2)}, u32[]{:S(2)}) collective-permute-start(bf16[32,2048]{1,0:T(8,128)(2,1)S(1)} %slice_select_fusion.5.refs_0_), channel_id=1, source_target_pairs={{0,2},{1,3},{2,0},{3,1},{16,18},{17,19},{18,16},{19,17},{4,6},{5,7... | collective-permute-start | bytes 393224 | tf_op jit(solution)/shard_map/ppermute | solution.py:252
  87.4 7.9 %collective-permute-start.26 = (bf16[32,2048]{1,0:T(8,128)(2,1)S(1)}, bf16[32,2048]{1,0:T(8,128)(2,1)S(1)}, u32[]{:S(2)}, u32[]{:S(2)}) collective-permute-start(bf16[32,2048]{1,0:T(8,128)(2,1)S(1)} %slice_select_fusion.5.refs_0_), channel_id=1, source_target_pairs={{0,16},{1,17},{2,18},{3,19},{16,0},{17,1},{18,2},{19,3},{4,20},{5,... | collective-permute-start | bytes 393224 | tf_op jit(solution)/shard_map/ppermute | solution.py:252
  88.3 12.0 %collective-permute-start.48 = (bf16[32,2048]{1,0:T(8,128)(2,1)S(1)}, bf16[32,2048]{1,0:T(8,128)(2,1)S(1)}, u32[]{:S(2)}, u32[]{:S(2)}) collective-permute-start(bf16[32,2048]{1,0:T(8,128)(2,1)S(1)} %slice.31.refs_0_), channel_id=1, source_target_pairs={{0,18},{1,19},{2,16},{3,17},{16,2},{17,3},{18,0},{19,1},{4,22},{5,... | collective-permute-start | bytes 393224 | tf_op jit(solution)/shard_map/ppermute | solution.py:252
  89.8 14.9 %collective-permute-start.49 = (bf16[32,2048]{1,0:T(8,128)(2,1)S(1)}, bf16[32,2048]{1,0:T(8,128)(2,1)S(1)}, u32[]{:S(2)}, u32[]{:S(2)}) collective-permute-start(bf16[32,2048]{1,0:T(8,128)(2,1)S(1)} %slice.31.refs_0_), channel_id=1, source_target_pairs={{0,2},{1,3},{2,0},{3,1},{16,18},{17,19},{18,16},{19,17},{4,6},{5,7... | collective-permute-start | bytes 393224 | tf_op jit(solution)/shard_map/ppermute | solution.py:252
  92.1 12.6 %collective-permute-start.50 = (bf16[32,2048]{1,0:T(8,128)(2,1)S(1)}, bf16[32,2048]{1,0:T(8,128)(2,1)S(1)}, u32[]{:S(2)}, u32[]{:S(2)}) collective-permute-start(bf16[32,2048]{1,0:T(8,128)(2,1)S(1)} %slice.31.refs_0_), channel_id=1, source_target_pairs={{0,16},{1,17},{2,18},{3,19},{16,0},{17,1},{18,2},{19,3},{4,20},{5,... | collective-permute-start | bytes 393224 | tf_op jit(solution)/shard_map/ppermute | solution.py:252
  97.4 12.8 %collective-permute-start.27 = (bf16[32,2048]{1,0:T(8,128)(2,1)S(1)}, bf16[32,2048]{1,0:T(8,128)(2,1)S(1)}, u32[]{:S(2)}, u32[]{:S(2)}) collective-permute-start(bf16[32,2048]{1,0:T(8,128)(2,1)S(1)} %get-tuple-element.105), channel_id=1, source_target_pairs={{0,18},{1,19},{2,16},{3,17},{16,2},{17,3},{18,0},{19,1},{4,22},{5,... | collective-permute-start | bytes 393224 | tf_op jit(solution)/shard_map/ppermute | solution.py:252
  98.9 12.0 %collective-permute-start.28 = (bf16[32,2048]{1,0:T(8,128)(2,1)S(1)}, bf16[32,2048]{1,0:T(8,128)(2,1)S(1)}, u32[]{:S(2)}, u32[]{:S(2)}) collective-permute-start(bf16[32,2048]{1,0:T(8,128)(2,1)S(1)} %get-tuple-element.106), channel_id=1, source_target_pairs={{0,2},{1,3},{2,0},{3,1},{16,18},{17,19},{18,16},{19,17},{4,6},{5,7... | collective-permute-start | bytes 393224 | tf_op jit(solution)/shard_map/ppermute | solution.py:252
  100.3 10.6 %collective-permute-start.29 = (bf16[32,2048]{1,0:T(8,128)(2,1)S(1)}, bf16[32,2048]{1,0:T(8,128)(2,1)S(1)}, u32[]{:S(2)}, u32[]{:S(2)}) collective-permute-start(bf16[32,2048]{1,0:T(8,128)(2,1)S(1)} %get-tuple-element.107), channel_id=1, source_target_pairs={{0,16},{1,17},{2,18},{3,19},{16,0},{17,1},{18,2},{19,3},{4,20},{5,... | collective-permute-start | bytes 393224 | tf_op jit(solution)/shard_map/ppermute | solution.py:252
  108.9 7.8 %collective-permute-start.52 = (bf16[32,2048]{1,0:T(8,128)(2,1)S(1)}, bf16[32,2048]{1,0:T(8,128)(2,1)S(1)}, u32[]{:S(2)}, u32[]{:S(2)}) collective-permute-start(bf16[32,2048]{1,0:T(8,128)(2,1)S(1)} %get-tuple-element.129), channel_id=1, source_target_pairs={{0,2},{1,3},{2,0},{3,1},{16,18},{17,19},{18,16},{19,17},{4,6},{5,7... | collective-permute-start | bytes 393224 | tf_op jit(solution)/shard_map/ppermute | solution.py:252
  117.9 7.9 %collective-permute-start.31 = (bf16[32,2048]{1,0:T(8,128)(2,1)S(1)}, bf16[32,2048]{1,0:T(8,128)(2,1)S(1)}, u32[]{:S(2)}, u32[]{:S(2)}) collective-permute-start(bf16[32,2048]{1,0:T(8,128)(2,1)S(1)} %collective-permute-done.30.refs_0_), channel_id=1, source_target_pairs={{0,18},{1,19},{2,16},{3,17},{16,2},{17,3},{18,0},{19,1},{4,22},{5,... | collective-permute-start | bytes 393224 | tf_op jit(solution)/shard_map/ppermute | solution.py:252
  119.3 9.2 %collective-permute-start.32 = (bf16[32,2048]{1,0:T(8,128)(2,1)S(1)}, bf16[32,2048]{1,0:T(8,128)(2,1)S(1)}, u32[]{:S(2)}, u32[]{:S(2)}) collective-permute-start(bf16[32,2048]{1,0:T(8,128)(2,1)S(1)} %collective-permute-done.30.refs_0_), channel_id=1, source_target_pairs={{0,2},{1,3},{2,0},{3,1},{16,18},{17,19},{18,16},{19,17},{4,6},{5,7... | collective-permute-start | bytes 393224 | tf_op jit(solution)/shard_map/ppermute | solution.py:252
  120.8 7.8 %collective-permute-start.33 = (bf16[32,2048]{1,0:T(8,128)(2,1)S(1)}, bf16[32,2048]{1,0:T(8,128)(2,1)S(1)}, u32[]{:S(2)}, u32[]{:S(2)}) collective-permute-start(bf16[32,2048]{1,0:T(8,128)(2,1)S(1)} %collective-permute-done.30.refs_0_), channel_id=1, source_target_pairs={{0,16},{1,17},{2,18},{3,19},{16,0},{17,1},{18,2},{19,3},{4,20},{5,... | collective-permute-start | bytes 393224 | tf_op jit(solution)/shard_map/ppermute | solution.py:252
  122.2 11.4 %collective-permute-start.55 = (bf16[32,2048]{1,0:T(8,128)(2,1)S(1)}, bf16[32,2048]{1,0:T(8,128)(2,1)S(1)}, u32[]{:S(2)}, u32[]{:S(2)}) collective-permute-start(bf16[32,2048]{1,0:T(8,128)(2,1)S(1)} %slice_select_fusion.refs_0_), channel_id=1, source_target_pairs={{0,18},{1,19},{2,16},{3,17},{16,2},{17,3},{18,0},{19,1},{4,22},{5,... | collective-permute-start | bytes 393224 | tf_op jit(solution)/shard_map/ppermute | solution.py:252
  123.4 10.8 %collective-permute-start.56 = (bf16[32,2048]{1,0:T(8,128)(2,1)S(1)}, bf16[32,2048]{1,0:T(8,128)(2,1)S(1)}, u32[]{:S(2)}, u32[]{:S(2)}) collective-permute-start(bf16[32,2048]{1,0:T(8,128)(2,1)S(1)} %slice_select_fusion.refs_0_), channel_id=1, source_target_pairs={{0,2},{1,3},{2,0},{3,1},{16,18},{17,19},{18,16},{19,17},{4,6},{5,7... | collective-permute-start | bytes 393224 | tf_op jit(solution)/shard_map/ppermute | solution.py:252
  125.8 8.5 %collective-permute-start.57 = (bf16[32,2048]{1,0:T(8,128)(2,1)S(1)}, bf16[32,2048]{1,0:T(8,128)(2,1)S(1)}, u32[]{:S(2)}, u32[]{:S(2)}) collective-permute-start(bf16[32,2048]{1,0:T(8,128)(2,1)S(1)} %slice_select_fusion.refs_0_), channel_id=1, source_target_pairs={{0,16},{1,17},{2,18},{3,19},{16,0},{17,1},{18,2},{19,3},{4,20},{5,... | collective-permute-start | bytes 393224 | tf_op jit(solution)/shard_map/ppermute | solution.py:252
  130.7 8.9 %collective-permute-start.34 = (bf16[32,2048]{1,0:T(8,128)(2,1)S(1)}, bf16[32,2048]{1,0:T(8,128)(2,1)S(1)}, u32[]{:S(2)}, u32[]{:S(2)}) collective-permute-start(bf16[32,2048]{1,0:T(8,128)(2,1)S(1)} %get-tuple-element.109), channel_id=1, source_target_pairs={{0,18},{1,19},{2,16},{3,17},{16,2},{17,3},{18,0},{19,1},{4,22},{5,... | collective-permute-start | bytes 393224 | tf_op jit(solution)/shard_map/ppermute | solution.py:252
  132.3 7.9 %collective-permute-start.35 = (bf16[32,2048]{1,0:T(8,128)(2,1)S(1)}, bf16[32,2048]{1,0:T(8,128)(2,1)S(1)}, u32[]{:S(2)}, u32[]{:S(2)}) collective-permute-start(bf16[32,2048]{1,0:T(8,128)(2,1)S(1)} %get-tuple-element.110), channel_id=1, source_target_pairs={{0,2},{1,3},{2,0},{3,1},{16,18},{17,19},{18,16},{19,17},{4,6},{5,7... | collective-permute-start | bytes 393224 | tf_op jit(solution)/shard_map/ppermute | solution.py:252
  138.2 8.7 %collective-permute-start.59 = (bf16[32,2048]{1,0:T(8,128)(2,1)S(1)}, bf16[32,2048]{1,0:T(8,128)(2,1)S(1)}, u32[]{:S(2)}, u32[]{:S(2)}) collective-permute-start(bf16[32,2048]{1,0:T(8,128)(2,1)S(1)} %get-tuple-element.137), channel_id=1, source_target_pairs={{0,2},{1,3},{2,0},{3,1},{16,18},{17,19},{18,16},{19,17},{4,6},{5,7... | collective-permute-start | bytes 393224 | tf_op jit(solution)/shard_map/ppermute | solution.py:252
  147.5 7.7 %collective-permute-start.38 = (bf16[32,2048]{1,0:T(8,128)(2,1)S(1)}, bf16[32,2048]{1,0:T(8,128)(2,1)S(1)}, u32[]{:S(2)}, u32[]{:S(2)}) collective-permute-start(bf16[32,2048]{1,0:T(8,128)(2,1)S(1)} %collective-permute-done.37.refs_0_), channel_id=1, source_target_pairs={{0,18},{1,19},{2,16},{3,17},{16,2},{17,3},{18,0},{19,1},{4,22},{5,... | collective-permute-start | bytes 393224 | tf_op jit(solution)/shard_map/ppermute | solution.py:252
  149.2 9.0 %collective-permute-start.39 = (bf16[32,2048]{1,0:T(8,128)(2,1)S(1)}, bf16[32,2048]{1,0:T(8,128)(2,1)S(1)}, u32[]{:S(2)}, u32[]{:S(2)}) collective-permute-start(bf16[32,2048]{1,0:T(8,128)(2,1)S(1)} %collective-permute-done.37.refs_0_), channel_id=1, source_target_pairs={{0,2},{1,3},{2,0},{3,1},{16,18},{17,19},{18,16},{19,17},{4,6},{5,7... | collective-permute-start | bytes 393224 | tf_op jit(solution)/shard_map/ppermute | solution.py:252
  150.2 8.0 %collective-permute-start.40 = (bf16[32,2048]{1,0:T(8,128)(2,1)S(1)}, bf16[32,2048]{1,0:T(8,128)(2,1)S(1)}, u32[]{:S(2)}, u32[]{:S(2)}) collective-permute-start(bf16[32,2048]{1,0:T(8,128)(2,1)S(1)} %collective-permute-done.37.refs_0_), channel_id=1, source_target_pairs={{0,16},{1,17},{2,18},{3,19},{16,0},{17,1},{18,2},{19,3},{4,20},{5,... | collective-permute-start | bytes 393224 | tf_op jit(solution)/shard_map/ppermute | solution.py:252
  152.5 10.5 %collective-permute-start.62 = (bf16[32,2048]{1,0:T(8,128)(2,1)S(1)}, bf16[32,2048]{1,0:T(8,128)(2,1)S(1)}, u32[]{:S(2)}, u32[]{:S(2)}) collective-permute-start(bf16[32,2048]{1,0:T(8,128)(2,1)S(1)} %slice_select_fusion.1.refs_0_), channel_id=1, source_target_pairs={{0,18},{1,19},{2,16},{3,17},{16,2},{17,3},{18,0},{19,1},{4,22},{5,... | collective-permute-start | bytes 393224 | tf_op jit(solution)/shard_map/ppermute | solution.py:252
  154.1 9.7 %collective-permute-start.63 = (bf16[32,2048]{1,0:T(8,128)(2,1)S(1)}, bf16[32,2048]{1,0:T(8,128)(2,1)S(1)}, u32[]{:S(2)}, u32[]{:S(2)}) collective-permute-start(bf16[32,2048]{1,0:T(8,128)(2,1)S(1)} %slice_select_fusion.1.refs_0_), channel_id=1, source_target_pairs={{0,2},{1,3},{2,0},{3,1},{16,18},{17,19},{18,16},{19,17},{4,6},{5,7... | collective-permute-start | bytes 393224 | tf_op jit(solution)/shard_map/ppermute | solution.py:252
  155.2 8.7 %collective-permute-start.64 = (bf16[32,2048]{1,0:T(8,128)(2,1)S(1)}, bf16[32,2048]{1,0:T(8,128)(2,1)S(1)}, u32[]{:S(2)}, u32[]{:S(2)}) collective-permute-start(bf16[32,2048]{1,0:T(8,128)(2,1)S(1)} %slice_select_fusion.1.refs_0_), channel_id=1, source_target_pairs={{0,16},{1,17},{2,18},{3,19},{16,0},{17,1},{18,2},{19,3},{4,20},{5,... | collective-permute-start | bytes 393224 | tf_op jit(solution)/shard_map/ppermute | solution.py:252
  160.3 8.7 %collective-permute-start.41 = (bf16[32,2048]{1,0:T(8,128)(2,1)S(1)}, bf16[32,2048]{1,0:T(8,128)(2,1)S(1)}, u32[]{:S(2)}, u32[]{:S(2)}) collective-permute-start(bf16[32,2048]{1,0:T(8,128)(2,1)S(1)} %get-tuple-element.113), channel_id=1, source_target_pairs={{0,18},{1,19},{2,16},{3,17},{16,2},{17,3},{18,0},{19,1},{4,22},{5,... | collective-permute-start | bytes 393224 | tf_op jit(solution)/shard_map/ppermute | solution.py:252
  161.9 8.9 %collective-permute-start.42 = (bf16[32,2048]{1,0:T(8,128)(2,1)S(1)}, bf16[32,2048]{1,0:T(8,128)(2,1)S(1)}, u32[]{:S(2)}, u32[]{:S(2)}) collective-permute-start(bf16[32,2048]{1,0:T(8,128)(2,1)S(1)} %get-tuple-element.114), channel_id=1, source_target_pairs={{0,2},{1,3},{2,0},{3,1},{16,18},{17,19},{18,16},{19,17},{4,6},{5,7... | collective-permute-start | bytes 393224 | tf_op jit(solution)/shard_map/ppermute | solution.py:252
  163.0 7.8 %collective-permute-start.43 = (bf16[32,2048]{1,0:T(8,128)(2,1)S(1)}, bf16[32,2048]{1,0:T(8,128)(2,1)S(1)}, u32[]{:S(2)}, u32[]{:S(2)}) collective-permute-start(bf16[32,2048]{1,0:T(8,128)(2,1)S(1)} %get-tuple-element.115), channel_id=1, source_target_pairs={{0,16},{1,17},{2,18},{3,19},{16,0},{17,1},{18,2},{19,3},{4,20},{5,... | collective-permute-start | bytes 393224 | tf_op jit(solution)/shard_map/ppermute | solution.py:252
  230.9 8.1 %collective-permute-start.86 = (bf16[32,2048]{1,0:T(8,128)(2,1)S(1)}, bf16[32,2048]{1,0:T(8,128)(2,1)S(1)}, u32[]{:S(2)}, u32[]{:S(2)}) collective-permute-start(bf16[32,2048]{1,0:T(8,128)(2,1)S(1)} %collective-permute-done.84.refs_0_), channel_id=1, source_target_pairs={{0,2},{1,3},{2,0},{3,1},{16,18},{17,19},{18,16},{19,17},{4,6},{5,7... | collective-permute-start | bytes 393224 | tf_op jit(solution)/shard_map/ppermute | solution.py:252
  245.0 14.1 %collective-permute-start.75 = (bf16[32,2048]{1,0:T(8,128)(2,1)S(1)}, bf16[32,2048]{1,0:T(8,128)(2,1)S(1)}, u32[]{:S(2)}, u32[]{:S(2)}) collective-permute-start(bf16[32,2048]{1,0:T(8,128)(2,1)S(1)} %get-tuple-element.151), channel_id=1, source_target_pairs={{0,18},{1,19},{2,16},{3,17},{16,2},{17,3},{18,0},{19,1},{4,22},{5,... | collective-permute-start | bytes 393224 | tf_op jit(solution)/shard_map/ppermute | solution.py:252
  (75 other events, 491.9 us)
